TPU v7x, 256 devices: a whole 4x4x8 slice. The times are simulated.
256 devices in a mesh: ep: 64 (over z, y, core), rep: 4 (over x).
Axes of the slice: x: 4, y: 4, z: 8, core: 2. Of those that a mesh axis runs over, the one named last changes fastest.
Arguments:
- residual: bfloat16 [4096, 2048], P('ep'), may hold values from -6 to 6
- query_latent: bfloat16 [4096, 8192], P(('ep', 'rep')), may hold values from -32.5 to 32.5
- query_rope: bfloat16 [4096, 1024], P(('ep', 'rep')), may hold values from -4 to 4
- cache_latent: bfloat16 [8192, 32, 512], P(('ep', 'rep')), may hold values from -4.6 to 4.6
- cache_rope: bfloat16 [8192, 2048], P(('ep', 'rep')), may hold values from -4 to 4
- page_table: int32 [4096, 9], P(('ep', 'rep')), may hold values from 0 to 31, as said below
- lengths: int32 [4096], P(('ep', 'rep')), may hold values from 257 to 288, as said below
- value_up: bfloat16 [16, 512, 128], P('rep'), may hold values from -0.25 to 0.25
- out_proj: bfloat16 [2048, 2048], P('rep'), may hold values from -0.125 to 0.125
- routes: int32 [4096, 6], P('ep'), may hold values from 0 to 63, all different within a row; in each aligned block of 64 rows (0 to 63, 64 to 127, ...) at most 12 rows name the same one
- route_weight: float32 [4096, 6], P('ep'), may hold values from 0.05 to 0.6
- placement: int32 [64], replicated, may hold values from 0 to 63, each once
- expert_gate: bfloat16 [64, 2048, 1408], P('ep', None, 'rep'), may hold values from -0.125 to 0.125
- expert_up: bfloat16 [64, 2048, 1408], P('ep', None, 'rep'), may hold values from -0.125 to 0.125
- expert_down: bfloat16 [64, 1408, 2048], P('ep', 'rep'), may hold values from -0.15625 to 0.15625
- shared_gate: bfloat16 [2048, 1408], P(None, 'rep'), may hold values from -0.125 to 0.125
- shared_up: bfloat16 [2048, 1408], P(None, 'rep'), may hold values from -0.125 to 0.125
- shared_down: bfloat16 [1408, 2048], P('rep'), may hold values from -0.15625 to 0.15625
- norm_gain: float32 [2048], replicated, may hold values from 0.5 to 1.5
Outputs:
- normed: bfloat16 [4096, 2048], P(('ep', 'rep'))
Inputs may be any that keep to these rules, and one draw needn't show every extreme that they name: `page_table`: entries number the 32 pages of the row's own device. A device's rows come in consecutive groups of 8 that share their first 8 entries; all other entries of a device are distinct. `lengths`: every row's context covers its shared prompt; the last row of every device has the greatest length. `routes`: within the 64 rows of one index of ep, no expert is named by more than 12 rows, a bound that some block reaches. `placement`: each slot holds exactly one expert.
All inputs are finite; a program needn't handle non-finite values.
Results may differ from a plain program's by a relative error of at most 0.014.
Values may be sent and summed in bfloat16 or wider, within the bound.
A program may use at most 128 MiB of HBM per device.

v0:
```python
import math

import jax
import jax.numpy as jnp
from jax import lax
from jax.sharding import PartitionSpec as P

ROPE = 64
VHEAD = 128


EPSILON = 1e-06


def attend_rows(query_latent, query_rope, cache_latent, cache_rope, page_table, lengths):
    row_count = page_table.shape[0]
    page_len = cache_latent.shape[1]
    latent_width = cache_latent.shape[2]
    rope_width = cache_rope.shape[1] // page_len
    head_count = query_rope.shape[1] // rope_width
    key_span = page_table.shape[1] * page_len
    keys_lat = cache_latent[page_table].reshape(row_count, key_span, latent_width)
    keys_rope = cache_rope[page_table].reshape(row_count, key_span, rope_width)
    query_lat = query_latent.reshape(row_count, head_count, latent_width)
    query_rot = query_rope.reshape(row_count, head_count, rope_width)
    score_scale = 1.0 / math.sqrt(VHEAD + ROPE)
    scores = (
        jnp.einsum("thr,tlr->thl", query_lat, keys_lat, preferred_element_type=jnp.float32)
        + jnp.einsum("thr,tlr->thl", query_rot, keys_rope, preferred_element_type=jnp.float32)
    ) * score_scale
    live_mask = (jnp.arange(key_span, dtype=jnp.int32)[None, :] < lengths[:, None])[:, None, :]
    masked = jnp.where(live_mask, scores, -jnp.inf)
    row_peak = jnp.max(masked, axis=2, keepdims=True)
    expons = jnp.where(live_mask, jnp.exp(scores - row_peak), 0.0)
    probs = (expons / jnp.sum(expons, axis=2, keepdims=True)).astype(jnp.bfloat16)
    latent_out = jnp.einsum("thl,tlr->thr", probs, keys_lat, preferred_element_type=jnp.float32)
    return latent_out.astype(jnp.bfloat16)


def per_device(
    residual,
    query_latent,
    query_rope,
    cache_latent,
    cache_rope,
    page_table,
    lengths,
    value_up,
    out_proj,
    routes,
    route_weight,
    placement,
    expert_gate,
    expert_up,
    expert_down,
    shared_gate,
    shared_up,
    shared_down,
    norm_gain,
):
    replicas = lax.axis_size("rep")
    expert_groups = lax.axis_size("ep")
    latent_out = attend_rows(
        query_latent, query_rope, cache_latent, cache_rope, page_table, lengths
    )
    own_count = latent_out.shape[0]
    swapped = lax.all_to_all(latent_out, "rep", split_axis=1, concat_axis=0, tiled=True)
    group_rows = swapped.shape[0]
    head_out = jnp.einsum(
        "thr,hrv->thv", swapped, value_up, preferred_element_type=jnp.float32
    ).astype(jnp.bfloat16)
    attn_terms = jnp.dot(
        head_out.reshape(group_rows, -1), out_proj, preferred_element_type=jnp.float32
    )
    attended = lax.psum(attn_terms.astype(jnp.bfloat16), "rep")
    hidden = (residual.astype(jnp.float32) + attended.astype(jnp.float32)).astype(jnp.bfloat16)
    model_width = hidden.shape[1]
    shared_act = (
        jax.nn.silu(jnp.dot(hidden, shared_gate, preferred_element_type=jnp.float32))
        * jnp.dot(hidden, shared_up, preferred_element_type=jnp.float32)
    ).astype(jnp.bfloat16)
    shared_terms = jnp.dot(shared_act, shared_down, preferred_element_type=jnp.float32)
    experts = placement.shape[0]
    route_count = routes.shape[1]
    per_group = experts // expert_groups
    capacity = max(
        replicas, min(group_rows, 2 * group_rows * route_count // experts // replicas * replicas)
    )
    expert_ids = jnp.arange(experts, dtype=jnp.int32)
    slot_index = jnp.sum(jnp.where(routes[:, :, None] == expert_ids, placement, 0), axis=2).reshape(
        -1
    )
    one_hot = (slot_index[:, None] == expert_ids[None, :]).astype(jnp.int32)
    earlier = jnp.cumsum(one_hot, axis=0) - one_hot
    position = jnp.sum(earlier * one_hot, axis=1)
    assignments = slot_index.shape[0]
    source_row = (
        jnp.full((experts * capacity,), group_rows, jnp.int32)
        .at[slot_index * capacity + position]
        .set(jnp.arange(assignments, dtype=jnp.int32) // route_count)
    )
    padded = jnp.concatenate([hidden, jnp.zeros((1, model_width), jnp.bfloat16)], axis=0)
    outgoing = padded[source_row].reshape(expert_groups, per_group * capacity, model_width)
    incoming = lax.all_to_all(outgoing, "ep", split_axis=0, concat_axis=0, tiled=True).reshape(
        expert_groups, per_group, capacity, model_width
    )
    gate_values = jnp.einsum(
        "secd,edf->secf", incoming, expert_gate, preferred_element_type=jnp.float32
    )
    up_values = jnp.einsum(
        "secd,edf->secf", incoming, expert_up, preferred_element_type=jnp.float32
    )
    activated = (jax.nn.silu(gate_values) * up_values).astype(jnp.bfloat16)
    expert_terms = jnp.einsum(
        "secf,efd->secd", activated, expert_down, preferred_element_type=jnp.float32
    )
    outbound = expert_terms.astype(jnp.bfloat16).reshape(
        expert_groups, per_group * capacity, model_width
    )
    returned = lax.all_to_all(outbound, "ep", split_axis=0, concat_axis=0, tiled=True)
    picked = returned.reshape(experts * capacity, model_width)[slot_index * capacity + position]
    weight_used = route_weight.reshape(-1)
    routed = jnp.sum(
        (picked.astype(jnp.float32) * weight_used[:, None]).reshape(
            group_rows, route_count, model_width
        ),
        axis=1,
    )
    row_sums = lax.psum_scatter(
        (routed + shared_terms).astype(jnp.bfloat16), "rep", scatter_dimension=0, tiled=True
    ).astype(jnp.float32)
    own_hidden = lax.dynamic_slice_in_dim(hidden, lax.axis_index("rep") * own_count, own_count, 0)
    mixed = row_sums + own_hidden.astype(jnp.float32)
    inverse = lax.rsqrt(jnp.mean(mixed * mixed, axis=1, keepdims=True) + EPSILON)
    return (mixed * inverse * norm_gain).astype(jnp.bfloat16)


def solution(mesh):
    in_specs = (
        P("ep", None),
        P(("ep", "rep"), None),
        P(("ep", "rep"), None),
        P(("ep", "rep"), None, None),
        P(("ep", "rep"), None),
        P(("ep", "rep"), None),
        P(("ep", "rep")),
        P("rep", None, None),
        P("rep", None),
        P("ep", None),
        P("ep", None),
        P(),
        P("ep", None, "rep"),
        P("ep", None, "rep"),
        P("ep", "rep", None),
        P(None, "rep"),
        P(None, "rep"),
        P("rep", None),
        P(),
    )
    out_specs = P(("ep", "rep"), None)
    return jax.shard_map(
        per_device, mesh=mesh, in_specs=in_specs, out_specs=out_specs, check_vma=False
    )
```

profile of v0, /device:TPU:1, one launch (start us, length us, event | category | flops | bytes accessed | tf_op | source)
XLA Modules:
  0.0 385.3 jit_solution(4769839513103228752)
XLA Ops:
  6.5 0.8 compare_select_fusion
  7.5 1.0 copy.57
  8.5 8.8 %gather_fusion = bf16[144,32,512]{2,1,0:T(8,128)(2,1)} fusion(bf16[32,32,512]{2,1,0:T(8,128)(2,1)} %param.22, s32[1024]{0:T(1024)S(1)} %pad_clamp_fusion.2), kind=kCustom, calls=%fused_computation | custom fusion | bytes 9437760 | tf_op jit(solution)/shard_map/gather | solution.py:22
  17.3 1.8 gather_fusion.1
  19.2 2.2 reshape.130
  21.4 1.5 reshape.131
  22.9 3.7 fusion.79
  26.6 0.5 fusion.36
  27.1 0.8 copy-done.3
  27.9 0.2 fusion.78
  28.1 3.5 convolution_convert_fusion.2
  31.7 0.9 copy.43
  32.6 4.8 %all-to-all-start = ((bf16[16,16,512]{2,0,1:T(8,128)(2,1)}), bf16[16,16,512]{2,0,1:T(8,128)(2,1)S(1)}, u32[]{:S(2)}, u32[]{:S(2)}) async-start(bf16[16,16,512]{2,0,1:T(8,128)(2,1)} %copy.43), calls=%async_computation | async-start | bytes 524288 | tf_op jit(solution)/shard_map/all_to_all | solution.py:67
  37.4 0.3 select_reduce_fusion.1
  37.7 0.1 copy.47
  37.8 0.1 eq.45
  37.9 0.1 eq.41
  38.1 0.9 reduce-window.6
  39.0 0.2 slice_reduce_fusion
  39.3 0.1 copy.46
  39.4 0.1 mul.72
  39.5 0.1 fusion.52
  39.7 2.9 scatter_custom_fusion
  42.6 0.3 all-to-all-done
  43.0 0.2 fusion.40
  43.2 1.2 convolution_convert_fusion.1
  44.4 48.2 %all-reduce.3.cloned.1.call-done = bf16[64,2048]{1,0:T(8,128)(2,1)} async-done(((bf16[64,2048]{1,0:T(8,128)(2,1)}), bf16[64,2048]{1,0:T(8,128)(2,1)}) %all-reduce.3.cloned.1.call-update) | async-done | bytes 262160 | tf_op jit(solution)/shard_map/psum | solution.py:75
  92.6 1.0 add_convert_fusion
  93.7 4.3 %gather_fusion.2 = bf16[768,2048]{1,0:T(8,128)(2,1)} fusion(bf16[65,2048]{1,0:T(8,128)(2,1)S(1)} %concatenate.3, s32[1024]{0:T(1024)S(1)} %pad_clamp_fusion.1), kind=kCustom, calls=%fused_computation.2 | custom fusion | bytes 6294528 | tf_op jit(solution)/shard_map/gather | solution.py:103
  98.0 6.1 %reshape.134 = bf16[64,12,2048]{2,1,0:T(8,128)(2,1)} reshape(bf16[768,2048]{1,0:T(8,128)(2,1)} %gather_fusion.2) | data formatting | bytes 6291456 | tf_op jit(solution)/shard_map/reshape | solution.py:103
  104.0 107.6 %all_to_all.28 = bf16[64,12,2048]{2,1,0:T(8,128)(2,1)S(1)} all-to-all(bf16[64,12,2048]{2,1,0:T(8,128)(2,1)} %reshape.134), channel_id=1, replica_groups=mesh['ep'=64,'rep'=4] {'ep'}, dimensions={0} | all-to-all | bytes 6291456 | tf_op jit(solution)/shard_map/all_to_all | solution.py:104
  211.6 2.0 copy-done.2
  213.6 3.1 fusion.9
  216.7 8.8 %convolution_convert_fusion = bf16[64,12,2048]{2,0,1:T(8,128)(2,1)} fusion(bf16[1,352,2048]{2,1,0:T(8,128)(2,1)} %param.33, bf16[1,2048,352]{1,2,0:T(8,128)(2,1)} %param.32, bf16[64,12,2048]{2,1,0:T(8,128)(2,1)} %copy-done.2, f32[64,1,12,352]{3,0,2,1:T(8,128)} %fusion.9), kind=kOutput, calls=%fused_computation.7 | convolution fusion | flops 2217787392 | bytes 10256384 | tf_op jit(solution)/shard_map/secf,efd->secd/dot_general | solution.py:114
  225.5 5.7 %copy.52 = bf16[64,12,2048]{2,1,0:T(8,128)(2,1)} copy(bf16[64,12,2048]{2,0,1:T(8,128)(2,1)} %convolution_convert_fusion) | data formatting | bytes 6291456 | tf_op jit(solution)/shard_map/convert_element_type | solution.py:117
  231.1 7.3 %all-to-all-start.2 = ((bf16[64,12,2048]{2,1,0:T(8,128)(2,1)}), bf16[64,12,2048]{2,1,0:T(8,128)(2,1)}, u32[]{:S(2)}, u32[]{:S(2)}) async-start(bf16[64,12,2048]{2,1,0:T(8,128)(2,1)} %copy.52), calls=%async_computation.2 | async-start | bytes 8388608 | tf_op jit(solution)/shard_map/all_to_all | solution.py:120
  238.5 0.3 reduce-scatter.2.cloned.1.call-start
  238.8 0.1 copy.53
  238.9 1.9 fusion.80
  240.8 92.3 %all-to-all-done.2 = bf16[64,12,2048]{2,1,0:T(8,128)(2,1)} async-done(((bf16[64,12,2048]{2,1,0:T(8,128)(2,1)}), bf16[64,12,2048]{2,1,0:T(8,128)(2,1)}, u32[]{:S(2)}, u32[]{:S(2)}) %all-to-all-start.2) | async-done | bytes 3145760 | tf_op jit(solution)/shard_map/all_to_all | solution.py:120
  333.1 6.2 %reshape.139 = bf16[768,2048]{1,0:T(8,128)(2,1)} reshape(bf16[64,12,2048]{2,1,0:T(8,128)(2,1)} %all-to-all-done.2) | data formatting | bytes 6291456 | tf_op jit(solution)/shard_map/reshape | solution.py:121
  339.2 7.4 %gather_fusion.3 = bf16[384,2048]{1,0:T(8,128)(2,1)} fusion(bf16[768,2048]{1,0:T(8,128)(2,1)} %reshape.139, s32[1024]{0:T(1024)S(1)} %pad_clamp_fusion), kind=kCustom, calls=%fused_computation.3 | custom fusion | bytes 3147264 | tf_op jit(solution)/shard_map/gather | solution.py:121
  346.6 3.9 %reshape.140 = f32[64,6,2048]{2,1,0:T(8,128)} reshape(bf16[384,2048]{1,0:T(8,128)(2,1)} %gather_fusion.3) | data formatting | bytes 4718592 | tf_op jit(solution)/shard_map/convert_element_type | solution.py:124
  350.5 3.7 multiply_reduce_fusion
  354.3 3.7 fusion.1
  358.0 17.9 %reduce-scatter.2.cloned.1.call-done = bf16[16,2048]{1,0:T(8,128)(2,1)} async-done(((bf16[64,2048]{1,0:T(8,128)(2,1)}), bf16[16,2048]{1,0:T(8,128)(2,1)}) %reduce-scatter.2.cloned.1.call-update) | async-done | bytes 65552 | tf_op jit(solution)/shard_map/reduce_scatter | solution.py:129
  375.9 1.0 multiply_reduce_fusion.1
  376.9 1.6 multiply_convert_fusion
  (41 shorter events, 0.4 us)
Async XLA Ops:
  6.5 36.7 %copy-start = (bf16[512,2048]{1,0:T(8,128)(2,1)S(1)}, bf16[512,2048]{1,0:T(8,128)(2,1)}, u32[]{:S(2)}) copy-start(bf16[512,2048]{1,0:T(8,128)(2,1)} %param.27) | copy-start | bytes 6291460
  8.5 8.8 %copy-start.1 = (bf16[32,2048]{1,0:T(8,128)(2,1)S(1)}, bf16[32,2048]{1,0:T(8,128)(2,1)}, u32[]{:S(2)}) copy-start(bf16[32,2048]{1,0:T(8,128)(2,1)} %param.23) | copy-start | bytes 393220
  19.2 3.7 copy-start.11
  22.9 3.7 copy-start.6
  27.1 0.8 copy-start.3
  28.1 9.3 %copy-start.9 = (s32[64,6]{0,1:T(8,128)S(1)}, s32[64,6]{0,1:T(8,128)}, u32[]{:S(2)}) copy-start(s32[64,6]{0,1:T(8,128)} %param.28) | copy-start | bytes 4612
  28.1 9.3 %copy-start.10 = (s32[64]{0:T(128)S(1)}, s32[64]{0:T(128)}, u32[]{:S(2)}) copy-start(s32[64]{0:T(128)} %param.30) | copy-start | bytes 772
  31.7 11.3 %copy-start.4 = (bf16[4,512,128]{2,1,0:T(8,128)(2,1)S(1)}, bf16[4,512,128]{2,1,0:T(8,128)(2,1)}, u32[]{:S(2)}) copy-start(bf16[4,512,128]{2,1,0:T(8,128)(2,1)} %param.26) | copy-start | bytes 1572868
  32.6 10.4 %all-to-all-start = ((bf16[16,16,512]{2,0,1:T(8,128)(2,1)}), bf16[16,16,512]{2,0,1:T(8,128)(2,1)S(1)}, u32[]{:S(2)}, u32[]{:S(2)}) async-start(bf16[16,16,512]{2,0,1:T(8,128)(2,1)} %copy.43), calls=%async_computation | async-start | bytes 524288 | tf_op jit(solution)/shard_map/all_to_all | solution.py:67
  37.4 55.3 %all-reduce.3.cloned.1.call-start = ((), (), s32[]{:S(2)}) async-start(), calls=%async_computation.4 | async-start | bytes 524288 | tf_op jit(solution)/shard_map/psum | solution.py:75
  43.0 49.7 %copy-start.5 = (bf16[64,2048]{1,0:T(8,128)(2,1)S(1)}, bf16[64,2048]{1,0:T(8,128)(2,1)}, u32[]{:S(2)}) copy-start(bf16[64,2048]{1,0:T(8,128)(2,1)} %param.19) | copy-start | bytes 786436
  104.0 109.6 %copy-start.12 = (bf16[1,2048,352]{1,2,0:T(8,128)(2,1)S(1)}, bf16[1,2048,352]{1,2,0:T(8,128)(2,1)}, u32[]{:S(2)}) copy-start(bf16[1,2048,352]{1,2,0:T(8,128)(2,1)} %param.31) | copy-start | bytes 4325380
  211.6 2.0 copy-start.2
  231.1 7.6 %copy-start.8 = (f32[64,6]{0,1:T(8,128)S(1)}, f32[64,6]{0,1:T(8,128)}, u32[]{:S(2)}) copy-start(f32[64,6]{0,1:T(8,128)} %param.29) | copy-start | bytes 4612
  231.1 101.9 %all-to-all-start.2 = ((bf16[64,12,2048]{2,1,0:T(8,128)(2,1)}), bf16[64,12,2048]{2,1,0:T(8,128)(2,1)}, u32[]{:S(2)}, u32[]{:S(2)}) async-start(bf16[64,12,2048]{2,1,0:T(8,128)(2,1)} %copy.52), calls=%async_computation.2 | async-start | bytes 8388608 | tf_op jit(solution)/shard_map/all_to_all | solution.py:120
  238.5 137.4 %reduce-scatter.2.cloned.1.call-start = ((), (), s32[]{:S(2)}) async-start(), calls=%async_computation.5 | async-start | bytes 327680 | tf_op jit(solution)/shard_map/reduce_scatter | solution.py:129
  354.3 22.6 %copy-start.7 = (f32[2048]{0:T(1024)S(1)}, f32[2048]{0:T(1024)}, u32[]{:S(2)}) copy-start(f32[2048]{0:T(1024)} %param.37) | copy-start | bytes 24580
Sparse Core Ops, SparseCore 0:
  44.5 48.0 all-reduce.2
  358.1 17.7 reduce-scatter.1
where the time goes:
time: 388 us; the launch traced here: 385 us
  waiting for transfers between devices  159 us (41%)
  blocking collectives  108 us (28%)
  local copies, waits for them, and re-layouts  56.4 us (15%)
  matrix products  26.6 us (7%)
  between operations  13.7 us (4%)
  starting transfers between devices  12.4 us (3%)
  other arithmetic  9.84 us (3%)
    all_to_all x1, blocking collectives, per_device(): lax.all_to_all(outgoing, 'ep', split_axis=0, concat_axis=0, tiled=True)  108 us
    all_to_all x1, waiting for transfers between devices, per_device(): lax.all_to_all(outbound, 'ep', split_axis=0, concat_axis=0, tiled=True)  92.3 us
    psum x1, waiting for transfers between devices, per_device(): attended = lax.psum(attn_terms.astype(jnp.bfloat16), 'rep')  48.2 us
    reduce_scatter x1, waiting for transfers between devices, per_device(): lax.psum_scatter((routed + shared_terms).astype(jnp.bfloat16), 'rep', sca...  17.9 us
    dot_general x1, matrix products, per_device(): jnp.einsum('secf,efd->secd', activated, expert_down, preferred_element_ty...  8.8 us
    gather x1, local copies, waits for them, and re-layouts, attend_rows(): cache_latent[page_table].reshape(row_count, key_span, latent_width)  8.77 us
  transfers between devices with their start and end apart: 4, of which 4 were waited for; matrix products, arithmetic and copies ran while one was open for 2% of the time, Pallas kernels for 0%

commit v1 on v0

--- a/solution.py
+++ b/solution.py
@@ -13,27 +13,37 @@
 
 
 def attend_rows(query_latent, query_rope, cache_latent, cache_rope, page_table, lengths):
-    row_count = page_table.shape[0]
-    page_len = cache_latent.shape[1]
-    latent_width = cache_latent.shape[2]
+    row_count, table_len = page_table.shape
+    page_count, page_len, latent_width = cache_latent.shape
     rope_width = cache_rope.shape[1] // page_len
     head_count = query_rope.shape[1] // rope_width
-    key_span = page_table.shape[1] * page_len
-    keys_lat = cache_latent[page_table].reshape(row_count, key_span, latent_width)
-    keys_rope = cache_rope[page_table].reshape(row_count, key_span, rope_width)
+    positions = page_count * page_len
+    keys_lat = cache_latent.reshape(positions, latent_width)
+    keys_rope = cache_rope.reshape(positions, rope_width)
     query_lat = query_latent.reshape(row_count, head_count, latent_width)
     query_rot = query_rope.reshape(row_count, head_count, rope_width)
     score_scale = 1.0 / math.sqrt(VHEAD + ROPE)
     scores = (
-        jnp.einsum("thr,tlr->thl", query_lat, keys_lat, preferred_element_type=jnp.float32)
-        + jnp.einsum("thr,tlr->thl", query_rot, keys_rope, preferred_element_type=jnp.float32)
+        jnp.einsum("thr,pr->thp", query_lat, keys_lat, preferred_element_type=jnp.float32)
+        + jnp.einsum("thr,pr->thp", query_rot, keys_rope, preferred_element_type=jnp.float32)
     ) * score_scale
-    live_mask = (jnp.arange(key_span, dtype=jnp.int32)[None, :] < lengths[:, None])[:, None, :]
-    masked = jnp.where(live_mask, scores, -jnp.inf)
+    page_hit = (
+        page_table[:, :, None] == jnp.arange(page_count, dtype=jnp.int32)[None, None, :]
+    ).astype(jnp.float32)
+    context_pos = (
+        jnp.arange(table_len, dtype=jnp.int32)[:, None] * page_len
+        + jnp.arange(page_len, dtype=jnp.int32)[None, :]
+    )
+    live = (context_pos[None, :, :] < lengths[:, None, None]).astype(jnp.float32)
+    count = jnp.einsum("tkp,tks->tps", page_hit, live).reshape(row_count, 1, positions)
+    present = count > 0
+    masked = jnp.where(present, scores, -jnp.inf)
     row_peak = jnp.max(masked, axis=2, keepdims=True)
-    expons = jnp.where(live_mask, jnp.exp(scores - row_peak), 0.0)
-    probs = (expons / jnp.sum(expons, axis=2, keepdims=True)).astype(jnp.bfloat16)
-    latent_out = jnp.einsum("thl,tlr->thr", probs, keys_lat, preferred_element_type=jnp.float32)
+    expons = jnp.where(present, jnp.exp(scores - row_peak), 0.0)
+    total = jnp.sum(expons * count, axis=2, keepdims=True)
+    probs = (expons / total).astype(jnp.bfloat16)
+    weighted = (probs.astype(jnp.float32) * count).astype(jnp.bfloat16)
+    latent_out = jnp.einsum("thp,pr->thr", weighted, keys_lat, preferred_element_type=jnp.float32)
     return latent_out.astype(jnp.bfloat16)
 
 
@@ -60,6 +70,7 @@
 ):
     replicas = lax.axis_size("rep")
     expert_groups = lax.axis_size("ep")
+    rep_index = lax.axis_index("rep")
     latent_out = attend_rows(
         query_latent, query_rope, cache_latent, cache_rope, page_table, lengths
     )
@@ -86,6 +97,7 @@
     capacity = max(
         replicas, min(group_rows, 2 * group_rows * route_count // experts // replicas * replicas)
     )
+    share = capacity // replicas
     expert_ids = jnp.arange(experts, dtype=jnp.int32)
     slot_index = jnp.sum(jnp.where(routes[:, :, None] == expert_ids, placement, 0), axis=2).reshape(
         -1
@@ -98,38 +110,50 @@
         jnp.full((experts * capacity,), group_rows, jnp.int32)
         .at[slot_index * capacity + position]
         .set(jnp.arange(assignments, dtype=jnp.int32) // route_count)
-    )
+    ).reshape(experts, capacity)
+    own_source = lax.dynamic_slice_in_dim(source_row, rep_index * share, share, 1).reshape(-1)
     padded = jnp.concatenate([hidden, jnp.zeros((1, model_width), jnp.bfloat16)], axis=0)
-    outgoing = padded[source_row].reshape(expert_groups, per_group * capacity, model_width)
-    incoming = lax.all_to_all(outgoing, "ep", split_axis=0, concat_axis=0, tiled=True).reshape(
-        expert_groups, per_group, capacity, model_width
+    outgoing = padded[own_source].reshape(expert_groups, per_group * share, model_width)
+    incoming = lax.all_to_all(outgoing, "ep", split_axis=0, concat_axis=0, tiled=True)
+    gathered = lax.all_gather(incoming, "rep", axis=0, tiled=False).reshape(
+        replicas, expert_groups, per_group, share, model_width
     )
     gate_values = jnp.einsum(
-        "secd,edf->secf", incoming, expert_gate, preferred_element_type=jnp.float32
+        "qsecd,edf->qsecf", gathered, expert_gate, preferred_element_type=jnp.float32
     )
     up_values = jnp.einsum(
-        "secd,edf->secf", incoming, expert_up, preferred_element_type=jnp.float32
+        "qsecd,edf->qsecf", gathered, expert_up, preferred_element_type=jnp.float32
     )
     activated = (jax.nn.silu(gate_values) * up_values).astype(jnp.bfloat16)
     expert_terms = jnp.einsum(
-        "secf,efd->secd", activated, expert_down, preferred_element_type=jnp.float32
+        "qsecf,efd->qsecd", activated, expert_down, preferred_element_type=jnp.float32
+    ).astype(jnp.bfloat16)
+    summed = lax.psum_scatter(expert_terms, "rep", scatter_dimension=0, tiled=True).reshape(
+        expert_groups, per_group * share, model_width
     )
-    outbound = expert_terms.astype(jnp.bfloat16).reshape(
-        expert_groups, per_group * capacity, model_width
+    returned = lax.all_to_all(summed, "ep", split_axis=0, concat_axis=0, tiled=True).reshape(
+        experts * share, model_width
     )
-    returned = lax.all_to_all(outbound, "ep", split_axis=0, concat_axis=0, tiled=True)
-    picked = returned.reshape(experts * capacity, model_width)[slot_index * capacity + position]
-    weight_used = route_weight.reshape(-1)
-    routed = jnp.sum(
-        (picked.astype(jnp.float32) * weight_used[:, None]).reshape(
-            group_rows, route_count, model_width
-        ),
+    local_pos = position - rep_index * share
+    mine = (local_pos >= 0) & (local_pos < share)
+    column = slot_index * share + jnp.clip(local_pos, 0, share - 1)
+    weight_used = jnp.where(mine, route_weight.reshape(-1), 0.0)
+    combine = jnp.sum(
+        jnp.where(
+            column[:, None] == jnp.arange(experts * share, dtype=jnp.int32)[None, :],
+            weight_used[:, None],
+            0.0,
+        ).reshape(group_rows, route_count, experts * share),
         axis=1,
+    )
+    routed = jnp.dot(
+        combine, returned.astype(jnp.float32), precision=lax.Precision.HIGHEST,
+        preferred_element_type=jnp.float32,
     )
     row_sums = lax.psum_scatter(
         (routed + shared_terms).astype(jnp.bfloat16), "rep", scatter_dimension=0, tiled=True
     ).astype(jnp.float32)
-    own_hidden = lax.dynamic_slice_in_dim(hidden, lax.axis_index("rep") * own_count, own_count, 0)
+    own_hidden = lax.dynamic_slice_in_dim(hidden, rep_index * own_count, own_count, 0)
     mixed = row_sums + own_hidden.astype(jnp.float32)
     inverse = lax.rsqrt(jnp.mean(mixed * mixed, axis=1, keepdims=True) + EPSILON)
     return (mixed * inverse * norm_gain).astype(jnp.bfloat16)

time: 388 us -> 296 us (0.76)
  blocking collectives: 108 us -> 40.6 us
  local copies, waits for them, and re-layouts: 56.4 us -> 20 us
  waiting for transfers between devices: 159 us -> 170 us
    all_to_all x1, blocking collectives: 108 us -> 40.6 us  [per_device(): lax.all_to_all(outgoing, 'ep', split_axis=0, concat_axis=0, tiled=True)]
    all_to_all x1, waiting for transfers between devices: 92.3 us -> 25.4 us  [per_device(): lax.all_to_all(summed, 'ep', split_axis=0, concat_axis=0, tiled=True)]
    reduce_scatter x0 -> x1, waiting for transfers between devices: none -> 41.3 us  [per_device(): lax.psum_scatter(expert_terms, 'rep', scatter_dimension=0, tiled=True)]
    all_gather x0 -> x1, waiting for transfers between devices: none -> 38.2 us  [per_device(): lax.all_gather(incoming, 'rep', axis=0, tiled=False)]
    gather x4 -> x1, local copies, waits for them, and re-layouts: 22.2 us -> 2.02 us  [per_device(): padded[own_source].reshape(expert_groups, per_group * share, model_width)]
    convert_element_type x2 -> x0, local copies, waits for them, and re-layouts: 9.57 us -> none  [the longest x1 5.66 us: per_device(): expert_terms.astype(jnp.bfloat16)]
    reshape x3 -> x7, local copies, waits for them, and re-layouts: 14.4 us -> 9.2 us  [the longest x1 2.8 us: per_device(): lax.psum_scatter(expert_terms, 'rep', scatter_dimension=0, tiled=True)]
    dot_general x5 -> x7, matrix products: 19.6 us -> 19.8 us  [the longest x1 8.22 us: per_device(): jnp.einsum('qsecf,efd->qsecd', activated, expert_down, preferred_element_...]
  transfers between devices with their start and end apart: 4 -> 6, of which waited for: 4 -> 5; matrix products, arithmetic and copies ran while one was open for 2% -> 3% of each run, Pallas kernels for 0% -> 0%
where the time goes in v1:
time: 296 us; the launch traced here: 294 us
  waiting for transfers between devices  170 us (57%)
  blocking collectives  40.6 us (14%)
  matrix products  26.9 us (9%)
  local copies, waits for them, and re-layouts  20 us (7%)
  starting transfers between devices  16.1 us (5%)
  between operations  13.4 us (5%)
  other arithmetic  6.52 us (2%)
    psum x1, waiting for transfers between devices, per_device(): attended = lax.psum(attn_terms.astype(jnp.bfloat16), 'rep')  48.5 us
    reduce_scatter x1, waiting for transfers between devices, per_device(): lax.psum_scatter(expert_terms, 'rep', scatter_dimension=0, tiled=True)  41.3 us
    all_to_all x1, blocking collectives, per_device(): lax.all_to_all(outgoing, 'ep', split_axis=0, concat_axis=0, tiled=True)  40.6 us
    all_gather x1, waiting for transfers between devices, per_device(): lax.all_gather(incoming, 'rep', axis=0, tiled=False)  38.2 us
    all_to_all x1, waiting for transfers between devices, per_device(): lax.all_to_all(summed, 'ep', split_axis=0, concat_axis=0, tiled=True)  25.4 us
    reduce_scatter x1, waiting for transfers between devices, per_device(): lax.psum_scatter((routed + shared_terms).astype(jnp.bfloat16), 'rep', sca...  16.6 us
    all_to_all x1, starting transfers between devices, per_device(): lax.all_to_all(summed, 'ep', split_axis=0, concat_axis=0, tiled=True)  10.9 us
    dot_general x1, matrix products, per_device(): jnp.einsum('qsecf,efd->qsecd', activated, expert_down, preferred_element_...  8.22 us
  transfers between devices with their start and end apart: 6, of which 5 were waited for; matrix products, arithmetic and copies ran while one was open for 3% of the time, Pallas kernels for 0%

profile of v1, /device:TPU:1, one launch (start us, length us, event | category | flops | bytes accessed | tf_op | source)
XLA Modules:
  0.0 293.6 jit_solution(4660298371691227361)
XLA Ops:
  6.5 1.2 copy.67
  7.7 1.2 reshape.224
  8.9 0.9 reshape.223
  9.9 1.0 fusion.77
  10.9 0.1 reshape.220
  11.1 1.7 fusion.104
  12.8 0.3 fusion.31
  13.1 1.3 fusion.26
  14.4 2.1 fusion.62
  16.5 0.8 copy.52
  17.3 4.8 %all-to-all-start = ((bf16[16,16,512]{2,0,1:T(8,128)(2,1)}), bf16[16,16,512]{2,0,1:T(8,128)(2,1)S(1)}, u32[]{:S(2)}, u32[]{:S(2)}) async-start(bf16[16,16,512]{2,0,1:T(8,128)(2,1)} %copy.52), calls=%async_computation | async-start | bytes 524288 | tf_op jit(solution)/shard_map/all_to_all | solution.py:78
  22.2 0.3 select_reduce_fusion.2
  22.4 0.1 copy.45
  22.5 0.1 eq.72
  22.7 0.1 eq.68
  22.9 0.9 reduce-window.6
  23.8 0.2 slice_reduce_fusion
  24.0 0.1 fusion.81
  24.2 0.1 min.12
  24.4 0.1 copy.55
  24.5 0.2 mul.105
  24.7 2.9 scatter_custom_fusion
  27.8 0.1 reshape.227
  28.0 0.2 fusion.66
  28.2 1.2 convolution_convert_fusion.1
  29.5 48.5 %all-reduce.3.cloned.1.call-done = bf16[64,2048]{1,0:T(8,128)(2,1)} async-done(((bf16[64,2048]{1,0:T(8,128)(2,1)}), bf16[64,2048]{1,0:T(8,128)(2,1)}) %all-reduce.3.cloned.1.call-update) | async-done | bytes 262160 | tf_op jit(solution)/shard_map/psum | solution.py:86
  78.0 1.0 add_convert_fusion
  79.0 2.0 gather_fusion
  81.0 2.4 reshape.228
  83.5 40.6 %all_to_all.28 = bf16[64,3,2048]{2,1,0:T(4,128)(2,1)S(1)} all-to-all(bf16[64,3,2048]{2,1,0:T(4,128)(2,1)S(1)} %reshape.228), channel_id=1, replica_groups=mesh['ep'=64,'rep'=4] {'ep'}, dimensions={0} | all-to-all | bytes 1572864 | tf_op jit(solution)/shard_map/all_to_all | solution.py:117
  124.1 1.5 copy.56
  125.6 0.2 reduce-scatter.3.cloned.1.call-start
  125.8 38.2 %all-gather.3.cloned.1.call-done = bf16[256,3,2048]{2,0,1:T(8,128)(2,1)} async-done(((bf16[64,3,2048]{2,0,1:T(8,128)(2,1)}), bf16[256,3,2048]{2,0,1:T(8,128)(2,1)}) %all-gather.3.cloned.1.call-update) | async-done | bytes 3145744 | tf_op jit(solution)/shard_map/all_gather | solution.py:118
  164.0 5.1 %fusion.11 = f32[4,64,1,3,352]{4,1,3,0,2:T(8,128)} fusion(bf16[1,2048,352]{1,2,0:T(8,128)(2,1)} %param.31, bf16[4,64,3,2048]{3,1,0,2:T(8,128)(2,1)} %bitcast.127), kind=kOutput, calls=%fused_computation.16 | convolution fusion | flops 1107296256 | bytes 5668864 | tf_op jit(solution)/shard_map/qsecd,edf->qsecf/dot_general | solution.py:121
  169.2 8.2 %fusion.2 = bf16[4,64,1,3,2048]{4,1,3,0,2:T(8,128)(2,1)} fusion(bf16[1,352,2048]{2,1,0:T(8,128)(2,1)} %param.33, bf16[1,2048,352]{1,2,0:T(8,128)(2,1)} %param.32, bf16[4,64,3,2048]{3,1,0,2:T(8,128)(2,1)} %bitcast.128, f32[4,64,1,3,352]{4,1,3,0,2:T(8,128)} %fusion.11), kind=kOutput, calls=%fused_computation.5 | convolution fusion | flops 2217787392 | bytes 10256384 | tf_op jit(solution)/shard_map/qsecf,efd->qsecd/dot_general | solution.py:128
  177.4 41.3 %reduce-scatter.3.cloned.1.call-done = bf16[1,64,1,3,2048]{4,1,3,0,2:T(8,128)(2,1)} async-done(((bf16[4,64,1,3,2048]{4,1,3,0,2:T(8,128)(2,1)}), bf16[1,64,1,3,2048]{4,1,3,0,2:T(8,128)(2,1)}) %reduce-scatter.3.cloned.1.call-update) | async-done | bytes 786448 | tf_op jit(solution)/shard_map/reduce_scatter | solution.py:131
  218.7 2.8 copy.59
  221.5 10.9 %all-to-all-start.2 = ((bf16[64,3,2048]{2,1,0:T(4,128)(2,1)}), bf16[64,3,2048]{2,1,0:T(4,128)(2,1)}, u32[]{:S(2)}, u32[]{:S(2)}) async-start(bf16[64,3,2048]{2,1,0:T(4,128)(2,1)} %copy.59), calls=%async_computation.3 | async-start | bytes 2097152 | tf_op jit(solution)/shard_map/all_to_all | solution.py:134
  232.5 0.1 and.16
  232.8 0.2 select_reduce_fusion.1
  233.0 1.9 fusion.106
  235.0 25.4 %all-to-all-done.2 = bf16[64,3,2048]{2,1,0:T(4,128)(2,1)} async-done(((bf16[64,3,2048]{2,1,0:T(4,128)(2,1)}), bf16[64,3,2048]{2,1,0:T(4,128)(2,1)}, u32[]{:S(2)}, u32[]{:S(2)}) %all-to-all-start.2) | async-done | bytes 786464 | tf_op jit(solution)/shard_map/all_to_all | solution.py:134
  260.3 2.4 reshape.234
  262.8 1.3 fusion.105
  264.1 3.8 %fusion.7 = bf16[64,2048]{1,0:T(8,128)(2,1)} fusion(f32[64,2048]{1,0:T(8,128)} %fusion.105, bf16[352,2048]{1,0:T(8,128)(2,1)} %param.36, bf16[64,2048]{1,0:T(8,128)(2,1)S(1)} %add_convert_fusion, bf16[2048,352]{0,1:T(8,128)(2,1)} %param.35, f32[64,352]{1,0:T(8,128)S(1)} %fusion.106), kind=kOutput, calls=%fused_computation.11 | convolution fusion | flops 184946688 | bytes 4022272 | tf_op jit(solution)/shard_map/dot_general | solution.py:93
  267.9 16.6 %reduce-scatter.5.cloned.1.call-done = bf16[16,2048]{1,0:T(8,128)(2,1)} async-done(((bf16[64,2048]{1,0:T(8,128)(2,1)}), bf16[16,2048]{1,0:T(8,128)(2,1)}) %reduce-scatter.5.cloned.1.call-update) | async-done | bytes 65552 | tf_op jit(solution)/shard_map/reduce_scatter | solution.py:153
  284.5 1.0 multiply_reduce_fusion.1
  285.5 1.6 multiply_convert_fusion
  (45 shorter events, 0.9 us)
Async XLA Ops:
  6.5 21.7 %copy-start = (bf16[512,2048]{1,0:T(8,128)(2,1)S(1)}, bf16[512,2048]{1,0:T(8,128)(2,1)}, u32[]{:S(2)}) copy-start(bf16[512,2048]{1,0:T(8,128)(2,1)} %param.27) | copy-start | bytes 6291460
  13.1 1.3 copy-start.1
  14.4 7.8 %copy-start.6 = (s32[64,6]{0,1:T(8,128)S(1)}, s32[64,6]{0,1:T(8,128)}, u32[]{:S(2)}) copy-start(s32[64,6]{0,1:T(8,128)} %param.28) | copy-start | bytes 4612
  14.4 7.8 %copy-start.7 = (s32[64]{0:T(128)S(1)}, s32[64]{0:T(128)}, u32[]{:S(2)}) copy-start(s32[64]{0:T(128)} %param.30) | copy-start | bytes 772
  16.5 11.5 %copy-start.2 = (bf16[4,512,128]{2,1,0:T(8,128)(2,1)S(1)}, bf16[4,512,128]{2,1,0:T(8,128)(2,1)}, u32[]{:S(2)}) copy-start(bf16[4,512,128]{2,1,0:T(8,128)(2,1)} %param.26) | copy-start | bytes 1572868
  17.3 10.6 %all-to-all-start = ((bf16[16,16,512]{2,0,1:T(8,128)(2,1)}), bf16[16,16,512]{2,0,1:T(8,128)(2,1)S(1)}, u32[]{:S(2)}, u32[]{:S(2)}) async-start(bf16[16,16,512]{2,0,1:T(8,128)(2,1)} %copy.52), calls=%async_computation | async-start | bytes 524288 | tf_op jit(solution)/shard_map/all_to_all | solution.py:78
  22.2 55.8 %all-reduce.3.cloned.1.call-start = ((), (), s32[]{:S(2)}) async-start(), calls=%async_computation.5 | async-start | bytes 524288 | tf_op jit(solution)/shard_map/psum | solution.py:86
  28.2 49.8 %copy-start.3 = (bf16[64,2048]{1,0:T(8,128)(2,1)S(1)}, bf16[64,2048]{1,0:T(8,128)(2,1)}, u32[]{:S(2)}) copy-start(bf16[64,2048]{1,0:T(8,128)(2,1)} %param.19) | copy-start | bytes 786436
  29.4 134.6 %all-gather.3.cloned.1.call-start = ((), (), s32[]{:S(2)}) async-start(), calls=%async_computation.8 | async-start | bytes 3932160 | tf_op jit(solution)/shard_map/all_gather | solution.py:118
  125.6 93.1 %reduce-scatter.3.cloned.1.call-start = ((), (), s32[]{:S(2)}) async-start(), calls=%async_computation.6 | async-start | bytes 3932160 | tf_op jit(solution)/shard_map/reduce_scatter | solution.py:131
  221.5 11.2 %copy-start.5 = (f32[64,6]{0,1:T(8,128)S(1)}, f32[64,6]{0,1:T(8,128)}, u32[]{:S(2)}) copy-start(f32[64,6]{0,1:T(8,128)} %param.29) | copy-start | bytes 4612
  221.5 38.8 %all-to-all-start.2 = ((bf16[64,3,2048]{2,1,0:T(4,128)(2,1)}), bf16[64,3,2048]{2,1,0:T(4,128)(2,1)}, u32[]{:S(2)}, u32[]{:S(2)}) async-start(bf16[64,3,2048]{2,1,0:T(4,128)(2,1)} %copy.59), calls=%async_computation.3 | async-start | bytes 2097152 | tf_op jit(solution)/shard_map/all_to_all | solution.py:134
  232.4 52.1 %reduce-scatter.5.cloned.1.call-start = ((), (), s32[]{:S(2)}) async-start(), calls=%async_computation.7 | async-start | bytes 327680 | tf_op jit(solution)/shard_map/reduce_scatter | solution.py:153
  264.1 21.4 %copy-start.4 = (f32[2048]{0:T(1024)S(1)}, f32[2048]{0:T(1024)}, u32[]{:S(2)}) copy-start(f32[2048]{0:T(1024)} %param.37) | copy-start | bytes 24580
Sparse Core Ops, SparseCore 0:
  29.6 48.3 all-reduce.2
  125.7 38.3 all-gather.2
  177.6 41.0 reduce-scatter.2
  268.0 16.4 reduce-scatter.4

commit v2 on v1

--- a/solution.py
+++ b/solution.py
@@ -45,6 +45,10 @@
     weighted = (probs.astype(jnp.float32) * count).astype(jnp.bfloat16)
     latent_out = jnp.einsum("thp,pr->thr", weighted, keys_lat, preferred_element_type=jnp.float32)
     return latent_out.astype(jnp.bfloat16)
+
+
+def rep_exchange(blocks):
+    return lax.all_to_all(blocks, "rep", split_axis=0, concat_axis=0, tiled=True)
 
 
 def per_device(
@@ -83,9 +87,16 @@
     attn_terms = jnp.dot(
         head_out.reshape(group_rows, -1), out_proj, preferred_element_type=jnp.float32
     )
-    attended = lax.psum(attn_terms.astype(jnp.bfloat16), "rep")
-    hidden = (residual.astype(jnp.float32) + attended.astype(jnp.float32)).astype(jnp.bfloat16)
-    model_width = hidden.shape[1]
+    model_width = attn_terms.shape[1]
+    terms_in = rep_exchange(attn_terms.astype(jnp.bfloat16).reshape(replicas, own_count, model_width))
+    attended = jnp.sum(terms_in.astype(jnp.float32), axis=0).astype(jnp.bfloat16)
+    own_residual = lax.dynamic_slice_in_dim(residual, rep_index * own_count, own_count, 0)
+    own_hidden = (own_residual.astype(jnp.float32) + attended.astype(jnp.float32)).astype(
+        jnp.bfloat16
+    )
+    hidden = rep_exchange(
+        jnp.broadcast_to(own_hidden[None], (replicas, own_count, model_width))
+    ).reshape(group_rows, model_width)
     shared_act = (
         jax.nn.silu(jnp.dot(hidden, shared_gate, preferred_element_type=jnp.float32))
         * jnp.dot(hidden, shared_up, preferred_element_type=jnp.float32)
@@ -115,7 +126,7 @@
     padded = jnp.concatenate([hidden, jnp.zeros((1, model_width), jnp.bfloat16)], axis=0)
     outgoing = padded[own_source].reshape(expert_groups, per_group * share, model_width)
     incoming = lax.all_to_all(outgoing, "ep", split_axis=0, concat_axis=0, tiled=True)
-    gathered = lax.all_gather(incoming, "rep", axis=0, tiled=False).reshape(
+    gathered = rep_exchange(jnp.broadcast_to(incoming[None], (replicas,) + incoming.shape)).reshape(
         replicas, expert_groups, per_group, share, model_width
     )
     gate_values = jnp.einsum(
@@ -128,8 +139,10 @@
     expert_terms = jnp.einsum(
         "qsecf,efd->qsecd", activated, expert_down, preferred_element_type=jnp.float32
     ).astype(jnp.bfloat16)
-    summed = lax.psum_scatter(expert_terms, "rep", scatter_dimension=0, tiled=True).reshape(
-        expert_groups, per_group * share, model_width
+    summed = (
+        jnp.sum(rep_exchange(expert_terms).astype(jnp.float32), axis=0)
+        .astype(jnp.bfloat16)
+        .reshape(expert_groups, per_group * share, model_width)
     )
     returned = lax.all_to_all(summed, "ep", split_axis=0, concat_axis=0, tiled=True).reshape(
         experts * share, model_width
@@ -150,10 +163,12 @@
         combine, returned.astype(jnp.float32), precision=lax.Precision.HIGHEST,
         preferred_element_type=jnp.float32,
     )
-    row_sums = lax.psum_scatter(
-        (routed + shared_terms).astype(jnp.bfloat16), "rep", scatter_dimension=0, tiled=True
-    ).astype(jnp.float32)
-    own_hidden = lax.dynamic_slice_in_dim(hidden, rep_index * own_count, own_count, 0)
+    row_sums = jnp.sum(
+        rep_exchange(
+            (routed + shared_terms).astype(jnp.bfloat16).reshape(replicas, own_count, model_width)
+        ).astype(jnp.float32),
+        axis=0,
+    )
     mixed = row_sums + own_hidden.astype(jnp.float32)
     inverse = lax.rsqrt(jnp.mean(mixed * mixed, axis=1, keepdims=True) + EPSILON)
     return (mixed * inverse * norm_gain).astype(jnp.bfloat16)

time: 296 us -> 239 us (0.81)
  waiting for transfers between devices: 170 us -> 35.6 us
  blocking collectives: 40.6 us -> 129 us
  between operations: 13.4 us -> 0.33 us
  starting transfers between devices: 16.1 us -> 22.3 us
    all_to_all x0 -> x3, blocking collectives: none -> 85.2 us  [rep_exchange(): lax.all_to_all(blocks, 'rep', split_axis=0, concat_axis=0, tiled=True)]
    reduce_scatter x2 -> x0, waiting for transfers between devices: 57.9 us -> none  [the longest x1 41.3 us: per_device(): lax.psum_scatter(expert_terms, 'rep', scatter_dimension=0, tiled=True)]
    psum x1 -> x0, waiting for transfers between devices: 48.5 us -> none  [per_device(): attended = lax.psum(attn_terms.astype(jnp.bfloat16), 'rep')]
    all_gather x1 -> x0, waiting for transfers between devices: 38.2 us -> none  [per_device(): lax.all_gather(incoming, 'rep', axis=0, tiled=False)]
    all_to_all x0 -> x2, waiting for transfers between devices: none -> 7.69 us  [rep_exchange(): lax.all_to_all(blocks, 'rep', split_axis=0, concat_axis=0, tiled=True)]
    all_to_all x0 -> x2, starting transfers between devices: none -> 6.81 us  [rep_exchange(): lax.all_to_all(blocks, 'rep', split_axis=0, concat_axis=0, tiled=True)]
    all_to_all x1, blocking collectives: 40.6 us -> 43.8 us  [per_device(): lax.all_to_all(outgoing, 'ep', split_axis=0, concat_axis=0, tiled=True)]
    all_to_all x1, waiting for transfers between devices: 0.01 us -> 3.03 us  [per_device(): lax.all_to_all(latent_out, 'rep', split_axis=1, concat_axis=0, tiled=True)]
  transfers between devices with their start and end apart: 6 -> 4, of which waited for: 5 -> 4; matrix products, arithmetic and copies ran while one was open for 3% -> 4% of each run, Pallas kernels for 0% -> 0%
where the time goes in v2:
time: 239 us; the launch traced here: 237 us
  blocking collectives  129 us (54%)
  waiting for transfers between devices  35.6 us (15%)
  matrix products  24.8 us (10%)
  starting transfers between devices  22.3 us (9%)
  local copies, waits for them, and re-layouts  19.8 us (8%)
  other arithmetic  5.35 us (2%)
    all_to_all x3, blocking collectives, rep_exchange(): lax.all_to_all(blocks, 'rep', split_axis=0, concat_axis=0, tiled=True)  85.2 us
    all_to_all x1, blocking collectives, per_device(): lax.all_to_all(outgoing, 'ep', split_axis=0, concat_axis=0, tiled=True)  43.8 us
    all_to_all x1, waiting for transfers between devices, per_device(): lax.all_to_all(summed, 'ep', split_axis=0, concat_axis=0, tiled=True)  24.9 us
    all_to_all x1, starting transfers between devices, per_device(): lax.all_to_all(summed, 'ep', split_axis=0, concat_axis=0, tiled=True)  10.6 us
    dot_general x1, matrix products, per_device(): jnp.einsum('qsecf,efd->qsecd', activated, expert_down, preferred_element_...  8.22 us
    all_to_all x2, waiting for transfers between devices, rep_exchange(): lax.all_to_all(blocks, 'rep', split_axis=0, concat_axis=0, tiled=True)  7.69 us
    all_to_all x2, starting transfers between devices, rep_exchange(): lax.all_to_all(blocks, 'rep', split_axis=0, concat_axis=0, tiled=True)  6.81 us
    all_to_all x1, starting transfers between devices, per_device(): lax.all_to_all(latent_out, 'rep', split_axis=1, concat_axis=0, tiled=True)  4.84 us
  transfers between devices with their start and end apart: 4, of which 4 were waited for; matrix products, arithmetic and copies ran while one was open for 4% of the time, Pallas kernels for 0%

profile of v2, /device:TPU:1, one launch (start us, length us, event | category | flops | bytes accessed | tf_op | source)
XLA Modules:
  0.0 237.2 jit_solution(1358578430401753667)
XLA Ops:
  0.0 1.2 copy.76
  1.2 1.2 reshape.235
  2.4 0.9 reshape.234
  3.3 1.0 fusion.63
  4.4 0.1 reshape.231
  4.5 1.7 fusion.90
  6.2 0.3 fusion.28
  6.5 1.3 fusion.23
  7.8 2.1 fusion.50
  9.9 0.8 copy.61
  10.8 4.8 %all-to-all-start = ((bf16[16,16,512]{2,0,1:T(8,128)(2,1)}), bf16[16,16,512]{2,0,1:T(8,128)(2,1)S(1)}, u32[]{:S(2)}, u32[]{:S(2)}) async-start(bf16[16,16,512]{2,0,1:T(8,128)(2,1)} %copy.61), calls=%async_computation | async-start | bytes 524288 | tf_op jit(solution)/shard_map/all_to_all | solution.py:82
  15.6 0.3 select_reduce_fusion.2
  16.0 0.1 eq.72
  16.3 0.9 reduce-window.6
  17.2 0.2 slice_reduce_fusion
  17.9 0.2 mul.106
  18.1 3.0 %all-to-all-done = bf16[16,16,512]{2,0,1:T(8,128)(2,1)S(1)} async-done(((bf16[16,16,512]{2,0,1:T(8,128)(2,1)}), bf16[16,16,512]{2,0,1:T(8,128)(2,1)S(1)}, u32[]{:S(2)}, u32[]{:S(2)}) %all-to-all-start) | async-done | bytes 262176 | tf_op jit(solution)/shard_map/all_to_all | solution.py:82
  21.2 0.2 fusion.54
  21.4 1.2 convolution_convert_fusion.1
  22.6 3.4 %all-to-all-start.1 = ((bf16[4,16,2048]{2,1,0:T(8,128)(2,1)}), bf16[4,16,2048]{2,1,0:T(8,128)(2,1)S(1)}, u32[]{:S(2)}, u32[]{:S(2)}) async-start(bf16[4,16,2048]{2,1,0:T(8,128)(2,1)} %bitcast.8), calls=%async_computation.1 | async-start | bytes 524288 | tf_op jit(solution)/shard_map/all_to_all | solution.py:51
  26.0 2.9 %scatter_custom_fusion = s32[768]{0:T(1024)S(1)} fusion(s32[384]{0:T(512)S(1)} %fusion.85, s32[384]{0:T(512)S(1)} %add_select_fusion, s32[]{:T(128)} %constant.26.clone.1), kind=kCustom, calls=%fused_computation.91 | custom fusion | bytes 3076 | tf_op jit(solution)/shard_map/scatter | solution.py:123
  29.3 2.2 all-to-all-done.1
  31.6 0.9 add_convert_fusion
  32.4 0.7 broadcast_in_dim.84
  33.1 3.4 %all-to-all-start.2 = ((bf16[4,16,2048]{2,1,0:T(8,128)(2,1)}), bf16[4,16,2048]{2,1,0:T(8,128)(2,1)S(1)}, u32[]{:S(2)}, u32[]{:S(2)}) async-start(bf16[4,16,2048]{2,1,0:T(8,128)(2,1)} %broadcast_in_dim.84), calls=%async_computation.2 | async-start | bytes 524288 | tf_op jit(solution)/shard_map/all_to_all | solution.py:51
  36.6 5.5 %all-to-all-done.2 = bf16[4,16,2048]{2,1,0:T(8,128)(2,1)S(1)} async-done(((bf16[4,16,2048]{2,1,0:T(8,128)(2,1)}), bf16[4,16,2048]{2,1,0:T(8,128)(2,1)S(1)}, u32[]{:S(2)}, u32[]{:S(2)}) %all-to-all-start.2) | async-done | bytes 262176 | tf_op jit(solution)/shard_map/all_to_all | solution.py:51
  42.1 2.0 gather_fusion
  44.1 2.4 %reshape.241 = bf16[64,3,2048]{2,1,0:T(4,128)(2,1)S(1)} reshape(bf16[192,2048]{1,0:T(8,128)(2,1)} %gather_fusion) | data formatting | bytes 1572864 | tf_op jit(solution)/shard_map/reshape | solution.py:127
  46.5 43.8 %all_to_all.53 = bf16[64,3,2048]{2,1,0:T(4,128)(2,1)S(1)} all-to-all(bf16[64,3,2048]{2,1,0:T(4,128)(2,1)S(1)} %reshape.241), channel_id=1, replica_groups=mesh['ep'=64,'rep'=4] {'ep'}, dimensions={0} | all-to-all | bytes 1572864 | tf_op jit(solution)/shard_map/all_to_all | solution.py:128
  90.4 0.6 copy.65
  90.9 0.4 broadcast_in_dim.86
  91.3 38.6 %all_to_all.54 = bf16[4,64,3,2048]{3,1,2,0:T(8,128)(2,1)S(1)} all-to-all(bf16[4,64,3,2048]{3,1,2,0:T(8,128)(2,1)S(1)} %broadcast_in_dim.86), channel_id=1, replica_groups=mesh['ep'=64,'rep'=4] {'rep'}, dimensions={0} | all-to-all | bytes 6291456 | tf_op jit(solution)/shard_map/all_to_all | solution.py:51
  129.9 1.7 copy-done.1
  131.6 2.8 %fusion.9 = f32[4,64,1,3,352]{4,1,3,0,2:T(8,128)} fusion(bf16[4,64,3,2048]{3,1,2,0:T(8,128)(2,1)S(1)} %all_to_all.54, bf16[1,2048,352]{1,2,0:T(8,128)(2,1)S(1)} %copy-done.9), kind=kOutput, calls=%fused_computation.15 | convolution fusion | flops 1107296256 | bytes 5668864 | tf_op jit(solution)/shard_map/qsecd,edf->qsecf/dot_general | solution.py:132
  134.5 8.2 %fusion.2 = bf16[4,64,1,3,2048]{4,1,3,2,0:T(8,128)(2,1)} fusion(bf16[1,352,2048]{2,1,0:T(8,128)(2,1)} %param.33, bf16[4,64,3,2048]{3,1,2,0:T(8,128)(2,1)} %copy-done.1, bf16[1,2048,352]{1,2,0:T(8,128)(2,1)} %param.32, f32[4,64,1,3,352]{4,1,3,0,2:T(8,128)} %fusion.9), kind=kOutput, calls=%fused_computation.6 | convolution fusion | flops 2217787392 | bytes 10256384 | tf_op jit(solution)/shard_map/qsecf,efd->qsecd/dot_general | solution.py:139
  142.7 38.7 %all_to_all.55 = bf16[4,64,1,3,2048]{4,1,3,2,0:T(8,128)(2,1)S(1)} all-to-all(bf16[4,64,1,3,2048]{4,1,3,2,0:T(8,128)(2,1)} %fusion.2), channel_id=1, replica_groups=mesh['ep'=64,'rep'=4] {'rep'}, dimensions={0} | all-to-all | bytes 6291456 | tf_op jit(solution)/shard_map/all_to_all | solution.py:51
  181.4 0.6 bitcast_reduce_fusion
  182.0 1.7 copy.68
  183.6 10.6 %all-to-all-start.6 = ((bf16[64,3,2048]{2,1,0:T(4,128)(2,1)}), bf16[64,3,2048]{2,1,0:T(4,128)(2,1)S(1)}, u32[]{:S(2)}, u32[]{:S(2)}) async-start(bf16[64,3,2048]{2,1,0:T(4,128)(2,1)} %copy.68), calls=%async_computation.6 | async-start | bytes 2097152 | tf_op jit(solution)/shard_map/all_to_all | solution.py:147
  194.3 0.1 and.16
  194.6 0.2 select_reduce_fusion.1
  194.8 2.6 %fusion.92 = f32[64,352]{1,0:T(8,128)} fusion(bf16[64,2048]{1,0:T(8,128)(2,1)S(1)} %bitcast.126, bf16[2048,352]{0,1:T(8,128)(2,1)} %param.34), kind=kOutput, calls=%fused_computation.106 | convolution fusion | flops 92274688 | bytes 1794048 | tf_op jit(solution)/shard_map/dot_general | solution.py:101
  197.4 24.9 %all-to-all-done.6 = bf16[64,3,2048]{2,1,0:T(4,128)(2,1)S(1)} async-done(((bf16[64,3,2048]{2,1,0:T(4,128)(2,1)}), bf16[64,3,2048]{2,1,0:T(4,128)(2,1)S(1)}, u32[]{:S(2)}, u32[]{:S(2)}) %all-to-all-start.6) | async-done | bytes 786464 | tf_op jit(solution)/shard_map/all_to_all | solution.py:147
  222.2 1.4 reshape.246
  223.7 1.7 fusion.91
  225.4 3.0 %fusion.3 = bf16[64,2048]{1,0:T(8,128)(2,1)S(1)} fusion(f32[64,2048]{1,0:T(8,128)S(1)} %fusion.91, bf16[352,2048]{1,0:T(8,128)(2,1)} %param.36, bf16[64,2048]{1,0:T(8,128)(2,1)S(1)} %bitcast.127, bf16[2048,352]{0,1:T(8,128)(2,1)} %param.35, f32[64,352]{1,0:T(8,128)S(1)} %copy-done.4), kind=kOutput, calls=%fused_computation.8 | convolution fusion | flops 184946688 | bytes 4022272 | tf_op jit(solution)/shard_map/dot_general | solution.py:104
  228.4 7.9 %all_to_all.56 = bf16[4,16,2048]{2,1,0:T(8,128)(2,1)S(1)} all-to-all(bf16[4,16,2048]{2,1,0:T(8,128)(2,1)S(1)} %bitcast.133), channel_id=1, replica_groups=mesh['ep'=64,'rep'=4] {'rep'}, dimensions={0} | all-to-all | bytes 524288 | tf_op jit(solution)/shard_map/all_to_all | solution.py:51
  236.5 0.7 multiply_convert_fusion
  (49 shorter events, 1.6 us)
Async XLA Ops:
  0.0 21.4 %copy-start = (bf16[512,2048]{1,0:T(8,128)(2,1)S(1)}, bf16[512,2048]{1,0:T(8,128)(2,1)}, u32[]{:S(2)}) copy-start(bf16[512,2048]{1,0:T(8,128)(2,1)} %param.27) | copy-start | bytes 6291460
  6.5 1.3 copy-start.2
  7.8 7.8 %copy-start.7 = (s32[64,6]{0,1:T(8,128)S(1)}, s32[64,6]{0,1:T(8,128)}, u32[]{:S(2)}) copy-start(s32[64,6]{0,1:T(8,128)} %param.28) | copy-start | bytes 4612
  7.8 7.8 %copy-start.8 = (s32[64]{0:T(128)S(1)}, s32[64]{0:T(128)}, u32[]{:S(2)}) copy-start(s32[64]{0:T(128)} %param.30) | copy-start | bytes 772
  9.9 11.2 %copy-start.3 = (bf16[4,512,128]{2,1,0:T(8,128)(2,1)S(1)}, bf16[4,512,128]{2,1,0:T(8,128)(2,1)}, u32[]{:S(2)}) copy-start(bf16[4,512,128]{2,1,0:T(8,128)(2,1)} %param.26) | copy-start | bytes 1572868
  10.8 10.4 %all-to-all-start = ((bf16[16,16,512]{2,0,1:T(8,128)(2,1)}), bf16[16,16,512]{2,0,1:T(8,128)(2,1)S(1)}, u32[]{:S(2)}, u32[]{:S(2)}) async-start(bf16[16,16,512]{2,0,1:T(8,128)(2,1)} %copy.61), calls=%async_computation | async-start | bytes 524288 | tf_op jit(solution)/shard_map/all_to_all | solution.py:82
  22.6 8.9 %all-to-all-start.1 = ((bf16[4,16,2048]{2,1,0:T(8,128)(2,1)}), bf16[4,16,2048]{2,1,0:T(8,128)(2,1)S(1)}, u32[]{:S(2)}, u32[]{:S(2)}) async-start(bf16[4,16,2048]{2,1,0:T(8,128)(2,1)} %bitcast.8), calls=%async_computation.1 | async-start | bytes 524288 | tf_op jit(solution)/shard_map/all_to_all | solution.py:51
  33.1 8.9 %all-to-all-start.2 = ((bf16[4,16,2048]{2,1,0:T(8,128)(2,1)}), bf16[4,16,2048]{2,1,0:T(8,128)(2,1)S(1)}, u32[]{:S(2)}, u32[]{:S(2)}) async-start(bf16[4,16,2048]{2,1,0:T(8,128)(2,1)} %broadcast_in_dim.84), calls=%async_computation.2 | async-start | bytes 524288 | tf_op jit(solution)/shard_map/all_to_all | solution.py:51
  91.3 40.3 %copy-start.9 = (bf16[1,2048,352]{1,2,0:T(8,128)(2,1)S(1)}, bf16[1,2048,352]{1,2,0:T(8,128)(2,1)}, u32[]{:S(2)}) copy-start(bf16[1,2048,352]{1,2,0:T(8,128)(2,1)} %param.31) | copy-start | bytes 4325380
  129.9 1.7 copy-start.1
  183.6 10.8 %copy-start.6 = (f32[64,6]{0,1:T(8,128)S(1)}, f32[64,6]{0,1:T(8,128)}, u32[]{:S(2)}) copy-start(f32[64,6]{0,1:T(8,128)} %param.29) | copy-start | bytes 4612
  183.6 38.6 %all-to-all-start.6 = ((bf16[64,3,2048]{2,1,0:T(4,128)(2,1)}), bf16[64,3,2048]{2,1,0:T(4,128)(2,1)S(1)}, u32[]{:S(2)}, u32[]{:S(2)}) async-start(bf16[64,3,2048]{2,1,0:T(4,128)(2,1)} %copy.68), calls=%async_computation.6 | async-start | bytes 2097152 | tf_op jit(solution)/shard_map/all_to_all | solution.py:147
  223.7 1.7 copy-start.4
  225.4 11.1 %copy-start.5 = (f32[2048]{0:T(1024)S(1)}, f32[2048]{0:T(1024)}, u32[]{:S(2)}) copy-start(f32[2048]{0:T(1024)} %param.37) | copy-start | bytes 24580

commit v3 on v2

--- a/solution.py
+++ b/solution.py
@@ -1,8 +1,11 @@
+import functools
 import math
 
 import jax
 import jax.numpy as jnp
 from jax import lax
+from jax.experimental import pallas as pl
+from jax.experimental.pallas import tpu as pltpu
 from jax.sharding import PartitionSpec as P
 
 ROPE = 64
@@ -45,6 +48,70 @@
     weighted = (probs.astype(jnp.float32) * count).astype(jnp.bfloat16)
     latent_out = jnp.einsum("thp,pr->thr", weighted, keys_lat, preferred_element_type=jnp.float32)
     return latent_out.astype(jnp.bfloat16)
+
+
+def _exchange_kernel(axis, other, src_ref, out_ref, send_sems, recv_sems, local_sem):
+    count = src_ref.shape[0]
+    me = lax.axis_index(axis)
+    fixed = lax.axis_index(other)
+
+    def device(peer):
+        return (peer, fixed) if axis == "ep" else (fixed, peer)
+
+    def remote(peer, slot):
+        return pltpu.make_async_remote_copy(
+            src_ref.at[peer],
+            out_ref.at[slot],
+            send_sems.at[peer],
+            recv_sems.at[slot],
+            device_id=device(peer),
+            device_id_type=pl.DeviceIdType.MESH,
+        )
+
+    barrier = pltpu.get_barrier_semaphore()
+
+    def greet(step, carry):
+        peer = lax.rem(me + step, count)
+        pl.semaphore_signal(
+            barrier, 1, device_id=device(peer), device_id_type=pl.DeviceIdType.MESH
+        )
+        return carry
+
+    lax.fori_loop(1, count, greet, 0)
+    pl.semaphore_wait(barrier, count - 1)
+    local = pltpu.make_async_copy(src_ref.at[me], out_ref.at[me], local_sem)
+    local.start()
+
+    def send(step, carry):
+        remote(lax.rem(me + step, count), me).start()
+        return carry
+
+    lax.fori_loop(1, count, send, 0)
+
+    def finish(step, carry):
+        peer = lax.rem(me + step, count)
+        remote(peer, me).wait_send()
+        remote(peer, peer).wait_recv()
+        return carry
+
+    lax.fori_loop(1, count, finish, 0)
+    local.wait()
+
+
+def exchange(blocks, axis, other, collective_id):
+    count = blocks.shape[0]
+    return pl.pallas_call(
+        functools.partial(_exchange_kernel, axis, other),
+        out_shape=jax.ShapeDtypeStruct(blocks.shape, blocks.dtype),
+        in_specs=[pl.BlockSpec(memory_space=pl.ANY)],
+        out_specs=pl.BlockSpec(memory_space=pl.ANY),
+        scratch_shapes=[
+            pltpu.SemaphoreType.DMA((count,)),
+            pltpu.SemaphoreType.DMA((count,)),
+            pltpu.SemaphoreType.DMA(()),
+        ],
+        compiler_params=pltpu.CompilerParams(collective_id=collective_id, has_side_effects=True),
+    )(blocks)
 
 
 def rep_exchange(blocks):
@@ -125,7 +192,7 @@
     own_source = lax.dynamic_slice_in_dim(source_row, rep_index * share, share, 1).reshape(-1)
     padded = jnp.concatenate([hidden, jnp.zeros((1, model_width), jnp.bfloat16)], axis=0)
     outgoing = padded[own_source].reshape(expert_groups, per_group * share, model_width)
-    incoming = lax.all_to_all(outgoing, "ep", split_axis=0, concat_axis=0, tiled=True)
+    incoming = exchange(outgoing, "ep", "rep", 0)
     gathered = rep_exchange(jnp.broadcast_to(incoming[None], (replicas,) + incoming.shape)).reshape(
         replicas, expert_groups, per_group, share, model_width
     )
@@ -144,7 +211,7 @@
         .astype(jnp.bfloat16)
         .reshape(expert_groups, per_group * share, model_width)
     )
-    returned = lax.all_to_all(summed, "ep", split_axis=0, concat_axis=0, tiled=True).reshape(
+    returned = exchange(summed, "ep", "rep", 1).reshape(
         experts * share, model_width
     )
     local_pos = position - rep_index * share

time: 239 us -> 238 us (level)
  blocking collectives: 129 us -> 48.8 us
  Pallas kernels: 0 us -> 73.8 us
  waiting for transfers between devices: 35.6 us -> 44.8 us
  starting transfers between devices: 22.3 us -> 16.6 us
    pallas_call x0 -> x2, Pallas kernels: none -> 73.8 us  [exchange(): pl.pallas_call(functools.partial(_exchange_kernel, axis, other), out_shap...]
    all_to_all x1 -> x0, blocking collectives: 43.8 us -> none  [per_device(): lax.all_to_all(outgoing, 'ep', split_axis=0, concat_axis=0, tiled=True)]
    all_to_all x3 -> x2, blocking collectives: 85.2 us -> 48.8 us  [rep_exchange(): lax.all_to_all(blocks, 'rep', split_axis=0, concat_axis=0, tiled=True)]
    all_to_all x2 -> x3, waiting for transfers between devices: 7.69 us -> 41.7 us  [rep_exchange(): lax.all_to_all(blocks, 'rep', split_axis=0, concat_axis=0, tiled=True)]
    all_to_all x1 -> x0, waiting for transfers between devices: 24.9 us -> none  [per_device(): lax.all_to_all(summed, 'ep', split_axis=0, concat_axis=0, tiled=True)]
    all_to_all x1 -> x0, starting transfers between devices: 10.6 us -> none  [per_device(): lax.all_to_all(summed, 'ep', split_axis=0, concat_axis=0, tiled=True)]
    all_to_all x2 -> x3, starting transfers between devices: 6.81 us -> 11.8 us  [rep_exchange(): lax.all_to_all(blocks, 'rep', split_axis=0, concat_axis=0, tiled=True)]
  transfers between devices with their start and end apart: 4 -> 4, of which waited for: 4 -> 4; matrix products, arithmetic and copies ran while one was open for 4% -> 3% of each run, Pallas kernels for 0% -> 0%
where the time goes in v3:
time: 238 us; the launch traced here: 236 us
  Pallas kernels  73.8 us (31%)
  blocking collectives  48.8 us (21%)
  waiting for transfers between devices  44.8 us (19%)
  matrix products  23.9 us (10%)
  local copies, waits for them, and re-layouts  20 us (8%)
  starting transfers between devices  16.6 us (7%)
  other arithmetic  7.23 us (3%)
    pallas_call x2, Pallas kernels, exchange(): pl.pallas_call(functools.partial(_exchange_kernel, axis, other), out_shap...  73.8 us
    all_to_all x2, blocking collectives, rep_exchange(): lax.all_to_all(blocks, 'rep', split_axis=0, concat_axis=0, tiled=True)  48.8 us
    all_to_all x3, waiting for transfers between devices, rep_exchange(): lax.all_to_all(blocks, 'rep', split_axis=0, concat_axis=0, tiled=True)  41.7 us
    all_to_all x3, starting transfers between devices, rep_exchange(): lax.all_to_all(blocks, 'rep', split_axis=0, concat_axis=0, tiled=True)  11.8 us
    dot_general x1, matrix products, per_device(): jnp.einsum('qsecf,efd->qsecd', activated, expert_down, preferred_element_...  8.19 us
    all_to_all x1, starting transfers between devices, per_device(): lax.all_to_all(latent_out, 'rep', split_axis=1, concat_axis=0, tiled=True)  4.84 us
  transfers between devices with their start and end apart: 4, of which 4 were waited for; matrix products, arithmetic and copies ran while one was open for 3% of the time, Pallas kernels for 0%

profile of v3, /device:TPU:1, one launch (start us, length us, event | category | flops | bytes accessed | tf_op | source)
XLA Modules:
  0.0 235.5 jit_solution(5335127290558495428)
XLA Ops:
  0.0 1.2 copy.65
  1.2 1.2 reshape.235
  2.4 0.9 reshape.234
  3.3 1.0 fusion.63
  4.4 0.1 reshape.231
  4.5 1.7 fusion.90
  6.2 0.3 fusion.28
  6.5 1.3 fusion.23
  7.8 2.1 fusion.50
  9.9 0.8 copy.50
  10.8 4.8 %all-to-all-start = ((bf16[16,16,512]{2,0,1:T(8,128)(2,1)}), bf16[16,16,512]{2,0,1:T(8,128)(2,1)S(1)}, u32[]{:S(2)}, u32[]{:S(2)}) async-start(bf16[16,16,512]{2,0,1:T(8,128)(2,1)} %copy.50), calls=%async_computation | async-start | bytes 524288 | tf_op jit(solution)/shard_map/all_to_all | solution.py:149
  15.6 0.3 select_reduce_fusion.2
  16.0 0.1 eq.72
  16.3 0.9 reduce-window.6
  17.2 0.2 slice_reduce_fusion
  17.9 0.2 mul.106
  18.1 3.0 %all-to-all-done = bf16[16,16,512]{2,0,1:T(8,128)(2,1)S(1)} async-done(((bf16[16,16,512]{2,0,1:T(8,128)(2,1)}), bf16[16,16,512]{2,0,1:T(8,128)(2,1)S(1)}, u32[]{:S(2)}, u32[]{:S(2)}) %all-to-all-start) | async-done | bytes 262176 | tf_op jit(solution)/shard_map/all_to_all | solution.py:149
  21.2 0.2 fusion.54
  21.4 1.2 convolution_convert_fusion.1
  22.6 3.4 %all-to-all-start.1 = ((bf16[4,16,2048]{2,1,0:T(8,128)(2,1)}), bf16[4,16,2048]{2,1,0:T(8,128)(2,1)S(1)}, u32[]{:S(2)}, u32[]{:S(2)}) async-start(bf16[4,16,2048]{2,1,0:T(8,128)(2,1)} %bitcast.8), calls=%async_computation.1 | async-start | bytes 524288 | tf_op jit(solution)/shard_map/all_to_all | solution.py:118
  26.0 2.9 %scatter_custom_fusion = s32[768]{0:T(1024)S(1)} fusion(s32[384]{0:T(512)S(1)} %fusion.85, s32[384]{0:T(512)S(1)} %add_select_fusion, s32[]{:T(128)} %constant.26.clone.1), kind=kCustom, calls=%fused_computation.91 | custom fusion | bytes 3076 | tf_op jit(solution)/shard_map/scatter | solution.py:190
  29.3 2.2 all-to-all-done.1
  31.6 0.9 add_convert_fusion
  32.4 0.7 broadcast_in_dim.84
  33.1 3.4 %all-to-all-start.2 = ((bf16[4,16,2048]{2,1,0:T(8,128)(2,1)}), bf16[4,16,2048]{2,1,0:T(8,128)(2,1)S(1)}, u32[]{:S(2)}, u32[]{:S(2)}) async-start(bf16[4,16,2048]{2,1,0:T(8,128)(2,1)} %broadcast_in_dim.84), calls=%async_computation.2 | async-start | bytes 524288 | tf_op jit(solution)/shard_map/all_to_all | solution.py:118
  36.6 5.5 %all-to-all-done.2 = bf16[4,16,2048]{2,1,0:T(8,128)(2,1)S(1)} async-done(((bf16[4,16,2048]{2,1,0:T(8,128)(2,1)}), bf16[4,16,2048]{2,1,0:T(8,128)(2,1)S(1)}, u32[]{:S(2)}, u32[]{:S(2)}) %all-to-all-start.2) | async-done | bytes 262176 | tf_op jit(solution)/shard_map/all_to_all | solution.py:118
  42.1 1.1 gather_fusion
  43.2 1.3 reshape.241.src_ref
  44.5 39.7 %shard_map.181 = bf16[64,3,2048]{2,1,0:T(4,128)(2,1)} custom-call(bf16[64,3,2048]{2,1,0:T(4,128)(2,1)} %reshape.241.src_ref), custom_call_target="tpu_custom_call" | custom-call | tf_op jit(solution)/shard_map/pallas_call | solution.py:103
  84.2 1.8 copy.54
  86.0 0.4 broadcast_in_dim.86
  86.4 40.0 %all_to_all.43 = bf16[4,64,3,2048]{3,1,2,0:T(8,128)(2,1)S(1)} all-to-all(bf16[4,64,3,2048]{3,1,2,0:T(8,128)(2,1)S(1)} %broadcast_in_dim.86), channel_id=1, replica_groups=mesh['ep'=64,'rep'=4] {'rep'}, dimensions={0} | all-to-all | bytes 6291456 | tf_op jit(solution)/shard_map/all_to_all | solution.py:118
  126.5 1.7 copy-done.1
  128.2 2.8 %fusion.9 = f32[4,64,1,3,352]{4,1,3,0,2:T(8,128)} fusion(bf16[4,64,3,2048]{3,1,2,0:T(8,128)(2,1)S(1)} %all_to_all.43, bf16[1,2048,352]{1,2,0:T(8,128)(2,1)S(1)} %copy-done.8), kind=kOutput, calls=%fused_computation.15 | convolution fusion | flops 1107296256 | bytes 5668864 | tf_op jit(solution)/shard_map/qsecd,edf->qsecf/dot_general | solution.py:199
  131.0 8.2 %fusion.2 = bf16[4,64,1,3,2048]{4,1,3,2,0:T(8,128)(2,1)} fusion(bf16[1,352,2048]{2,1,0:T(8,128)(2,1)} %param.33, bf16[4,64,3,2048]{3,1,2,0:T(8,128)(2,1)} %copy-done.1, bf16[1,2048,352]{1,2,0:T(8,128)(2,1)} %param.32, f32[4,64,1,3,352]{4,1,3,0,2:T(8,128)} %fusion.9), kind=kOutput, calls=%fused_computation.6 | convolution fusion | flops 2217787392 | bytes 10256384 | tf_op jit(solution)/shard_map/qsecf,efd->qsecd/dot_general | solution.py:206
  139.2 5.0 %all-to-all-start.4 = ((bf16[4,64,1,3,2048]{4,1,3,2,0:T(8,128)(2,1)}), bf16[4,64,1,3,2048]{4,1,3,2,0:T(8,128)(2,1)}, u32[]{:S(2)}, u32[]{:S(2)}) async-start(bf16[4,64,1,3,2048]{4,1,3,2,0:T(8,128)(2,1)} %fusion.2), calls=%async_computation.4 | async-start | bytes 6291456 | tf_op jit(solution)/shard_map/all_to_all | solution.py:118
  144.2 0.1 and.16
  144.5 0.2 select_reduce_fusion.1
  144.7 1.9 fusion.92
  146.6 34.0 %all-to-all-done.4 = bf16[4,64,1,3,2048]{4,1,3,2,0:T(8,128)(2,1)} async-done(((bf16[4,64,1,3,2048]{4,1,3,2,0:T(8,128)(2,1)}), bf16[4,64,1,3,2048]{4,1,3,2,0:T(8,128)(2,1)}, u32[]{:S(2)}, u32[]{:S(2)}) %all-to-all-start.4) | async-done | bytes 3145760 | tf_op jit(solution)/shard_map/all_to_all | solution.py:118
  180.7 2.5 %bitcast_reduce_fusion = bf16[64,3,2048]{2,0,1:T(8,128)(2,1)S(1)} fusion(bf16[4,64,1,3,2048]{4,1,3,2,0:T(8,128)(2,1)} %all-to-all-done.4), kind=kLoop, calls=%fused_computation.5 | loop fusion | flops 1179648 | bytes 3932160 | tf_op jit(solution)/shard_map/reduce_sum | solution.py:210
  183.2 1.7 copy.57.src_ref
  184.8 34.1 %shard_map.182 = bf16[64,3,2048]{2,1,0:T(4,128)(2,1)} custom-call(bf16[64,3,2048]{2,1,0:T(4,128)(2,1)} %copy.57.src_ref), custom_call_target="tpu_custom_call" | custom-call | tf_op jit(solution)/shard_map/pallas_call | solution.py:103
  218.9 2.4 %reshape.246 = bf16[192,2048]{1,0:T(8,128)(2,1)S(1)} reshape(bf16[64,3,2048]{2,1,0:T(4,128)(2,1)} %shard_map.182) | data formatting | bytes 1572864 | tf_op jit(solution)/shard_map/reshape | solution.py:214
  221.3 1.3 fusion.91
  222.7 3.1 %fusion.3 = bf16[64,2048]{1,0:T(8,128)(2,1)S(1)} fusion(f32[64,2048]{1,0:T(8,128)} %fusion.91, bf16[352,2048]{1,0:T(8,128)(2,1)} %param.36, bf16[64,2048]{1,0:T(8,128)(2,1)S(1)} %bitcast.127, bf16[2048,352]{0,1:T(8,128)(2,1)} %param.35, f32[64,352]{1,0:T(8,128)S(1)} %fusion.92), kind=kOutput, calls=%fused_computation.8 | convolution fusion | flops 184946688 | bytes 4022272 | tf_op jit(solution)/shard_map/dot_general | solution.py:171
  225.8 8.8 %all_to_all.44 = bf16[4,16,2048]{2,1,0:T(8,128)(2,1)S(1)} all-to-all(bf16[4,16,2048]{2,1,0:T(8,128)(2,1)S(1)} %bitcast.133), channel_id=1, replica_groups=mesh['ep'=64,'rep'=4] {'rep'}, dimensions={0} | all-to-all | bytes 524288 | tf_op jit(solution)/shard_map/all_to_all | solution.py:118
  234.8 0.7 multiply_convert_fusion
  (47 shorter events, 1.6 us)
Async XLA Ops:
  0.0 21.4 %copy-start = (bf16[512,2048]{1,0:T(8,128)(2,1)S(1)}, bf16[512,2048]{1,0:T(8,128)(2,1)}, u32[]{:S(2)}) copy-start(bf16[512,2048]{1,0:T(8,128)(2,1)} %param.27) | copy-start | bytes 6291460
  6.5 1.3 copy-start.2
  7.8 7.8 %copy-start.6 = (s32[64,6]{0,1:T(8,128)S(1)}, s32[64,6]{0,1:T(8,128)}, u32[]{:S(2)}) copy-start(s32[64,6]{0,1:T(8,128)} %param.28) | copy-start | bytes 4612
  7.8 7.8 %copy-start.7 = (s32[64]{0:T(128)S(1)}, s32[64]{0:T(128)}, u32[]{:S(2)}) copy-start(s32[64]{0:T(128)} %param.30) | copy-start | bytes 772
  9.9 11.2 %copy-start.3 = (bf16[4,512,128]{2,1,0:T(8,128)(2,1)S(1)}, bf16[4,512,128]{2,1,0:T(8,128)(2,1)}, u32[]{:S(2)}) copy-start(bf16[4,512,128]{2,1,0:T(8,128)(2,1)} %param.26) | copy-start | bytes 1572868
  10.8 10.4 %all-to-all-start = ((bf16[16,16,512]{2,0,1:T(8,128)(2,1)}), bf16[16,16,512]{2,0,1:T(8,128)(2,1)S(1)}, u32[]{:S(2)}, u32[]{:S(2)}) async-start(bf16[16,16,512]{2,0,1:T(8,128)(2,1)} %copy.50), calls=%async_computation | async-start | bytes 524288 | tf_op jit(solution)/shard_map/all_to_all | solution.py:149
  22.6 8.9 %all-to-all-start.1 = ((bf16[4,16,2048]{2,1,0:T(8,128)(2,1)}), bf16[4,16,2048]{2,1,0:T(8,128)(2,1)S(1)}, u32[]{:S(2)}, u32[]{:S(2)}) async-start(bf16[4,16,2048]{2,1,0:T(8,128)(2,1)} %bitcast.8), calls=%async_computation.1 | async-start | bytes 524288 | tf_op jit(solution)/shard_map/all_to_all | solution.py:118
  33.1 8.9 %all-to-all-start.2 = ((bf16[4,16,2048]{2,1,0:T(8,128)(2,1)}), bf16[4,16,2048]{2,1,0:T(8,128)(2,1)S(1)}, u32[]{:S(2)}, u32[]{:S(2)}) async-start(bf16[4,16,2048]{2,1,0:T(8,128)(2,1)} %broadcast_in_dim.84), calls=%async_computation.2 | async-start | bytes 524288 | tf_op jit(solution)/shard_map/all_to_all | solution.py:118
  86.4 41.7 %copy-start.8 = (bf16[1,2048,352]{1,2,0:T(8,128)(2,1)S(1)}, bf16[1,2048,352]{1,2,0:T(8,128)(2,1)}, u32[]{:S(2)}) copy-start(bf16[1,2048,352]{1,2,0:T(8,128)(2,1)} %param.31) | copy-start | bytes 4325380
  126.5 1.7 copy-start.1
  139.2 5.1 %copy-start.5 = (f32[64,6]{0,1:T(8,128)S(1)}, f32[64,6]{0,1:T(8,128)}, u32[]{:S(2)}) copy-start(f32[64,6]{0,1:T(8,128)} %param.29) | copy-start | bytes 4612
  139.2 41.5 %all-to-all-start.4 = ((bf16[4,64,1,3,2048]{4,1,3,2,0:T(8,128)(2,1)}), bf16[4,64,1,3,2048]{4,1,3,2,0:T(8,128)(2,1)}, u32[]{:S(2)}, u32[]{:S(2)}) async-start(bf16[4,64,1,3,2048]{4,1,3,2,0:T(8,128)(2,1)} %fusion.2), calls=%async_computation.4 | async-start | bytes 6291456 | tf_op jit(solution)/shard_map/all_to_all | solution.py:118
  222.7 12.1 %copy-start.4 = (f32[2048]{0:T(1024)S(1)}, f32[2048]{0:T(1024)}, u32[]{:S(2)}) copy-start(f32[2048]{0:T(1024)} %param.37) | copy-start | bytes 24580

commit v4 on v3

--- a/solution.py
+++ b/solution.py
@@ -111,6 +111,104 @@
             pltpu.SemaphoreType.DMA(()),
         ],
         compiler_params=pltpu.CompilerParams(collective_id=collective_id, has_side_effects=True),
+    )(blocks)
+
+
+def _dispatch_kernel(src_ref, out_ref, ep_send, ep_recv, local_sem, x_send, x_recv):
+    chunks, groups = src_ref.shape[0], src_ref.shape[1]
+    replicas = out_ref.shape[1]
+    me_e = lax.axis_index("ep")
+    me_r = lax.axis_index("rep")
+    mesh_id = pl.DeviceIdType.MESH
+
+    def ep_copy(c, peer, slot):
+        return pltpu.make_async_remote_copy(
+            src_ref.at[c, peer],
+            out_ref.at[c, me_r, slot],
+            ep_send.at[c, peer],
+            ep_recv.at[c, slot],
+            device_id=(peer, me_r),
+            device_id_type=mesh_id,
+        )
+
+    def x_copy(c, peer, slot):
+        return pltpu.make_async_remote_copy(
+            out_ref.at[c, me_r],
+            out_ref.at[c, slot],
+            x_send.at[c, peer],
+            x_recv.at[c, slot],
+            device_id=(me_e, peer),
+            device_id_type=mesh_id,
+        )
+
+    barrier = pltpu.get_barrier_semaphore()
+
+    def greet(step, carry):
+        pl.semaphore_signal(
+            barrier, 1, device_id=(lax.rem(me_e + step, groups), me_r), device_id_type=mesh_id
+        )
+        return carry
+
+    lax.fori_loop(1, groups, greet, 0)
+    for step in range(1, replicas):
+        pl.semaphore_signal(
+            barrier, 1, device_id=(me_e, lax.rem(me_r + step, replicas)), device_id_type=mesh_id
+        )
+    pl.semaphore_wait(barrier, groups - 1 + replicas - 1)
+
+    locals_ = []
+    for c in range(chunks):
+        local = pltpu.make_async_copy(src_ref.at[c, me_e], out_ref.at[c, me_r, me_e], local_sem.at[c])
+        local.start()
+        locals_.append(local)
+
+        def send(step, carry, c=c):
+            ep_copy(c, lax.rem(me_e + step, groups), me_e).start()
+            return carry
+
+        lax.fori_loop(1, groups, send, 0)
+
+    for c in range(chunks):
+        locals_[c].wait()
+
+        def arrive(step, carry, c=c):
+            peer = lax.rem(me_e + step, groups)
+            ep_copy(c, peer, peer).wait_recv()
+            return carry
+
+        lax.fori_loop(1, groups, arrive, 0)
+        for step in range(1, replicas):
+            x_copy(c, lax.rem(me_r + step, replicas), me_r).start()
+
+    for c in range(chunks):
+        for step in range(1, replicas):
+            peer = lax.rem(me_r + step, replicas)
+            x_copy(c, peer, me_r).wait_send()
+            x_copy(c, peer, peer).wait_recv()
+
+        def sent(step, carry, c=c):
+            ep_copy(c, lax.rem(me_e + step, groups), me_e).wait_send()
+            return carry
+
+        lax.fori_loop(1, groups, sent, 0)
+
+
+def dispatch(blocks, replicas):
+    chunks, groups = blocks.shape[:2]
+    out_shape = (chunks, replicas) + blocks.shape[1:]
+    return pl.pallas_call(
+        _dispatch_kernel,
+        out_shape=jax.ShapeDtypeStruct(out_shape, blocks.dtype),
+        in_specs=[pl.BlockSpec(memory_space=pl.ANY)],
+        out_specs=pl.BlockSpec(memory_space=pl.ANY),
+        scratch_shapes=[
+            pltpu.SemaphoreType.DMA((chunks, groups)),
+            pltpu.SemaphoreType.DMA((chunks, groups)),
+            pltpu.SemaphoreType.DMA((chunks,)),
+            pltpu.SemaphoreType.DMA((chunks, replicas)),
+            pltpu.SemaphoreType.DMA((chunks, replicas)),
+        ],
+        compiler_params=pltpu.CompilerParams(collective_id=2, has_side_effects=True),
     )(blocks)
 
 
@@ -171,7 +269,7 @@
     shared_terms = jnp.dot(shared_act, shared_down, preferred_element_type=jnp.float32)
     experts = placement.shape[0]
     route_count = routes.shape[1]
-    per_group = experts // expert_groups
+    assert experts == expert_groups
     capacity = max(
         replicas, min(group_rows, 2 * group_rows * route_count // experts // replicas * replicas)
     )
@@ -189,29 +287,23 @@
         .at[slot_index * capacity + position]
         .set(jnp.arange(assignments, dtype=jnp.int32) // route_count)
     ).reshape(experts, capacity)
-    own_source = lax.dynamic_slice_in_dim(source_row, rep_index * share, share, 1).reshape(-1)
+    own_source = lax.dynamic_slice_in_dim(source_row, rep_index * share, share, 1).T.reshape(-1)
     padded = jnp.concatenate([hidden, jnp.zeros((1, model_width), jnp.bfloat16)], axis=0)
-    outgoing = padded[own_source].reshape(expert_groups, per_group * share, model_width)
-    incoming = exchange(outgoing, "ep", "rep", 0)
-    gathered = rep_exchange(jnp.broadcast_to(incoming[None], (replicas,) + incoming.shape)).reshape(
-        replicas, expert_groups, per_group, share, model_width
-    )
+    lanes = 128
+    outgoing = padded[own_source].reshape(share, experts, model_width // lanes, lanes)
+    gathered = dispatch(outgoing, replicas).reshape(share, replicas, expert_groups, model_width)
     gate_values = jnp.einsum(
-        "qsecd,edf->qsecf", gathered, expert_gate, preferred_element_type=jnp.float32
+        "cqgd,df->cqgf", gathered, expert_gate[0], preferred_element_type=jnp.float32
     )
     up_values = jnp.einsum(
-        "qsecd,edf->qsecf", gathered, expert_up, preferred_element_type=jnp.float32
+        "cqgd,df->cqgf", gathered, expert_up[0], preferred_element_type=jnp.float32
     )
     activated = (jax.nn.silu(gate_values) * up_values).astype(jnp.bfloat16)
     expert_terms = jnp.einsum(
-        "qsecf,efd->qsecd", activated, expert_down, preferred_element_type=jnp.float32
+        "cqgf,fd->qcgd", activated, expert_down[0], preferred_element_type=jnp.float32
     ).astype(jnp.bfloat16)
-    summed = (
-        jnp.sum(rep_exchange(expert_terms).astype(jnp.float32), axis=0)
-        .astype(jnp.bfloat16)
-        .reshape(expert_groups, per_group * share, model_width)
-    )
-    returned = exchange(summed, "ep", "rep", 1).reshape(
+    summed = jnp.sum(rep_exchange(expert_terms).astype(jnp.float32), axis=0).astype(jnp.bfloat16)
+    returned = exchange(jnp.transpose(summed, (1, 0, 2)), "ep", "rep", 1).reshape(
         experts * share, model_width
     )
     local_pos = position - rep_index * share

time: 238 us -> 229 us (0.962)
  blocking collectives: 48.8 us -> 9.54 us
  Pallas kernels: 73.8 us -> 96.2 us
  local copies, waits for them, and re-layouts: 20 us -> 25.7 us
    pallas_call x0 -> x1, Pallas kernels: none -> 63 us  [dispatch(): pl.pallas_call(_dispatch_kernel, out_shape=jax.ShapeDtypeStruct(out_shape...]
    pallas_call x2 -> x1, Pallas kernels: 73.8 us -> 33.2 us  [exchange(): pl.pallas_call(functools.partial(_exchange_kernel, axis, other), out_shap...]
    all_to_all x2 -> x1, blocking collectives: 48.8 us -> 9.54 us  [rep_exchange(): lax.all_to_all(blocks, 'rep', split_axis=0, concat_axis=0, tiled=True)]
    reshape x2, local copies, waits for them, and re-layouts: 3.72 us -> 8.23 us  [the longest x1 5.82 us: per_device(): dispatch(outgoing, replicas)]
    convert_element_type x0 -> x1, local copies, waits for them, and re-layouts: none -> 3.97 us  [per_device(): expert_terms = jnp.einsum('cqgf,fd->qcgd', activated, expert_down[0], pre...]
  transfers between devices with their start and end apart: 4 -> 4, of which waited for: 4 -> 4; matrix products, arithmetic and copies ran while one was open for 3% -> 4% of each run, Pallas kernels for 0% -> 0%
where the time goes in v4:
time: 229 us; the launch traced here: 227 us
  Pallas kernels  96.2 us (42%)
  waiting for transfers between devices  44.7 us (20%)
  matrix products  26.2 us (11%)
  local copies, waits for them, and re-layouts  25.7 us (11%)
  starting transfers between devices  16.6 us (7%)
  blocking collectives  9.54 us (4%)
  other arithmetic  7.33 us (3%)
    pallas_call x1, Pallas kernels, dispatch(): pl.pallas_call(_dispatch_kernel, out_shape=jax.ShapeDtypeStruct(out_shape...  63 us
    all_to_all x3, waiting for transfers between devices, rep_exchange(): lax.all_to_all(blocks, 'rep', split_axis=0, concat_axis=0, tiled=True)  41.7 us
    pallas_call x1, Pallas kernels, exchange(): pl.pallas_call(functools.partial(_exchange_kernel, axis, other), out_shap...  33.2 us
    all_to_all x3, starting transfers between devices, rep_exchange(): lax.all_to_all(blocks, 'rep', split_axis=0, concat_axis=0, tiled=True)  11.8 us
    all_to_all x1, blocking collectives, rep_exchange(): lax.all_to_all(blocks, 'rep', split_axis=0, concat_axis=0, tiled=True)  9.54 us
    dot_general x1, matrix products, per_device(): jnp.einsum('cqgf,fd->qcgd', activated, expert_down[0], preferred_element_...  8.22 us
    reshape x1, local copies, waits for them, and re-layouts, per_device(): dispatch(outgoing, replicas)  5.82 us
    dot_general x1, matrix products, per_device(): jnp.einsum('cqgd,df->cqgf', gathered, expert_gate[0], preferred_element_t...  5.15 us
  transfers between devices with their start and end apart: 4, of which 4 were waited for; matrix products, arithmetic and copies ran while one was open for 4% of the time, Pallas kernels for 0%

profile of v4, /device:TPU:1, one launch (start us, length us, event | category | flops | bytes accessed | tf_op | source)
XLA Modules:
  0.0 226.6 jit_solution(7181570083726554137)
XLA Ops:
  0.0 1.2 copy.65
  1.2 1.2 reshape.213
  2.4 0.9 reshape.212
  3.3 1.0 fusion.54
  4.4 0.1 reshape.209
  4.5 1.7 fusion.81
  6.2 0.3 fusion.22
  6.5 1.3 fusion.17
  7.8 2.1 fusion.41
  9.9 0.8 copy.49
  10.8 4.8 %all-to-all-start = ((bf16[16,16,512]{2,0,1:T(8,128)(2,1)}), bf16[16,16,512]{2,0,1:T(8,128)(2,1)S(1)}, u32[]{:S(2)}, u32[]{:S(2)}) async-start(bf16[16,16,512]{2,0,1:T(8,128)(2,1)} %copy.49), calls=%async_computation | async-start | bytes 524288 | tf_op jit(solution)/shard_map/all_to_all | solution.py:247
  15.6 0.3 select_reduce_fusion.2
  16.0 0.1 eq.72
  16.1 0.1 eq.68
  16.3 0.9 reduce-window.6
  17.2 0.2 slice_reduce_fusion
  17.9 0.2 mul.106
  18.1 3.0 %all-to-all-done = bf16[16,16,512]{2,0,1:T(8,128)(2,1)S(1)} async-done(((bf16[16,16,512]{2,0,1:T(8,128)(2,1)}), bf16[16,16,512]{2,0,1:T(8,128)(2,1)S(1)}, u32[]{:S(2)}, u32[]{:S(2)}) %all-to-all-start) | async-done | bytes 262176 | tf_op jit(solution)/shard_map/all_to_all | solution.py:247
  21.2 0.2 fusion.45
  21.4 1.2 convolution_convert_fusion.1
  22.6 3.4 %all-to-all-start.1 = ((bf16[4,16,2048]{2,1,0:T(8,128)(2,1)}), bf16[4,16,2048]{2,1,0:T(8,128)(2,1)S(1)}, u32[]{:S(2)}, u32[]{:S(2)}) async-start(bf16[4,16,2048]{2,1,0:T(8,128)(2,1)} %bitcast.8), calls=%async_computation.1 | async-start | bytes 524288 | tf_op jit(solution)/shard_map/all_to_all | solution.py:216
  26.0 2.9 %scatter_custom_fusion = s32[768]{0:T(1024)S(1)} fusion(s32[384]{0:T(512)S(1)} %fusion.76, s32[384]{0:T(512)S(1)} %add_select_fusion, s32[]{:T(128)} %constant.26.clone.1), kind=kCustom, calls=%fused_computation.89 | custom fusion | bytes 3076 | tf_op jit(solution)/shard_map/scatter | solution.py:288
  29.3 2.2 all-to-all-done.1
  31.6 0.9 add_convert_fusion
  32.4 0.7 broadcast_in_dim.78
  33.1 3.6 %all-to-all-start.2 = ((bf16[4,16,2048]{2,1,0:T(8,128)(2,1)}), bf16[4,16,2048]{2,1,0:T(8,128)(2,1)S(1)}, u32[]{:S(2)}, u32[]{:S(2)}) async-start(bf16[4,16,2048]{2,1,0:T(8,128)(2,1)} %broadcast_in_dim.78), calls=%async_computation.2 | async-start | bytes 524288 | tf_op jit(solution)/shard_map/all_to_all | solution.py:216
  36.8 5.3 %all-to-all-done.2 = bf16[4,16,2048]{2,1,0:T(8,128)(2,1)S(1)} async-done(((bf16[4,16,2048]{2,1,0:T(8,128)(2,1)}), bf16[4,16,2048]{2,1,0:T(8,128)(2,1)S(1)}, u32[]{:S(2)}, u32[]{:S(2)}) %all-to-all-start.2) | async-done | bytes 262176 | tf_op jit(solution)/shard_map/all_to_all | solution.py:216
  42.1 1.1 gather_fusion
  43.2 1.0 copy.66
  44.3 63.0 %shard_map.181 = bf16[3,4,64,16,128]{4,3,2,1,0:T(8,128)(2,1)} custom-call(bf16[3,64,16,128]{3,2,1,0:T(8,128)(2,1)} %bitcast.102), custom_call_target="tpu_custom_call" | custom-call | tf_op jit(solution)/shard_map/pallas_call | solution.py:199
  107.3 5.8 %reshape.220 = bf16[3,4,64,2048]{3,2,1,0:T(8,128)(2,1)} reshape(bf16[3,4,64,16,128]{4,3,2,1,0:T(8,128)(2,1)} %shard_map.181) | data formatting | bytes 6291456 | tf_op jit(solution)/shard_map/reshape | solution.py:294
  113.1 5.1 %fusion.7 = f32[3,4,64,352]{3,2,1,0:T(8,128)} fusion(bf16[3,4,64,2048]{3,2,1,0:T(8,128)(2,1)} %reshape.220, bf16[1,2048,352]{1,2,0:T(8,128)(2,1)} %param.31), kind=kOutput, calls=%fused_computation.12 | convolution fusion | flops 1107296256 | bytes 5668864 | tf_op jit(solution)/shard_map/cqgd,df->cqgf/dot_general | solution.py:295
  118.3 8.2 %fusion.2 = bf16[4,3,64,2048]{3,2,0,1:T(8,128)(2,1)} fusion(bf16[1,352,2048]{2,1,0:T(8,128)(2,1)} %param.33, bf16[3,4,64,2048]{3,2,1,0:T(8,128)(2,1)} %reshape.220, bf16[1,2048,352]{1,2,0:T(8,128)(2,1)} %param.32, f32[3,4,64,352]{3,2,1,0:T(8,128)} %fusion.7), kind=kOutput, calls=%fused_computation.5 | convolution fusion | flops 2217787392 | bytes 10256384 | tf_op jit(solution)/shard_map/cqgf,fd->qcgd/dot_general | solution.py:302
  126.5 4.0 %copy.54 = bf16[4,3,64,2048]{3,2,1,0:T(8,128)(2,1)} copy(bf16[4,3,64,2048]{3,2,0,1:T(8,128)(2,1)} %fusion.2) | data formatting | bytes 6291456 | tf_op jit(solution)/shard_map/convert_element_type | solution.py:304
  130.5 4.8 %all-to-all-start.3 = ((bf16[4,3,64,2048]{3,2,1,0:T(8,128)(2,1)}), bf16[4,3,64,2048]{3,2,1,0:T(8,128)(2,1)}, u32[]{:S(2)}, u32[]{:S(2)}) async-start(bf16[4,3,64,2048]{3,2,1,0:T(8,128)(2,1)} %copy.54), calls=%async_computation.3 | async-start | bytes 6291456 | tf_op jit(solution)/shard_map/all_to_all | solution.py:216
  135.3 0.1 and.16
  135.6 0.2 select_reduce_fusion.1
  135.8 1.9 fusion.83
  137.7 34.2 %all-to-all-done.3 = bf16[4,3,64,2048]{3,2,1,0:T(8,128)(2,1)} async-done(((bf16[4,3,64,2048]{3,2,1,0:T(8,128)(2,1)}), bf16[4,3,64,2048]{3,2,1,0:T(8,128)(2,1)}, u32[]{:S(2)}, u32[]{:S(2)}) %all-to-all-start.3) | async-done | bytes 3145760 | tf_op jit(solution)/shard_map/all_to_all | solution.py:216
  171.9 2.6 %reduce_sum.86 = bf16[3,64,2048]{2,1,0:T(8,128)(2,1)S(1)} reduce(bf16[4,3,64,2048]{3,2,1,0:T(8,128)(2,1)} %all-to-all-done.3, bf16[]{:T(256)} %constant.15.clone.1), dimensions={0}, to_apply=%region_9.10 | reduce | flops 1179648 | bytes 3932162 | tf_op jit(solution)/shard_map/reduce_sum | solution.py:305
  174.4 1.7 copy.73
  176.1 33.2 %shard_map.182 = bf16[64,3,2048]{2,1,0:T(4,128)(2,1)} custom-call(bf16[64,3,2048]{2,1,0:T(4,128)(2,1)} %bitcast.97), custom_call_target="tpu_custom_call" | custom-call | tf_op jit(solution)/shard_map/pallas_call | solution.py:103
  209.3 2.4 %reshape.221 = bf16[192,2048]{1,0:T(8,128)(2,1)S(1)} reshape(bf16[64,3,2048]{2,1,0:T(4,128)(2,1)} %shard_map.182) | data formatting | bytes 1572864 | tf_op jit(solution)/shard_map/reshape | solution.py:306
  211.8 1.3 fusion.82
  213.1 3.1 %fusion.3 = bf16[64,2048]{1,0:T(8,128)(2,1)S(1)} fusion(f32[64,2048]{1,0:T(8,128)} %fusion.82, bf16[352,2048]{1,0:T(8,128)(2,1)} %param.36, bf16[64,2048]{1,0:T(8,128)(2,1)S(1)} %bitcast.100, bf16[2048,352]{0,1:T(8,128)(2,1)} %param.35, f32[64,352]{1,0:T(8,128)S(1)} %fusion.83), kind=kOutput, calls=%fused_computation.7 | convolution fusion | flops 184946688 | bytes 4022272 | tf_op jit(solution)/shard_map/dot_general | solution.py:269
  216.2 9.5 %all_to_all.38 = bf16[4,16,2048]{2,1,0:T(8,128)(2,1)S(1)} all-to-all(bf16[4,16,2048]{2,1,0:T(8,128)(2,1)S(1)} %bitcast.108), channel_id=1, replica_groups=mesh['ep'=64,'rep'=4] {'rep'}, dimensions={0} | all-to-all | bytes 524288 | tf_op jit(solution)/shard_map/all_to_all | solution.py:216
  225.8 0.1 multiply_reduce_fusion.1
  225.9 0.7 multiply_convert_fusion
  (43 shorter events, 1.4 us)
Async XLA Ops:
  0.0 21.4 %copy-start = (bf16[512,2048]{1,0:T(8,128)(2,1)S(1)}, bf16[512,2048]{1,0:T(8,128)(2,1)}, u32[]{:S(2)}) copy-start(bf16[512,2048]{1,0:T(8,128)(2,1)} %param.27) | copy-start | bytes 6291460
  6.5 1.3 copy-start.1
  7.8 7.8 %copy-start.5 = (s32[64,6]{0,1:T(8,128)S(1)}, s32[64,6]{0,1:T(8,128)}, u32[]{:S(2)}) copy-start(s32[64,6]{0,1:T(8,128)} %param.28) | copy-start | bytes 4612
  7.8 7.8 %copy-start.6 = (s32[64]{0:T(128)S(1)}, s32[64]{0:T(128)}, u32[]{:S(2)}) copy-start(s32[64]{0:T(128)} %param.30) | copy-start | bytes 772
  9.9 11.2 %copy-start.2 = (bf16[4,512,128]{2,1,0:T(8,128)(2,1)S(1)}, bf16[4,512,128]{2,1,0:T(8,128)(2,1)}, u32[]{:S(2)}) copy-start(bf16[4,512,128]{2,1,0:T(8,128)(2,1)} %param.26) | copy-start | bytes 1572868
  10.8 10.4 %all-to-all-start = ((bf16[16,16,512]{2,0,1:T(8,128)(2,1)}), bf16[16,16,512]{2,0,1:T(8,128)(2,1)S(1)}, u32[]{:S(2)}, u32[]{:S(2)}) async-start(bf16[16,16,512]{2,0,1:T(8,128)(2,1)} %copy.49), calls=%async_computation | async-start | bytes 524288 | tf_op jit(solution)/shard_map/all_to_all | solution.py:247
  22.6 8.9 %all-to-all-start.1 = ((bf16[4,16,2048]{2,1,0:T(8,128)(2,1)}), bf16[4,16,2048]{2,1,0:T(8,128)(2,1)S(1)}, u32[]{:S(2)}, u32[]{:S(2)}) async-start(bf16[4,16,2048]{2,1,0:T(8,128)(2,1)} %bitcast.8), calls=%async_computation.1 | async-start | bytes 524288 | tf_op jit(solution)/shard_map/all_to_all | solution.py:216
  33.1 8.9 %all-to-all-start.2 = ((bf16[4,16,2048]{2,1,0:T(8,128)(2,1)}), bf16[4,16,2048]{2,1,0:T(8,128)(2,1)S(1)}, u32[]{:S(2)}, u32[]{:S(2)}) async-start(bf16[4,16,2048]{2,1,0:T(8,128)(2,1)} %broadcast_in_dim.78), calls=%async_computation.2 | async-start | bytes 524288 | tf_op jit(solution)/shard_map/all_to_all | solution.py:216
  130.5 4.9 %copy-start.4 = (f32[64,6]{0,1:T(8,128)S(1)}, f32[64,6]{0,1:T(8,128)}, u32[]{:S(2)}) copy-start(f32[64,6]{0,1:T(8,128)} %param.29) | copy-start | bytes 4612
  130.5 41.4 %all-to-all-start.3 = ((bf16[4,3,64,2048]{3,2,1,0:T(8,128)(2,1)}), bf16[4,3,64,2048]{3,2,1,0:T(8,128)(2,1)}, u32[]{:S(2)}, u32[]{:S(2)}) async-start(bf16[4,3,64,2048]{3,2,1,0:T(8,128)(2,1)} %copy.54), calls=%async_computation.3 | async-start | bytes 6291456 | tf_op jit(solution)/shard_map/all_to_all | solution.py:216
  213.1 12.8 %copy-start.3 = (f32[2048]{0:T(1024)S(1)}, f32[2048]{0:T(1024)}, u32[]{:S(2)}) copy-start(f32[2048]{0:T(1024)} %param.37) | copy-start | bytes 24580

commit v5 on v4

--- a/solution.py
+++ b/solution.py
@@ -210,6 +210,111 @@
         ],
         compiler_params=pltpu.CompilerParams(collective_id=2, has_side_effects=True),
     )(blocks)
+
+
+def _combine_kernel(terms_ref, out_ref, parts, sums, x_send, x_recv, x_local, ep_send, ep_recv, ep_local):
+    replicas, chunks, groups = terms_ref.shape[:3]
+    me_e = lax.axis_index("ep")
+    me_r = lax.axis_index("rep")
+    mesh_id = pl.DeviceIdType.MESH
+
+    def x_copy(c, peer, slot):
+        return pltpu.make_async_remote_copy(
+            terms_ref.at[peer, c],
+            parts.at[c, slot],
+            x_send.at[c, peer],
+            x_recv.at[c, slot],
+            device_id=(me_e, peer),
+            device_id_type=mesh_id,
+        )
+
+    def ep_copy(c, peer, slot):
+        return pltpu.make_async_remote_copy(
+            sums.at[c, peer],
+            out_ref.at[c, slot],
+            ep_send.at[c, peer],
+            ep_recv.at[c, slot],
+            device_id=(peer, me_r),
+            device_id_type=mesh_id,
+        )
+
+    barrier = pltpu.get_barrier_semaphore()
+
+    def greet(step, carry):
+        pl.semaphore_signal(
+            barrier, 1, device_id=(lax.rem(me_e + step, groups), me_r), device_id_type=mesh_id
+        )
+        return carry
+
+    lax.fori_loop(1, groups, greet, 0)
+    for step in range(1, replicas):
+        pl.semaphore_signal(
+            barrier, 1, device_id=(me_e, lax.rem(me_r + step, replicas)), device_id_type=mesh_id
+        )
+    pl.semaphore_wait(barrier, groups - 1 + replicas - 1)
+
+    x_locals = []
+    for c in range(chunks):
+        local = pltpu.make_async_copy(terms_ref.at[me_r, c], parts.at[c, me_r], x_local.at[c])
+        local.start()
+        x_locals.append(local)
+        for step in range(1, replicas):
+            x_copy(c, lax.rem(me_r + step, replicas), me_r).start()
+
+    ep_locals = []
+    for c in range(chunks):
+        x_locals[c].wait()
+        for step in range(1, replicas):
+            peer = lax.rem(me_r + step, replicas)
+            x_copy(c, peer, peer).wait_recv()
+        total = parts[c, 0].astype(jnp.float32)
+        for source in range(1, replicas):
+            total = total + parts[c, source].astype(jnp.float32)
+        sums[c] = total.astype(sums.dtype)
+        local = pltpu.make_async_copy(sums.at[c, me_e], out_ref.at[c, me_e], ep_local.at[c])
+        local.start()
+        ep_locals.append(local)
+
+        def send(step, carry, c=c):
+            ep_copy(c, lax.rem(me_e + step, groups), me_e).start()
+            return carry
+
+        lax.fori_loop(1, groups, send, 0)
+
+    for c in range(chunks):
+        for step in range(1, replicas):
+            x_copy(c, lax.rem(me_r + step, replicas), me_r).wait_send()
+        ep_locals[c].wait()
+
+        def finish(step, carry, c=c):
+            peer = lax.rem(me_e + step, groups)
+            ep_copy(c, peer, me_e).wait_send()
+            ep_copy(c, peer, peer).wait_recv()
+            return carry
+
+        lax.fori_loop(1, groups, finish, 0)
+
+
+def combine_return(terms):
+    replicas, chunks, groups = terms.shape[:3]
+    tile = terms.shape[3:]
+    return pl.pallas_call(
+        _combine_kernel,
+        out_shape=jax.ShapeDtypeStruct((chunks, groups) + tile, terms.dtype),
+        in_specs=[pl.BlockSpec(memory_space=pl.ANY)],
+        out_specs=pl.BlockSpec(memory_space=pl.ANY),
+        scratch_shapes=[
+            pltpu.VMEM((chunks, replicas, groups) + tile, terms.dtype),
+            pltpu.VMEM((chunks, groups) + tile, terms.dtype),
+            pltpu.SemaphoreType.DMA((chunks, replicas)),
+            pltpu.SemaphoreType.DMA((chunks, replicas)),
+            pltpu.SemaphoreType.DMA((chunks,)),
+            pltpu.SemaphoreType.DMA((chunks, groups)),
+            pltpu.SemaphoreType.DMA((chunks, groups)),
+            pltpu.SemaphoreType.DMA((chunks,)),
+        ],
+        compiler_params=pltpu.CompilerParams(collective_id=3, has_side_effects=True),
+    )(terms)
 
 
 def rep_exchange(blocks):
@@ -302,13 +407,12 @@
     expert_terms = jnp.einsum(
         "cqgf,fd->qcgd", activated, expert_down[0], preferred_element_type=jnp.float32
     ).astype(jnp.bfloat16)
-    summed = jnp.sum(rep_exchange(expert_terms).astype(jnp.float32), axis=0).astype(jnp.bfloat16)
-    returned = exchange(jnp.transpose(summed, (1, 0, 2)), "ep", "rep", 1).reshape(
-        experts * share, model_width
-    )
+    returned = combine_return(
+        expert_terms.reshape(expert_terms.shape[:3] + (model_width // lanes, lanes))
+    ).reshape(share * experts, model_width)
     local_pos = position - rep_index * share
     mine = (local_pos >= 0) & (local_pos < share)
-    column = slot_index * share + jnp.clip(local_pos, 0, share - 1)
+    column = jnp.clip(local_pos, 0, share - 1) * experts + slot_index
     weight_used = jnp.where(mine, route_weight.reshape(-1), 0.0)
     combine = jnp.sum(
         jnp.where(

time: 229 us -> 206 us (0.90)
  waiting for transfers between devices: 44.7 us -> 10 us
  Pallas kernels: 96.2 us -> 120 us
  starting transfers between devices: 16.6 us -> 12.7 us
  local copies, waits for them, and re-layouts: 25.7 us -> 22.8 us
    all_to_all x3 -> x2, waiting for transfers between devices: 41.7 us -> 10 us  [rep_exchange(): lax.all_to_all(blocks, 'rep', split_axis=0, concat_axis=0, tiled=True)]
    pallas_call x1, Pallas kernels: 33.2 us -> 57.4 us  [combine_return(): pl.pallas_call(_combine_kernel, out_shape=jax.ShapeDtypeStruct((chunks, g...]
    convert_element_type x1 -> x0, local copies, waits for them, and re-layouts: 3.97 us -> none  [per_device(): expert_terms = jnp.einsum('cqgf,fd->qcgd', activated, expert_down[0], pre...]
    all_to_all x3 -> x2, starting transfers between devices: 11.8 us -> 7.82 us  [rep_exchange(): lax.all_to_all(blocks, 'rep', split_axis=0, concat_axis=0, tiled=True)]
    all_to_all x1, waiting for transfers between devices: 3.03 us -> 0.01 us  [per_device(): lax.all_to_all(latent_out, 'rep', split_axis=1, concat_axis=0, tiled=True)]
    unnamed x17 -> x22, local copies, waits for them, and re-layouts: 2.35 us -> 5.27 us
    reduce_sum x1 -> x0, other arithmetic: 2.56 us -> none  [per_device(): jnp.sum(rep_exchange(expert_terms).astype(jnp.float32), axis=0)]
  transfers between devices with their start and end apart: 4 -> 3, of which waited for: 4 -> 2; matrix products, arithmetic and copies ran while one was open for 4% -> 3% of each run, Pallas kernels for 0% -> 0%
where the time goes in v5:
time: 206 us; the launch traced here: 205 us
  Pallas kernels  120 us (58%)
  matrix products  25.4 us (12%)
  local copies, waits for them, and re-layouts  22.8 us (11%)
  starting transfers between devices  12.7 us (6%)
  waiting for transfers between devices  10 us (5%)
  blocking collectives  8.79 us (4%)
  other arithmetic  5.39 us (3%)
    pallas_call x1, Pallas kernels, dispatch(): pl.pallas_call(_dispatch_kernel, out_shape=jax.ShapeDtypeStruct(out_shape...  62.4 us
    pallas_call x1, Pallas kernels, combine_return(): pl.pallas_call(_combine_kernel, out_shape=jax.ShapeDtypeStruct((chunks, g...  57.4 us
    all_to_all x2, waiting for transfers between devices, rep_exchange(): lax.all_to_all(blocks, 'rep', split_axis=0, concat_axis=0, tiled=True)  10 us
    all_to_all x1, blocking collectives, rep_exchange(): lax.all_to_all(blocks, 'rep', split_axis=0, concat_axis=0, tiled=True)  8.79 us
    dot_general x1, matrix products, per_device(): jnp.einsum('cqgf,fd->qcgd', activated, expert_down[0], preferred_element_...  8.22 us
    all_to_all x2, starting transfers between devices, rep_exchange(): lax.all_to_all(blocks, 'rep', split_axis=0, concat_axis=0, tiled=True)  7.82 us
    reshape x1, local copies, waits for them, and re-layouts, per_device(): dispatch(outgoing, replicas)  5.82 us
    unnamed x22, local copies, waits for them, and re-layouts  5.27 us
  transfers between devices with their start and end apart: 3, of which 2 were waited for; matrix products, arithmetic and copies ran while one was open for 3% of the time, Pallas kernels for 0%

profile of v5, /device:TPU:1, one launch (start us, length us, event | category | flops | bytes accessed | tf_op | source)
XLA Modules:
  0.0 205.3 jit_solution(7183492457714713497)
XLA Ops:
  0.0 1.2 copy.63
  1.2 1.2 reshape.218
  2.4 0.9 reshape.217
  3.3 1.0 fusion.56
  4.4 0.1 reshape.214
  4.5 1.7 fusion.83
  6.2 0.3 fusion.21
  6.5 1.3 fusion.16
  7.8 2.1 %fusion.40 = bf16[16,16,512]{2,1,0:T(8,128)(2,1)S(1)} fusion(bf16[1024,512,1]{1,0,2:T(8,128)(2,1)S(1)} %bitcast.114, f32[16,16,1024]{2,1,0:T(8,128)} %fusion.16, f32[16,1024]{1,0:T(8,128)S(1)} %reshape.214), kind=kOutput, calls=%fused_computation.30 | convolution fusion | flops 270140672 | bytes 2424832 | tf_op jit(solution)/shard_map/thp,pr->thr/dot_general | solution.py:49
  10.0 0.8 copy.49
  10.8 4.8 %all-to-all-start = ((bf16[16,16,512]{2,0,1:T(8,128)(2,1)}), bf16[16,16,512]{2,0,1:T(8,128)(2,1)S(1)}, u32[]{:S(2)}, u32[]{:S(2)}) async-start(bf16[16,16,512]{2,0,1:T(8,128)(2,1)} %copy.49), calls=%async_computation | async-start | bytes 524288 | tf_op jit(solution)/shard_map/all_to_all | solution.py:352
  15.6 0.3 select_reduce_fusion.2
  15.9 0.1 copy.42
  16.0 0.1 eq.72
  16.2 0.1 eq.68
  16.3 0.9 reduce-window.6
  17.2 0.2 slice_reduce_fusion
  17.5 0.1 fusion.60
  17.7 0.1 mul.104
  17.9 0.1 copy.52
  18.0 0.2 mul.114
  18.2 2.9 %scatter_custom_fusion = s32[768]{0:T(1024)S(1)} fusion(s32[384]{0:T(512)S(1)} %fusion.78, s32[384]{0:T(512)S(1)} %add_select_fusion, s32[]{:T(128)} %constant.24.clone.1), kind=kCustom, calls=%fused_computation.89 | custom fusion | bytes 3076 | tf_op jit(solution)/shard_map/scatter | solution.py:393
  21.4 0.2 and.16
  21.6 0.1 copy.46
  21.8 0.2 fusion.44
  22.1 1.2 convolution_convert_fusion.1
  23.2 4.2 %all-to-all-start.1 = ((bf16[4,16,2048]{2,1,0:T(8,128)(2,1)}), bf16[4,16,2048]{2,1,0:T(8,128)(2,1)S(1)}, u32[]{:S(2)}, u32[]{:S(2)}) async-start(bf16[4,16,2048]{2,1,0:T(8,128)(2,1)} %bitcast.8), calls=%async_computation.1 | async-start | bytes 524288 | tf_op jit(solution)/shard_map/all_to_all | solution.py:321
  27.5 5.5 %all-to-all-done.1 = bf16[4,16,2048]{2,1,0:T(8,128)(2,1)S(1)} async-done(((bf16[4,16,2048]{2,1,0:T(8,128)(2,1)}), bf16[4,16,2048]{2,1,0:T(8,128)(2,1)S(1)}, u32[]{:S(2)}, u32[]{:S(2)}) %all-to-all-start.1) | async-done | bytes 262176 | tf_op jit(solution)/shard_map/all_to_all | solution.py:321
  33.1 0.9 add_convert_fusion
  33.9 0.7 broadcast_in_dim.78
  34.6 3.6 %all-to-all-start.2 = ((bf16[4,16,2048]{2,1,0:T(8,128)(2,1)}), bf16[4,16,2048]{2,1,0:T(8,128)(2,1)S(1)}, u32[]{:S(2)}, u32[]{:S(2)}) async-start(bf16[4,16,2048]{2,1,0:T(8,128)(2,1)} %broadcast_in_dim.78), calls=%async_computation.2 | async-start | bytes 524288 | tf_op jit(solution)/shard_map/all_to_all | solution.py:321
  38.2 0.8 select_reduce_fusion.1
  39.0 4.5 %all-to-all-done.2 = bf16[4,16,2048]{2,1,0:T(8,128)(2,1)S(1)} async-done(((bf16[4,16,2048]{2,1,0:T(8,128)(2,1)}), bf16[4,16,2048]{2,1,0:T(8,128)(2,1)S(1)}, u32[]{:S(2)}, u32[]{:S(2)}) %all-to-all-start.2) | async-done | bytes 262176 | tf_op jit(solution)/shard_map/all_to_all | solution.py:321
  43.6 1.1 gather_fusion
  44.7 1.0 copy.64
  45.8 62.4 %shard_map.181 = bf16[3,4,64,16,128]{4,3,2,1,0:T(8,128)(2,1)} custom-call(bf16[3,64,16,128]{3,2,1,0:T(8,128)(2,1)} %bitcast.110), custom_call_target="tpu_custom_call" | custom-call | tf_op jit(solution)/shard_map/pallas_call | solution.py:199
  108.2 5.8 %reshape.225 = bf16[3,4,64,2048]{3,2,1,0:T(8,128)(2,1)} reshape(bf16[3,4,64,16,128]{4,3,2,1,0:T(8,128)(2,1)} %shard_map.181) | data formatting | bytes 6291456 | tf_op jit(solution)/shard_map/reshape | solution.py:399
  114.0 5.1 %fusion.6 = f32[3,4,64,352]{3,2,1,0:T(8,128)} fusion(bf16[3,4,64,2048]{3,2,1,0:T(8,128)(2,1)} %reshape.225, bf16[1,2048,352]{1,2,0:T(8,128)(2,1)} %param.31), kind=kOutput, calls=%fused_computation.11 | convolution fusion | flops 1107296256 | bytes 5668864 | tf_op jit(solution)/shard_map/cqgd,df->cqgf/dot_general | solution.py:400
  119.1 8.2 %convolution_convert_fusion = bf16[3,4,64,2048]{3,2,1,0:T(8,128)(2,1)} fusion(bf16[1,352,2048]{2,1,0:T(8,128)(2,1)} %param.33, bf16[3,4,64,2048]{3,2,1,0:T(8,128)(2,1)} %reshape.225, bf16[1,2048,352]{1,2,0:T(8,128)(2,1)} %param.32, f32[3,4,64,352]{3,2,1,0:T(8,128)} %fusion.6), kind=kOutput, calls=%fused_computation.4 | convolution fusion | flops 2217787392 | bytes 10256384 | tf_op jit(solution)/shard_map/cqgf,fd->qcgd/dot_general | solution.py:407
  127.3 2.9 %copy.65 = bf16[96,8,16,128]{3,2,1,0:T(8,128)(2,1)S(1)} copy(bf16[96,8,16,128]{3,1,2,0:T(8,128)(2,1)} %bitcast.108) | data formatting | bytes 6291456
  130.3 2.2 %copy.60.terms_ref = bf16[4,3,64,16,128]{4,3,2,1,0:T(8,128)(2,1)} copy(bf16[4,3,64,16,128]{4,3,2,0,1:T(8,128)(2,1)S(1)} %bitcast.104) | data formatting | bytes 6291456 | tf_op jit(solution)/shard_map/reshape | solution.py:411
  132.5 57.4 %shard_map.182 = bf16[3,64,16,128]{3,2,1,0:T(8,128)(2,1)} custom-call(bf16[4,3,64,16,128]{4,3,2,1,0:T(8,128)(2,1)} %copy.60.terms_ref), custom_call_target="tpu_custom_call" | custom-call | tf_op jit(solution)/shard_map/pallas_call | solution.py:301
  190.0 2.0 fusion.84
  192.0 0.6 fusion.47
  192.6 3.0 %fusion.2 = bf16[64,2048]{1,0:T(8,128)(2,1)S(1)} fusion(f32[64,2048]{1,0:T(8,128)S(1)} %fusion.47, bf16[352,2048]{1,0:T(8,128)(2,1)} %param.36, bf16[64,2048]{1,0:T(8,128)(2,1)S(1)} %bitcast.107, bf16[2048,352]{0,1:T(8,128)(2,1)} %param.35, f32[64,352]{1,0:T(8,128)S(1)} %fusion.84), kind=kOutput, calls=%fused_computation.6 | convolution fusion | flops 184946688 | bytes 4022272 | tf_op jit(solution)/shard_map/dot_general | solution.py:374
  195.6 8.8 %all_to_all.33 = bf16[4,16,2048]{2,1,0:T(8,128)(2,1)S(1)} all-to-all(bf16[4,16,2048]{2,1,0:T(8,128)(2,1)S(1)} %bitcast.117), channel_id=1, replica_groups=mesh['ep'=64,'rep'=4] {'rep'}, dimensions={0} | all-to-all | bytes 524288 | tf_op jit(solution)/shard_map/all_to_all | solution.py:321
  204.4 0.1 multiply_reduce_fusion.1
  204.5 0.7 multiply_convert_fusion
  (43 shorter events, 0.9 us)
Async XLA Ops:
  0.0 22.1 %copy-start = (bf16[512,2048]{1,0:T(8,128)(2,1)S(1)}, bf16[512,2048]{1,0:T(8,128)(2,1)}, u32[]{:S(2)}) copy-start(bf16[512,2048]{1,0:T(8,128)(2,1)} %param.27) | copy-start | bytes 6291460
  6.5 1.3 copy-start.2
  7.8 7.8 %copy-start.7 = (s32[64,6]{0,1:T(8,128)S(1)}, s32[64,6]{0,1:T(8,128)}, u32[]{:S(2)}) copy-start(s32[64,6]{0,1:T(8,128)} %param.28) | copy-start | bytes 4612
  7.8 7.8 %copy-start.8 = (s32[64]{0:T(128)S(1)}, s32[64]{0:T(128)}, u32[]{:S(2)}) copy-start(s32[64]{0:T(128)} %param.30) | copy-start | bytes 772
  9.9 11.7 %copy-start.6 = (f32[64,6]{0,1:T(8,128)S(1)}, f32[64,6]{0,1:T(8,128)}, u32[]{:S(2)}) copy-start(f32[64,6]{0,1:T(8,128)} %param.29) | copy-start | bytes 4612
  9.9 11.9 %copy-start.3 = (bf16[4,512,128]{2,1,0:T(8,128)(2,1)S(1)}, bf16[4,512,128]{2,1,0:T(8,128)(2,1)}, u32[]{:S(2)}) copy-start(bf16[4,512,128]{2,1,0:T(8,128)(2,1)} %param.26) | copy-start | bytes 1572868
  10.8 11.0 %all-to-all-start = ((bf16[16,16,512]{2,0,1:T(8,128)(2,1)}), bf16[16,16,512]{2,0,1:T(8,128)(2,1)S(1)}, u32[]{:S(2)}, u32[]{:S(2)}) async-start(bf16[16,16,512]{2,0,1:T(8,128)(2,1)} %copy.49), calls=%async_computation | async-start | bytes 524288 | tf_op jit(solution)/shard_map/all_to_all | solution.py:352
  23.2 9.8 %all-to-all-start.1 = ((bf16[4,16,2048]{2,1,0:T(8,128)(2,1)}), bf16[4,16,2048]{2,1,0:T(8,128)(2,1)S(1)}, u32[]{:S(2)}, u32[]{:S(2)}) async-start(bf16[4,16,2048]{2,1,0:T(8,128)(2,1)} %bitcast.8), calls=%async_computation.1 | async-start | bytes 524288 | tf_op jit(solution)/shard_map/all_to_all | solution.py:321
  34.6 8.9 %all-to-all-start.2 = ((bf16[4,16,2048]{2,1,0:T(8,128)(2,1)}), bf16[4,16,2048]{2,1,0:T(8,128)(2,1)S(1)}, u32[]{:S(2)}, u32[]{:S(2)}) async-start(bf16[4,16,2048]{2,1,0:T(8,128)(2,1)} %broadcast_in_dim.78), calls=%async_computation.2 | async-start | bytes 524288 | tf_op jit(solution)/shard_map/all_to_all | solution.py:321
  189.9 2.0 copy-start.1
  189.9 2.0 copy-start.4
  192.5 12.0 %copy-start.5 = (f32[2048]{0:T(1024)S(1)}, f32[2048]{0:T(1024)}, u32[]{:S(2)}) copy-start(f32[2048]{0:T(1024)} %param.37) | copy-start | bytes 24580

commit v6 on v5

--- a/solution.py
+++ b/solution.py
@@ -50,75 +50,33 @@
     return latent_out.astype(jnp.bfloat16)
 
 
-def _exchange_kernel(axis, other, src_ref, out_ref, send_sems, recv_sems, local_sem):
-    count = src_ref.shape[0]
-    me = lax.axis_index(axis)
-    fixed = lax.axis_index(other)
-
-    def device(peer):
-        return (peer, fixed) if axis == "ep" else (fixed, peer)
-
-    def remote(peer, slot):
-        return pltpu.make_async_remote_copy(
-            src_ref.at[peer],
-            out_ref.at[slot],
-            send_sems.at[peer],
-            recv_sems.at[slot],
-            device_id=device(peer),
-            device_id_type=pl.DeviceIdType.MESH,
-        )
-
+def _greet_all(me_e, me_r, groups, replicas):
+    mesh_id = pl.DeviceIdType.MESH
     barrier = pltpu.get_barrier_semaphore()
 
     def greet(step, carry):
-        peer = lax.rem(me + step, count)
         pl.semaphore_signal(
-            barrier, 1, device_id=device(peer), device_id_type=pl.DeviceIdType.MESH
+            barrier, 1, device_id=(lax.rem(me_e + step, groups), me_r), device_id_type=mesh_id
         )
         return carry
 
-    lax.fori_loop(1, count, greet, 0)
-    pl.semaphore_wait(barrier, count - 1)
-    local = pltpu.make_async_copy(src_ref.at[me], out_ref.at[me], local_sem)
-    local.start()
-
-    def send(step, carry):
-        remote(lax.rem(me + step, count), me).start()
-        return carry
-
-    lax.fori_loop(1, count, send, 0)
-
-    def finish(step, carry):
-        peer = lax.rem(me + step, count)
-        remote(peer, me).wait_send()
-        remote(peer, peer).wait_recv()
-        return carry
-
-    lax.fori_loop(1, count, finish, 0)
-    local.wait()
-
-
-def exchange(blocks, axis, other, collective_id):
-    count = blocks.shape[0]
-    return pl.pallas_call(
-        functools.partial(_exchange_kernel, axis, other),
-        out_shape=jax.ShapeDtypeStruct(blocks.shape, blocks.dtype),
-        in_specs=[pl.BlockSpec(memory_space=pl.ANY)],
-        out_specs=pl.BlockSpec(memory_space=pl.ANY),
-        scratch_shapes=[
-            pltpu.SemaphoreType.DMA((count,)),
-            pltpu.SemaphoreType.DMA((count,)),
-            pltpu.SemaphoreType.DMA(()),
-        ],
-        compiler_params=pltpu.CompilerParams(collective_id=collective_id, has_side_effects=True),
-    )(blocks)
-
-
-def _dispatch_kernel(src_ref, out_ref, ep_send, ep_recv, local_sem, x_send, x_recv):
-    chunks, groups = src_ref.shape[0], src_ref.shape[1]
+    lax.fori_loop(1, groups, greet, 0)
+    for step in range(1, replicas):
+        pl.semaphore_signal(
+            barrier, 1, device_id=(me_e, lax.rem(me_r + step, replicas)), device_id_type=mesh_id
+        )
+    pl.semaphore_wait(barrier, groups - 1 + replicas - 1)
+
+
+def _dispatch_kernel(src_ref, out_ref, ep_send, ep_recv, local_sem, x_send, x_recv, f_send, f_recv):
+    chunks, groups = src_ref.shape[:2]
     replicas = out_ref.shape[1]
+    half = groups // 2
     me_e = lax.axis_index("ep")
     me_r = lax.axis_index("rep")
+    right = lax.rem(me_r + 1, replicas)
+    left = lax.rem(me_r + replicas - 1, replicas)
+    across = lax.rem(me_r + 2, replicas)
     mesh_id = pl.DeviceIdType.MESH
 
     def ep_copy(c, peer, slot):
@@ -131,30 +89,28 @@
             device_id_type=mesh_id,
         )
 
-    def x_copy(c, peer, slot):
-        return pltpu.make_async_remote_copy(
-            out_ref.at[c, me_r],
+    def x_copy(c, side, slot):
+        return pltpu.make_async_remote_copy(
             out_ref.at[c, slot],
-            x_send.at[c, peer],
-            x_recv.at[c, slot],
-            device_id=(me_e, peer),
-            device_id_type=mesh_id,
-        )
-
-    barrier = pltpu.get_barrier_semaphore()
-
-    def greet(step, carry):
-        pl.semaphore_signal(
-            barrier, 1, device_id=(lax.rem(me_e + step, groups), me_r), device_id_type=mesh_id
-        )
-        return carry
-
-    lax.fori_loop(1, groups, greet, 0)
-    for step in range(1, replicas):
-        pl.semaphore_signal(
-            barrier, 1, device_id=(me_e, lax.rem(me_r + step, replicas)), device_id_type=mesh_id
-        )
-    pl.semaphore_wait(barrier, groups - 1 + replicas - 1)
+            out_ref.at[c, slot],
+            x_send.at[c, side],
+            x_recv.at[c, side],
+            device_id=(me_e, right if side == 0 else left),
+            device_id_type=mesh_id,
+        )
+
+    def f_copy(c, side, slot, part):
+        rows = pl.ds(part * half, half)
+        return pltpu.make_async_remote_copy(
+            out_ref.at[c, slot, rows],
+            out_ref.at[c, slot, rows],
+            f_send.at[c, side],
+            f_recv.at[c, side],
+            device_id=(me_e, right if side == 0 else left),
+            device_id_type=mesh_id,
+        )
+
+    _greet_all(me_e, me_r, groups, replicas)
 
     locals_ = []
     for c in range(chunks):
@@ -167,6 +123,12 @@
             return carry
 
         lax.fori_loop(1, groups, send, 0)
+
+    def forward(c):
+        x_copy(c, 0, left).wait_recv()
+        f_copy(c, 0, left, 1).start()
+        x_copy(c, 1, right).wait_recv()
+        f_copy(c, 1, right, 0).start()
 
     for c in range(chunks):
         locals_[c].wait()
@@ -177,14 +139,19 @@
             return carry
 
         lax.fori_loop(1, groups, arrive, 0)
-        for step in range(1, replicas):
-            x_copy(c, lax.rem(me_r + step, replicas), me_r).start()
-
-    for c in range(chunks):
-        for step in range(1, replicas):
-            peer = lax.rem(me_r + step, replicas)
-            x_copy(c, peer, me_r).wait_send()
-            x_copy(c, peer, peer).wait_recv()
+        x_copy(c, 0, me_r).start()
+        x_copy(c, 1, me_r).start()
+        if c >= 1:
+            forward(c - 1)
+    forward(chunks - 1)
+
+    for c in range(chunks):
+        f_copy(c, 0, across, 1).wait_recv()
+        f_copy(c, 1, across, 0).wait_recv()
+        for side in range(2):
+            x_copy(c, side, me_r).wait_send()
+        f_copy(c, 0, left, 1).wait_send()
+        f_copy(c, 1, right, 0).wait_send()
 
         def sent(step, carry, c=c):
             ep_copy(c, lax.rem(me_e + step, groups), me_e).wait_send()
@@ -205,26 +172,70 @@
             pltpu.SemaphoreType.DMA((chunks, groups)),
             pltpu.SemaphoreType.DMA((chunks, groups)),
             pltpu.SemaphoreType.DMA((chunks,)),
-            pltpu.SemaphoreType.DMA((chunks, replicas)),
-            pltpu.SemaphoreType.DMA((chunks, replicas)),
+            pltpu.SemaphoreType.DMA((chunks, 2)),
+            pltpu.SemaphoreType.DMA((chunks, 2)),
+            pltpu.SemaphoreType.DMA((chunks, 2)),
+            pltpu.SemaphoreType.DMA((chunks, 2)),
         ],
         compiler_params=pltpu.CompilerParams(collective_id=2, has_side_effects=True),
     )(blocks)
 
 
-def _combine_kernel(terms_ref, out_ref, parts, sums, x_send, x_recv, x_local, ep_send, ep_recv, ep_local):
+def _combine_kernel(
+    terms_ref, out_ref, parts, transit, sums,
+    x_send, x_recv, t_send, t_recv, f_send, f_recv, x_local, ep_send, ep_recv, ep_local,
+):
     replicas, chunks, groups = terms_ref.shape[:3]
+    half = groups // 2
     me_e = lax.axis_index("ep")
     me_r = lax.axis_index("rep")
+    right = lax.rem(me_r + 1, replicas)
+    left = lax.rem(me_r + replicas - 1, replicas)
+    across = lax.rem(me_r + 2, replicas)
     mesh_id = pl.DeviceIdType.MESH
 
-    def x_copy(c, peer, slot):
-        return pltpu.make_async_remote_copy(
-            terms_ref.at[peer, c],
-            parts.at[c, slot],
-            x_send.at[c, peer],
-            x_recv.at[c, slot],
-            device_id=(me_e, peer),
+    def side_peer(side):
+        return right if side == 0 else left
+
+    def x_copy(c, side):
+        return pltpu.make_async_remote_copy(
+            terms_ref.at[side_peer(side), c],
+            parts.at[c, me_r],
+            x_send.at[c, side],
+            x_recv.at[c, side],
+            device_id=(me_e, side_peer(side)),
+            device_id_type=mesh_id,
+        )
+
+    def x_wait(c, side):
+        return pltpu.make_async_remote_copy(
+            terms_ref.at[me_r, c],
+            parts.at[c, left if side == 0 else right],
+            x_send.at[c, side],
+            x_recv.at[c, side],
+            device_id=(me_e, side_peer(side)),
+            device_id_type=mesh_id,
+        )
+
+    def t_copy(c, side):
+        rows = pl.ds((1 - side) * half, half)
+        return pltpu.make_async_remote_copy(
+            terms_ref.at[across, c, rows],
+            transit.at[c, side],
+            t_send.at[c, side],
+            t_recv.at[c, side],
+            device_id=(me_e, side_peer(side)),
+            device_id_type=mesh_id,
+        )
+
+    def f_copy(c, side, source):
+        rows = pl.ds((1 - side) * half, half)
+        return pltpu.make_async_remote_copy(
+            transit.at[c, side],
+            parts.at[c, source, rows],
+            f_send.at[c, side],
+            f_recv.at[c, side],
+            device_id=(me_e, side_peer(side)),
             device_id_type=mesh_id,
         )
 
@@ -238,35 +249,27 @@
             device_id_type=mesh_id,
         )
 
-    barrier = pltpu.get_barrier_semaphore()
-
-    def greet(step, carry):
-        pl.semaphore_signal(
-            barrier, 1, device_id=(lax.rem(me_e + step, groups), me_r), device_id_type=mesh_id
-        )
-        return carry
-
-    lax.fori_loop(1, groups, greet, 0)
-    for step in range(1, replicas):
-        pl.semaphore_signal(
-            barrier, 1, device_id=(me_e, lax.rem(me_r + step, replicas)), device_id_type=mesh_id
-        )
-    pl.semaphore_wait(barrier, groups - 1 + replicas - 1)
+    _greet_all(me_e, me_r, groups, replicas)
 
     x_locals = []
     for c in range(chunks):
         local = pltpu.make_async_copy(terms_ref.at[me_r, c], parts.at[c, me_r], x_local.at[c])
         local.start()
         x_locals.append(local)
-        for step in range(1, replicas):
-            x_copy(c, lax.rem(me_r + step, replicas), me_r).start()
+        for side in range(2):
+            t_copy(c, side).start()
+            x_copy(c, side).start()
 
     ep_locals = []
     for c in range(chunks):
+        t_copy(c, 0).wait_recv()
+        f_copy(c, 0, left).start()
+        t_copy(c, 1).wait_recv()
+        f_copy(c, 1, right).start()
         x_locals[c].wait()
-        for step in range(1, replicas):
-            peer = lax.rem(me_r + step, replicas)
-            x_copy(c, peer, peer).wait_recv()
+        for side in range(2):
+            x_wait(c, side).wait_recv()
+            f_copy(c, side, across).wait_recv()
         total = parts[c, 0].astype(jnp.float32)
         for source in range(1, replicas):
             total = total + parts[c, source].astype(jnp.float32)
@@ -282,8 +285,11 @@
         lax.fori_loop(1, groups, send, 0)
 
     for c in range(chunks):
-        for step in range(1, replicas):
-            x_copy(c, lax.rem(me_r + step, replicas), me_r).wait_send()
+        for side in range(2):
+            x_copy(c, side).wait_send()
+            t_copy(c, side).wait_send()
+        f_copy(c, 0, left).wait_send()
+        f_copy(c, 1, right).wait_send()
         ep_locals[c].wait()
 
         def finish(step, carry, c=c):
@@ -305,9 +311,11 @@
         out_specs=pl.BlockSpec(memory_space=pl.ANY),
         scratch_shapes=[
             pltpu.VMEM((chunks, replicas, groups) + tile, terms.dtype),
+            pltpu.VMEM((chunks, 2, groups // 2) + tile, terms.dtype),
             pltpu.VMEM((chunks, groups) + tile, terms.dtype),
-            pltpu.SemaphoreType.DMA((chunks, replicas)),
-            pltpu.SemaphoreType.DMA((chunks, replicas)),
+        ]
+        + [pltpu.SemaphoreType.DMA((chunks, 2))] * 6
+        + [
             pltpu.SemaphoreType.DMA((chunks,)),
             pltpu.SemaphoreType.DMA((chunks, groups)),
             pltpu.SemaphoreType.DMA((chunks, groups)),
@@ -374,7 +382,7 @@
     shared_terms = jnp.dot(shared_act, shared_down, preferred_element_type=jnp.float32)
     experts = placement.shape[0]
     route_count = routes.shape[1]
-    assert experts == expert_groups
+    assert experts == expert_groups and replicas == 4
     capacity = max(
         replicas, min(group_rows, 2 * group_rows * route_count // experts // replicas * replicas)
     )

time: 206 us -> 203 us (0.985)
  Pallas kernels: 120 us -> 117 us
    pallas_call x1, Pallas kernels: 62.4 us -> 54.4 us  [dispatch(): pl.pallas_call(_dispatch_kernel, out_shape=jax.ShapeDtypeStruct(out_shape...]
    pallas_call x1, Pallas kernels: 57.4 us -> 62.6 us  [combine_return(): pl.pallas_call(_combine_kernel, out_shape=jax.ShapeDtypeStruct((chunks, g...]
where the time goes in v6:
time: 203 us; the launch traced here: 202 us
  Pallas kernels  117 us (58%)
  matrix products  25.4 us (13%)
  local copies, waits for them, and re-layouts  22.8 us (11%)
  starting transfers between devices  12.7 us (6%)
  waiting for transfers between devices  10 us (5%)
  blocking collectives  8.22 us (4%)
  other arithmetic  5.39 us (3%)
    pallas_call x1, Pallas kernels, combine_return(): pl.pallas_call(_combine_kernel, out_shape=jax.ShapeDtypeStruct((chunks, g...  62.6 us
    pallas_call x1, Pallas kernels, dispatch(): pl.pallas_call(_dispatch_kernel, out_shape=jax.ShapeDtypeStruct(out_shape...  54.4 us
    all_to_all x2, waiting for transfers between devices, rep_exchange(): lax.all_to_all(blocks, 'rep', split_axis=0, concat_axis=0, tiled=True)  10 us
    dot_general x1, matrix products, per_device(): jnp.einsum('cqgf,fd->qcgd', activated, expert_down[0], preferred_element_...  8.22 us
    all_to_all x1, blocking collectives, rep_exchange(): lax.all_to_all(blocks, 'rep', split_axis=0, concat_axis=0, tiled=True)  8.22 us
    all_to_all x2, starting transfers between devices, rep_exchange(): lax.all_to_all(blocks, 'rep', split_axis=0, concat_axis=0, tiled=True)  7.82 us
    reshape x1, local copies, waits for them, and re-layouts, per_device(): dispatch(outgoing, replicas)  5.82 us
    unnamed x22, local copies, waits for them, and re-layouts  5.27 us
  transfers between devices with their start and end apart: 3, of which 2 were waited for; matrix products, arithmetic and copies ran while one was open for 3% of the time, Pallas kernels for 0%

profile of v6, /device:TPU:1, one launch (start us, length us, event | category | flops | bytes accessed | tf_op | source)
XLA Modules:
  0.0 201.9 jit_solution(11241756926454572710)
XLA Ops:
  0.0 1.2 copy.63
  1.2 1.2 reshape.218
  2.4 0.9 reshape.217
  3.3 1.0 fusion.56
  4.4 0.1 reshape.214
  4.5 1.7 fusion.83
  6.2 0.3 fusion.21
  6.5 1.3 fusion.16
  7.8 2.1 %fusion.40 = bf16[16,16,512]{2,1,0:T(8,128)(2,1)S(1)} fusion(bf16[1024,512,1]{1,0,2:T(8,128)(2,1)S(1)} %bitcast.114, f32[16,16,1024]{2,1,0:T(8,128)} %fusion.16, f32[16,1024]{1,0:T(8,128)S(1)} %reshape.214), kind=kOutput, calls=%fused_computation.30 | convolution fusion | flops 270140672 | bytes 2424832 | tf_op jit(solution)/shard_map/thp,pr->thr/dot_general | solution.py:49
  10.0 0.8 copy.49
  10.8 4.8 %all-to-all-start = ((bf16[16,16,512]{2,0,1:T(8,128)(2,1)}), bf16[16,16,512]{2,0,1:T(8,128)(2,1)S(1)}, u32[]{:S(2)}, u32[]{:S(2)}) async-start(bf16[16,16,512]{2,0,1:T(8,128)(2,1)} %copy.49), calls=%async_computation | async-start | bytes 524288 | tf_op jit(solution)/shard_map/all_to_all | solution.py:360
  15.6 0.3 select_reduce_fusion.2
  15.9 0.1 copy.42
  16.0 0.1 eq.72
  16.2 0.1 eq.68
  16.3 0.9 reduce-window.6
  17.2 0.2 slice_reduce_fusion
  17.5 0.1 fusion.60
  17.7 0.1 mul.104
  17.9 0.1 copy.52
  18.0 0.2 mul.114
  18.2 2.9 %scatter_custom_fusion = s32[768]{0:T(1024)S(1)} fusion(s32[384]{0:T(512)S(1)} %fusion.78, s32[384]{0:T(512)S(1)} %add_select_fusion, s32[]{:T(128)} %constant.24.clone.1), kind=kCustom, calls=%fused_computation.89 | custom fusion | bytes 3076 | tf_op jit(solution)/shard_map/scatter | solution.py:401
  21.4 0.2 and.16
  21.6 0.1 copy.46
  21.8 0.2 fusion.44
  22.1 1.2 convolution_convert_fusion.1
  23.2 4.2 %all-to-all-start.1 = ((bf16[4,16,2048]{2,1,0:T(8,128)(2,1)}), bf16[4,16,2048]{2,1,0:T(8,128)(2,1)S(1)}, u32[]{:S(2)}, u32[]{:S(2)}) async-start(bf16[4,16,2048]{2,1,0:T(8,128)(2,1)} %bitcast.8), calls=%async_computation.1 | async-start | bytes 524288 | tf_op jit(solution)/shard_map/all_to_all | solution.py:329
  27.5 5.5 %all-to-all-done.1 = bf16[4,16,2048]{2,1,0:T(8,128)(2,1)S(1)} async-done(((bf16[4,16,2048]{2,1,0:T(8,128)(2,1)}), bf16[4,16,2048]{2,1,0:T(8,128)(2,1)S(1)}, u32[]{:S(2)}, u32[]{:S(2)}) %all-to-all-start.1) | async-done | bytes 262176 | tf_op jit(solution)/shard_map/all_to_all | solution.py:329
  33.1 0.9 add_convert_fusion
  33.9 0.7 broadcast_in_dim.78
  34.6 3.6 %all-to-all-start.2 = ((bf16[4,16,2048]{2,1,0:T(8,128)(2,1)}), bf16[4,16,2048]{2,1,0:T(8,128)(2,1)S(1)}, u32[]{:S(2)}, u32[]{:S(2)}) async-start(bf16[4,16,2048]{2,1,0:T(8,128)(2,1)} %broadcast_in_dim.78), calls=%async_computation.2 | async-start | bytes 524288 | tf_op jit(solution)/shard_map/all_to_all | solution.py:329
  38.2 0.8 select_reduce_fusion.1
  39.0 4.5 %all-to-all-done.2 = bf16[4,16,2048]{2,1,0:T(8,128)(2,1)S(1)} async-done(((bf16[4,16,2048]{2,1,0:T(8,128)(2,1)}), bf16[4,16,2048]{2,1,0:T(8,128)(2,1)S(1)}, u32[]{:S(2)}, u32[]{:S(2)}) %all-to-all-start.2) | async-done | bytes 262176 | tf_op jit(solution)/shard_map/all_to_all | solution.py:329
  43.6 1.1 gather_fusion
  44.7 1.0 copy.64
  45.8 54.4 %shard_map.181 = bf16[3,4,64,16,128]{4,3,2,1,0:T(8,128)(2,1)} custom-call(bf16[3,64,16,128]{3,2,1,0:T(8,128)(2,1)} %bitcast.110), custom_call_target="tpu_custom_call" | custom-call | tf_op jit(solution)/shard_map/pallas_call | solution.py:166
  100.1 5.8 %reshape.225 = bf16[3,4,64,2048]{3,2,1,0:T(8,128)(2,1)} reshape(bf16[3,4,64,16,128]{4,3,2,1,0:T(8,128)(2,1)} %shard_map.181) | data formatting | bytes 6291456 | tf_op jit(solution)/shard_map/reshape | solution.py:407
  106.0 5.1 %fusion.6 = f32[3,4,64,352]{3,2,1,0:T(8,128)} fusion(bf16[3,4,64,2048]{3,2,1,0:T(8,128)(2,1)} %reshape.225, bf16[1,2048,352]{1,2,0:T(8,128)(2,1)} %param.31), kind=kOutput, calls=%fused_computation.11 | convolution fusion | flops 1107296256 | bytes 5668864 | tf_op jit(solution)/shard_map/cqgd,df->cqgf/dot_general | solution.py:408
  111.1 8.2 %convolution_convert_fusion = bf16[3,4,64,2048]{3,2,1,0:T(8,128)(2,1)} fusion(bf16[1,352,2048]{2,1,0:T(8,128)(2,1)} %param.33, bf16[3,4,64,2048]{3,2,1,0:T(8,128)(2,1)} %reshape.225, bf16[1,2048,352]{1,2,0:T(8,128)(2,1)} %param.32, f32[3,4,64,352]{3,2,1,0:T(8,128)} %fusion.6), kind=kOutput, calls=%fused_computation.4 | convolution fusion | flops 2217787392 | bytes 10256384 | tf_op jit(solution)/shard_map/cqgf,fd->qcgd/dot_general | solution.py:415
  119.3 2.9 %copy.65 = bf16[96,8,16,128]{3,2,1,0:T(8,128)(2,1)S(1)} copy(bf16[96,8,16,128]{3,1,2,0:T(8,128)(2,1)} %bitcast.108) | data formatting | bytes 6291456
  122.2 2.2 %copy.60.terms_ref = bf16[4,3,64,16,128]{4,3,2,1,0:T(8,128)(2,1)} copy(bf16[4,3,64,16,128]{4,3,2,0,1:T(8,128)(2,1)S(1)} %bitcast.104) | data formatting | bytes 6291456 | tf_op jit(solution)/shard_map/reshape | solution.py:419
  124.5 62.6 %shard_map.182 = bf16[3,64,16,128]{3,2,1,0:T(8,128)(2,1)} custom-call(bf16[4,3,64,16,128]{4,3,2,1,0:T(8,128)(2,1)} %copy.60.terms_ref), custom_call_target="tpu_custom_call" | custom-call | tf_op jit(solution)/shard_map/pallas_call | solution.py:307
  187.1 2.0 fusion.84
  189.2 0.6 fusion.47
  189.7 3.0 %fusion.2 = bf16[64,2048]{1,0:T(8,128)(2,1)S(1)} fusion(f32[64,2048]{1,0:T(8,128)S(1)} %fusion.47, bf16[352,2048]{1,0:T(8,128)(2,1)} %param.36, bf16[64,2048]{1,0:T(8,128)(2,1)S(1)} %bitcast.107, bf16[2048,352]{0,1:T(8,128)(2,1)} %param.35, f32[64,352]{1,0:T(8,128)S(1)} %fusion.84), kind=kOutput, calls=%fused_computation.6 | convolution fusion | flops 184946688 | bytes 4022272 | tf_op jit(solution)/shard_map/dot_general | solution.py:382
  192.7 8.2 %all_to_all.33 = bf16[4,16,2048]{2,1,0:T(8,128)(2,1)S(1)} all-to-all(bf16[4,16,2048]{2,1,0:T(8,128)(2,1)S(1)} %bitcast.117), channel_id=1, replica_groups=mesh['ep'=64,'rep'=4] {'rep'}, dimensions={0} | all-to-all | bytes 524288 | tf_op jit(solution)/shard_map/all_to_all | solution.py:329
  201.0 0.1 multiply_reduce_fusion.1
  201.1 0.7 multiply_convert_fusion
  (43 shorter events, 0.9 us)
Async XLA Ops:
  0.0 22.1 %copy-start = (bf16[512,2048]{1,0:T(8,128)(2,1)S(1)}, bf16[512,2048]{1,0:T(8,128)(2,1)}, u32[]{:S(2)}) copy-start(bf16[512,2048]{1,0:T(8,128)(2,1)} %param.27) | copy-start | bytes 6291460
  6.5 1.3 copy-start.2
  7.8 7.8 %copy-start.7 = (s32[64,6]{0,1:T(8,128)S(1)}, s32[64,6]{0,1:T(8,128)}, u32[]{:S(2)}) copy-start(s32[64,6]{0,1:T(8,128)} %param.28) | copy-start | bytes 4612
  7.8 7.8 %copy-start.8 = (s32[64]{0:T(128)S(1)}, s32[64]{0:T(128)}, u32[]{:S(2)}) copy-start(s32[64]{0:T(128)} %param.30) | copy-start | bytes 772
  9.9 11.7 %copy-start.6 = (f32[64,6]{0,1:T(8,128)S(1)}, f32[64,6]{0,1:T(8,128)}, u32[]{:S(2)}) copy-start(f32[64,6]{0,1:T(8,128)} %param.29) | copy-start | bytes 4612
  9.9 11.9 %copy-start.3 = (bf16[4,512,128]{2,1,0:T(8,128)(2,1)S(1)}, bf16[4,512,128]{2,1,0:T(8,128)(2,1)}, u32[]{:S(2)}) copy-start(bf16[4,512,128]{2,1,0:T(8,128)(2,1)} %param.26) | copy-start | bytes 1572868
  10.8 11.0 %all-to-all-start = ((bf16[16,16,512]{2,0,1:T(8,128)(2,1)}), bf16[16,16,512]{2,0,1:T(8,128)(2,1)S(1)}, u32[]{:S(2)}, u32[]{:S(2)}) async-start(bf16[16,16,512]{2,0,1:T(8,128)(2,1)} %copy.49), calls=%async_computation | async-start | bytes 524288 | tf_op jit(solution)/shard_map/all_to_all | solution.py:360
  23.2 9.8 %all-to-all-start.1 = ((bf16[4,16,2048]{2,1,0:T(8,128)(2,1)}), bf16[4,16,2048]{2,1,0:T(8,128)(2,1)S(1)}, u32[]{:S(2)}, u32[]{:S(2)}) async-start(bf16[4,16,2048]{2,1,0:T(8,128)(2,1)} %bitcast.8), calls=%async_computation.1 | async-start | bytes 524288 | tf_op jit(solution)/shard_map/all_to_all | solution.py:329
  34.6 8.9 %all-to-all-start.2 = ((bf16[4,16,2048]{2,1,0:T(8,128)(2,1)}), bf16[4,16,2048]{2,1,0:T(8,128)(2,1)S(1)}, u32[]{:S(2)}, u32[]{:S(2)}) async-start(bf16[4,16,2048]{2,1,0:T(8,128)(2,1)} %broadcast_in_dim.78), calls=%async_computation.2 | async-start | bytes 524288 | tf_op jit(solution)/shard_map/all_to_all | solution.py:329
  187.1 2.0 %copy-start.1 = (bf16[3,64,16,128]{3,2,1,0:T(8,128)(2,1)S(1)}, bf16[3,64,16,128]{3,2,1,0:T(8,128)(2,1)}, u32[]{:S(2)}) copy-start(bf16[3,64,16,128]{3,2,1,0:T(8,128)(2,1)} %shard_map.182) | copy-start | bytes 2359300
  187.1 2.0 %copy-start.4 = (f32[64,192]{1,0:T(8,128)S(1)}, f32[64,192]{1,0:T(8,128)}, u32[]{:S(2)}) copy-start(f32[64,192]{1,0:T(8,128)} %select_reduce_fusion.1) | copy-start | bytes 147460
  189.7 11.4 %copy-start.5 = (f32[2048]{0:T(1024)S(1)}, f32[2048]{0:T(1024)}, u32[]{:S(2)}) copy-start(f32[2048]{0:T(1024)} %param.37) | copy-start | bytes 24580

commit v7 on v6

--- a/solution.py
+++ b/solution.py
@@ -181,61 +181,19 @@
     )(blocks)
 
 
-def _combine_kernel(
-    terms_ref, out_ref, parts, transit, sums,
-    x_send, x_recv, t_send, t_recv, f_send, f_recv, x_local, ep_send, ep_recv, ep_local,
-):
+def _combine_kernel(terms_ref, out_ref, parts, sums, x_send, x_recv, x_local, ep_send, ep_recv, ep_local):
     replicas, chunks, groups = terms_ref.shape[:3]
-    half = groups // 2
     me_e = lax.axis_index("ep")
     me_r = lax.axis_index("rep")
-    right = lax.rem(me_r + 1, replicas)
-    left = lax.rem(me_r + replicas - 1, replicas)
-    across = lax.rem(me_r + 2, replicas)
     mesh_id = pl.DeviceIdType.MESH
 
-    def side_peer(side):
-        return right if side == 0 else left
-
-    def x_copy(c, side):
+    def x_copy(c, peer, slot):
         return pltpu.make_async_remote_copy(
-            terms_ref.at[side_peer(side), c],
-            parts.at[c, me_r],
-            x_send.at[c, side],
-            x_recv.at[c, side],
-            device_id=(me_e, side_peer(side)),
-            device_id_type=mesh_id,
-        )
-
-    def x_wait(c, side):
-        return pltpu.make_async_remote_copy(
-            terms_ref.at[me_r, c],
-            parts.at[c, left if side == 0 else right],
-            x_send.at[c, side],
-            x_recv.at[c, side],
-            device_id=(me_e, side_peer(side)),
-            device_id_type=mesh_id,
-        )
-
-    def t_copy(c, side):
-        rows = pl.ds((1 - side) * half, half)
-        return pltpu.make_async_remote_copy(
-            terms_ref.at[across, c, rows],
-            transit.at[c, side],
-            t_send.at[c, side],
-            t_recv.at[c, side],
-            device_id=(me_e, side_peer(side)),
-            device_id_type=mesh_id,
-        )
-
-    def f_copy(c, side, source):
-        rows = pl.ds((1 - side) * half, half)
-        return pltpu.make_async_remote_copy(
-            transit.at[c, side],
-            parts.at[c, source, rows],
-            f_send.at[c, side],
-            f_recv.at[c, side],
-            device_id=(me_e, side_peer(side)),
+            terms_ref.at[peer, c],
+            parts.at[c, slot],
+            x_send.at[c, peer],
+            x_recv.at[c, slot],
+            device_id=(me_e, peer),
             device_id_type=mesh_id,
         )
 
@@ -249,27 +207,35 @@
             device_id_type=mesh_id,
         )
 
-    _greet_all(me_e, me_r, groups, replicas)
+    barrier = pltpu.get_barrier_semaphore()
+
+    def greet(step, carry):
+        pl.semaphore_signal(
+            barrier, 1, device_id=(lax.rem(me_e + step, groups), me_r), device_id_type=mesh_id
+        )
+        return carry
+
+    lax.fori_loop(1, groups, greet, 0)
+    for step in range(1, replicas):
+        pl.semaphore_signal(
+            barrier, 1, device_id=(me_e, lax.rem(me_r + step, replicas)), device_id_type=mesh_id
+        )
+    pl.semaphore_wait(barrier, groups - 1 + replicas - 1)
 
     x_locals = []
     for c in range(chunks):
         local = pltpu.make_async_copy(terms_ref.at[me_r, c], parts.at[c, me_r], x_local.at[c])
         local.start()
         x_locals.append(local)
-        for side in range(2):
-            t_copy(c, side).start()
-            x_copy(c, side).start()
+        for step in range(1, replicas):
+            x_copy(c, lax.rem(me_r + step, replicas), me_r).start()
 
     ep_locals = []
     for c in range(chunks):
-        t_copy(c, 0).wait_recv()
-        f_copy(c, 0, left).start()
-        t_copy(c, 1).wait_recv()
-        f_copy(c, 1, right).start()
         x_locals[c].wait()
-        for side in range(2):
-            x_wait(c, side).wait_recv()
-            f_copy(c, side, across).wait_recv()
+        for step in range(1, replicas):
+            peer = lax.rem(me_r + step, replicas)
+            x_copy(c, peer, peer).wait_recv()
         total = parts[c, 0].astype(jnp.float32)
         for source in range(1, replicas):
             total = total + parts[c, source].astype(jnp.float32)
@@ -285,11 +251,8 @@
         lax.fori_loop(1, groups, send, 0)
 
     for c in range(chunks):
-        for side in range(2):
-            x_copy(c, side).wait_send()
-            t_copy(c, side).wait_send()
-        f_copy(c, 0, left).wait_send()
-        f_copy(c, 1, right).wait_send()
+        for step in range(1, replicas):
+            x_copy(c, lax.rem(me_r + step, replicas), me_r).wait_send()
         ep_locals[c].wait()
 
         def finish(step, carry, c=c):
@@ -311,11 +274,9 @@
         out_specs=pl.BlockSpec(memory_space=pl.ANY),
         scratch_shapes=[
             pltpu.VMEM((chunks, replicas, groups) + tile, terms.dtype),
-            pltpu.VMEM((chunks, 2, groups // 2) + tile, terms.dtype),
             pltpu.VMEM((chunks, groups) + tile, terms.dtype),
-        ]
-        + [pltpu.SemaphoreType.DMA((chunks, 2))] * 6
-        + [
+            pltpu.SemaphoreType.DMA((chunks, replicas)),
+            pltpu.SemaphoreType.DMA((chunks, replicas)),
             pltpu.SemaphoreType.DMA((chunks,)),
             pltpu.SemaphoreType.DMA((chunks, groups)),
             pltpu.SemaphoreType.DMA((chunks, groups)),

time: 203 us -> 197 us (0.970)
  Pallas kernels: 117 us -> 111 us
    pallas_call x1, Pallas kernels: 62.6 us -> 56.3 us  [combine_return(): pl.pallas_call(_combine_kernel, out_shape=jax.ShapeDtypeStruct((chunks, g...]
  transfers between devices with their start and end apart: 3 -> 3, of which waited for: 2 -> 2; matrix products, arithmetic and copies ran while one was open for 3% -> 4% of each run, Pallas kernels for 0% -> 0%
where the time goes in v7:
time: 197 us; the launch traced here: 196 us
  Pallas kernels  111 us (56%)
  matrix products  25.4 us (13%)
  local copies, waits for them, and re-layouts  22.8 us (12%)
  starting transfers between devices  12.7 us (6%)
  waiting for transfers between devices  10 us (5%)
  blocking collectives  8.59 us (4%)
  other arithmetic  5.39 us (3%)
    pallas_call x1, Pallas kernels, combine_return(): pl.pallas_call(_combine_kernel, out_shape=jax.ShapeDtypeStruct((chunks, g...  56.3 us
    pallas_call x1, Pallas kernels, dispatch(): pl.pallas_call(_dispatch_kernel, out_shape=jax.ShapeDtypeStruct(out_shape...  54.4 us
    all_to_all x2, waiting for transfers between devices, rep_exchange(): lax.all_to_all(blocks, 'rep', split_axis=0, concat_axis=0, tiled=True)  10 us
    all_to_all x1, blocking collectives, rep_exchange(): lax.all_to_all(blocks, 'rep', split_axis=0, concat_axis=0, tiled=True)  8.59 us
    dot_general x1, matrix products, per_device(): jnp.einsum('cqgf,fd->qcgd', activated, expert_down[0], preferred_element_...  8.22 us
    all_to_all x2, starting transfers between devices, rep_exchange(): lax.all_to_all(blocks, 'rep', split_axis=0, concat_axis=0, tiled=True)  7.82 us
    reshape x1, local copies, waits for them, and re-layouts, per_device(): dispatch(outgoing, replicas)  5.82 us
    unnamed x22, local copies, waits for them, and re-layouts  5.27 us
  transfers between devices with their start and end apart: 3, of which 2 were waited for; matrix products, arithmetic and copies ran while one was open for 4% of the time, Pallas kernels for 0%

profile of v7, /device:TPU:1, one launch (start us, length us, event | category | flops | bytes accessed | tf_op | source)
XLA Modules:
  0.0 195.9 jit_solution(16123809799852969411)
XLA Ops:
  0.0 1.2 copy.63
  1.2 1.2 reshape.218
  2.4 0.9 reshape.217
  3.3 1.0 fusion.56
  4.4 0.1 reshape.214
  4.5 1.7 fusion.83
  6.2 0.3 fusion.21
  6.5 1.3 fusion.16
  7.8 2.1 %fusion.40 = bf16[16,16,512]{2,1,0:T(8,128)(2,1)S(1)} fusion(bf16[1024,512,1]{1,0,2:T(8,128)(2,1)S(1)} %bitcast.114, f32[16,16,1024]{2,1,0:T(8,128)} %fusion.16, f32[16,1024]{1,0:T(8,128)S(1)} %reshape.214), kind=kOutput, calls=%fused_computation.30 | convolution fusion | flops 270140672 | bytes 2424832 | tf_op jit(solution)/shard_map/thp,pr->thr/dot_general | solution.py:49
  10.0 0.8 copy.49
  10.8 4.8 %all-to-all-start = ((bf16[16,16,512]{2,0,1:T(8,128)(2,1)}), bf16[16,16,512]{2,0,1:T(8,128)(2,1)S(1)}, u32[]{:S(2)}, u32[]{:S(2)}) async-start(bf16[16,16,512]{2,0,1:T(8,128)(2,1)} %copy.49), calls=%async_computation | async-start | bytes 524288 | tf_op jit(solution)/shard_map/all_to_all | solution.py:321
  15.6 0.3 select_reduce_fusion.2
  15.9 0.1 copy.42
  16.0 0.1 eq.72
  16.2 0.1 eq.68
  16.3 0.9 reduce-window.6
  17.2 0.2 slice_reduce_fusion
  17.5 0.1 fusion.60
  17.7 0.1 mul.104
  17.9 0.1 copy.52
  18.0 0.2 mul.114
  18.2 2.9 %scatter_custom_fusion = s32[768]{0:T(1024)S(1)} fusion(s32[384]{0:T(512)S(1)} %fusion.78, s32[384]{0:T(512)S(1)} %add_select_fusion, s32[]{:T(128)} %constant.24.clone.1), kind=kCustom, calls=%fused_computation.89 | custom fusion | bytes 3076 | tf_op jit(solution)/shard_map/scatter | solution.py:362
  21.4 0.2 and.16
  21.6 0.1 copy.46
  21.8 0.2 fusion.44
  22.1 1.2 convolution_convert_fusion.1
  23.2 4.2 %all-to-all-start.1 = ((bf16[4,16,2048]{2,1,0:T(8,128)(2,1)}), bf16[4,16,2048]{2,1,0:T(8,128)(2,1)S(1)}, u32[]{:S(2)}, u32[]{:S(2)}) async-start(bf16[4,16,2048]{2,1,0:T(8,128)(2,1)} %bitcast.8), calls=%async_computation.1 | async-start | bytes 524288 | tf_op jit(solution)/shard_map/all_to_all | solution.py:290
  27.5 5.5 %all-to-all-done.1 = bf16[4,16,2048]{2,1,0:T(8,128)(2,1)S(1)} async-done(((bf16[4,16,2048]{2,1,0:T(8,128)(2,1)}), bf16[4,16,2048]{2,1,0:T(8,128)(2,1)S(1)}, u32[]{:S(2)}, u32[]{:S(2)}) %all-to-all-start.1) | async-done | bytes 262176 | tf_op jit(solution)/shard_map/all_to_all | solution.py:290
  33.1 0.9 add_convert_fusion
  33.9 0.7 broadcast_in_dim.78
  34.6 3.6 %all-to-all-start.2 = ((bf16[4,16,2048]{2,1,0:T(8,128)(2,1)}), bf16[4,16,2048]{2,1,0:T(8,128)(2,1)S(1)}, u32[]{:S(2)}, u32[]{:S(2)}) async-start(bf16[4,16,2048]{2,1,0:T(8,128)(2,1)} %broadcast_in_dim.78), calls=%async_computation.2 | async-start | bytes 524288 | tf_op jit(solution)/shard_map/all_to_all | solution.py:290
  38.2 0.8 select_reduce_fusion.1
  39.0 4.5 %all-to-all-done.2 = bf16[4,16,2048]{2,1,0:T(8,128)(2,1)S(1)} async-done(((bf16[4,16,2048]{2,1,0:T(8,128)(2,1)}), bf16[4,16,2048]{2,1,0:T(8,128)(2,1)S(1)}, u32[]{:S(2)}, u32[]{:S(2)}) %all-to-all-start.2) | async-done | bytes 262176 | tf_op jit(solution)/shard_map/all_to_all | solution.py:290
  43.6 1.1 gather_fusion
  44.7 1.0 copy.64
  45.8 54.4 %shard_map.181 = bf16[3,4,64,16,128]{4,3,2,1,0:T(8,128)(2,1)} custom-call(bf16[3,64,16,128]{3,2,1,0:T(8,128)(2,1)} %bitcast.110), custom_call_target="tpu_custom_call" | custom-call | tf_op jit(solution)/shard_map/pallas_call | solution.py:166
  100.1 5.8 %reshape.225 = bf16[3,4,64,2048]{3,2,1,0:T(8,128)(2,1)} reshape(bf16[3,4,64,16,128]{4,3,2,1,0:T(8,128)(2,1)} %shard_map.181) | data formatting | bytes 6291456 | tf_op jit(solution)/shard_map/reshape | solution.py:368
  106.0 5.1 %fusion.6 = f32[3,4,64,352]{3,2,1,0:T(8,128)} fusion(bf16[3,4,64,2048]{3,2,1,0:T(8,128)(2,1)} %reshape.225, bf16[1,2048,352]{1,2,0:T(8,128)(2,1)} %param.31), kind=kOutput, calls=%fused_computation.11 | convolution fusion | flops 1107296256 | bytes 5668864 | tf_op jit(solution)/shard_map/cqgd,df->cqgf/dot_general | solution.py:369
  111.1 8.2 %convolution_convert_fusion = bf16[3,4,64,2048]{3,2,1,0:T(8,128)(2,1)} fusion(bf16[1,352,2048]{2,1,0:T(8,128)(2,1)} %param.33, bf16[3,4,64,2048]{3,2,1,0:T(8,128)(2,1)} %reshape.225, bf16[1,2048,352]{1,2,0:T(8,128)(2,1)} %param.32, f32[3,4,64,352]{3,2,1,0:T(8,128)} %fusion.6), kind=kOutput, calls=%fused_computation.4 | convolution fusion | flops 2217787392 | bytes 10256384 | tf_op jit(solution)/shard_map/cqgf,fd->qcgd/dot_general | solution.py:376
  119.3 2.9 %copy.65 = bf16[96,8,16,128]{3,2,1,0:T(8,128)(2,1)S(1)} copy(bf16[96,8,16,128]{3,1,2,0:T(8,128)(2,1)} %bitcast.108) | data formatting | bytes 6291456
  122.2 2.2 %copy.60.terms_ref = bf16[4,3,64,16,128]{4,3,2,1,0:T(8,128)(2,1)} copy(bf16[4,3,64,16,128]{4,3,2,0,1:T(8,128)(2,1)S(1)} %bitcast.104) | data formatting | bytes 6291456 | tf_op jit(solution)/shard_map/reshape | solution.py:380
  124.5 56.3 %shard_map.182 = bf16[3,64,16,128]{3,2,1,0:T(8,128)(2,1)} custom-call(bf16[4,3,64,16,128]{4,3,2,1,0:T(8,128)(2,1)} %copy.60.terms_ref), custom_call_target="tpu_custom_call" | custom-call | tf_op jit(solution)/shard_map/pallas_call | solution.py:270
  180.8 2.0 %fusion.84 = f32[64,352]{1,0:T(8,128)S(1)} fusion(bf16[64,2048]{1,0:T(8,128)(2,1)S(1)} %bitcast.106, bf16[2048,352]{0,1:T(8,128)(2,1)} %param.34), kind=kOutput, calls=%fused_computation.102 | convolution fusion | flops 92274688 | bytes 1794048 | tf_op jit(solution)/shard_map/dot_general | solution.py:340
  182.8 0.6 fusion.47
  183.4 3.0 %fusion.2 = bf16[64,2048]{1,0:T(8,128)(2,1)S(1)} fusion(f32[64,2048]{1,0:T(8,128)S(1)} %fusion.47, bf16[352,2048]{1,0:T(8,128)(2,1)} %param.36, bf16[64,2048]{1,0:T(8,128)(2,1)S(1)} %bitcast.107, bf16[2048,352]{0,1:T(8,128)(2,1)} %param.35, f32[64,352]{1,0:T(8,128)S(1)} %fusion.84), kind=kOutput, calls=%fused_computation.6 | convolution fusion | flops 184946688 | bytes 4022272 | tf_op jit(solution)/shard_map/dot_general | solution.py:343
  186.4 8.6 %all_to_all.33 = bf16[4,16,2048]{2,1,0:T(8,128)(2,1)S(1)} all-to-all(bf16[4,16,2048]{2,1,0:T(8,128)(2,1)S(1)} %bitcast.117), channel_id=1, replica_groups=mesh['ep'=64,'rep'=4] {'rep'}, dimensions={0} | all-to-all | bytes 524288 | tf_op jit(solution)/shard_map/all_to_all | solution.py:290
  195.0 0.1 multiply_reduce_fusion.1
  195.1 0.7 multiply_convert_fusion
  (43 shorter events, 0.9 us)
Async XLA Ops:
  0.0 22.1 %copy-start = (bf16[512,2048]{1,0:T(8,128)(2,1)S(1)}, bf16[512,2048]{1,0:T(8,128)(2,1)}, u32[]{:S(2)}) copy-start(bf16[512,2048]{1,0:T(8,128)(2,1)} %param.27) | copy-start | bytes 6291460
  6.5 1.3 copy-start.2
  7.8 7.8 %copy-start.7 = (s32[64,6]{0,1:T(8,128)S(1)}, s32[64,6]{0,1:T(8,128)}, u32[]{:S(2)}) copy-start(s32[64,6]{0,1:T(8,128)} %param.28) | copy-start | bytes 4612
  7.8 7.8 %copy-start.8 = (s32[64]{0:T(128)S(1)}, s32[64]{0:T(128)}, u32[]{:S(2)}) copy-start(s32[64]{0:T(128)} %param.30) | copy-start | bytes 772
  9.9 11.7 %copy-start.6 = (f32[64,6]{0,1:T(8,128)S(1)}, f32[64,6]{0,1:T(8,128)}, u32[]{:S(2)}) copy-start(f32[64,6]{0,1:T(8,128)} %param.29) | copy-start | bytes 4612
  9.9 11.9 %copy-start.3 = (bf16[4,512,128]{2,1,0:T(8,128)(2,1)S(1)}, bf16[4,512,128]{2,1,0:T(8,128)(2,1)}, u32[]{:S(2)}) copy-start(bf16[4,512,128]{2,1,0:T(8,128)(2,1)} %param.26) | copy-start | bytes 1572868
  10.8 11.0 %all-to-all-start = ((bf16[16,16,512]{2,0,1:T(8,128)(2,1)}), bf16[16,16,512]{2,0,1:T(8,128)(2,1)S(1)}, u32[]{:S(2)}, u32[]{:S(2)}) async-start(bf16[16,16,512]{2,0,1:T(8,128)(2,1)} %copy.49), calls=%async_computation | async-start | bytes 524288 | tf_op jit(solution)/shard_map/all_to_all | solution.py:321
  23.2 9.8 %all-to-all-start.1 = ((bf16[4,16,2048]{2,1,0:T(8,128)(2,1)}), bf16[4,16,2048]{2,1,0:T(8,128)(2,1)S(1)}, u32[]{:S(2)}, u32[]{:S(2)}) async-start(bf16[4,16,2048]{2,1,0:T(8,128)(2,1)} %bitcast.8), calls=%async_computation.1 | async-start | bytes 524288 | tf_op jit(solution)/shard_map/all_to_all | solution.py:290
  34.6 8.9 %all-to-all-start.2 = ((bf16[4,16,2048]{2,1,0:T(8,128)(2,1)}), bf16[4,16,2048]{2,1,0:T(8,128)(2,1)S(1)}, u32[]{:S(2)}, u32[]{:S(2)}) async-start(bf16[4,16,2048]{2,1,0:T(8,128)(2,1)} %broadcast_in_dim.78), calls=%async_computation.2 | async-start | bytes 524288 | tf_op jit(solution)/shard_map/all_to_all | solution.py:290
  180.7 2.0 %copy-start.1 = (bf16[3,64,16,128]{3,2,1,0:T(8,128)(2,1)S(1)}, bf16[3,64,16,128]{3,2,1,0:T(8,128)(2,1)}, u32[]{:S(2)}) copy-start(bf16[3,64,16,128]{3,2,1,0:T(8,128)(2,1)} %shard_map.182) | copy-start | bytes 2359300
  180.8 2.0 %copy-start.4 = (f32[64,192]{1,0:T(8,128)S(1)}, f32[64,192]{1,0:T(8,128)}, u32[]{:S(2)}) copy-start(f32[64,192]{1,0:T(8,128)} %select_reduce_fusion.1) | copy-start | bytes 147460
  183.4 11.8 %copy-start.5 = (f32[2048]{0:T(1024)S(1)}, f32[2048]{0:T(1024)}, u32[]{:S(2)}) copy-start(f32[2048]{0:T(1024)} %param.37) | copy-start | bytes 24580

commit v8 on v7

--- a/solution.py
+++ b/solution.py
@@ -284,6 +284,85 @@
         ],
         compiler_params=pltpu.CompilerParams(collective_id=3, has_side_effects=True),
     )(terms)
+
+
+def _hidden_kernel(terms_ref, resid_ref, out_ref, parts, own, t_send, t_recv, t_local, h_send, h_recv, h_local):
+    replicas = terms_ref.shape[0]
+    me_e = lax.axis_index("ep")
+    me_r = lax.axis_index("rep")
+    mesh_id = pl.DeviceIdType.MESH
+
+    def t_copy(peer, slot):
+        return pltpu.make_async_remote_copy(
+            terms_ref.at[peer],
+            parts.at[slot],
+            t_send.at[peer],
+            t_recv.at[slot],
+            device_id=(me_e, peer),
+            device_id_type=mesh_id,
+        )
+
+    def h_copy(peer, slot):
+        return pltpu.make_async_remote_copy(
+            own,
+            out_ref.at[slot],
+            h_send.at[peer],
+            h_recv.at[slot],
+            device_id=(me_e, peer),
+            device_id_type=mesh_id,
+        )
+
+    barrier = pltpu.get_barrier_semaphore()
+    for step in range(1, replicas):
+        pl.semaphore_signal(
+            barrier, 1, device_id=(me_e, lax.rem(me_r + step, replicas)), device_id_type=mesh_id
+        )
+    pl.semaphore_wait(barrier, replicas - 1)
+    local = pltpu.make_async_copy(terms_ref.at[me_r], parts.at[me_r], t_local)
+    local.start()
+    for step in range(1, replicas):
+        t_copy(lax.rem(me_r + step, replicas), me_r).start()
+    local.wait()
+    for step in range(1, replicas):
+        peer = lax.rem(me_r + step, replicas)
+        t_copy(peer, peer).wait_recv()
+    total = parts[0].astype(jnp.float32)
+    for source in range(1, replicas):
+        total = total + parts[source].astype(jnp.float32)
+    attended = total.astype(own.dtype).astype(jnp.float32)
+    own[...] = (resid_ref[...].astype(jnp.float32) + attended).astype(own.dtype)
+    keep = pltpu.make_async_copy(own, out_ref.at[me_r], h_local)
+    keep.start()
+    for step in range(1, replicas):
+        h_copy(lax.rem(me_r + step, replicas), me_r).start()
+    for step in range(1, replicas):
+        peer = lax.rem(me_r + step, replicas)
+        t_copy(peer, me_r).wait_send()
+        h_copy(peer, me_r).wait_send()
+        h_copy(peer, peer).wait_recv()
+    keep.wait()
+
+
+def hidden_rows(terms, residual_block):
+    replicas = terms.shape[0]
+    block = terms.shape[1:]
+    return pl.pallas_call(
+        _hidden_kernel,
+        out_shape=jax.ShapeDtypeStruct(terms.shape, terms.dtype),
+        in_specs=[pl.BlockSpec(memory_space=pl.ANY), pl.BlockSpec(memory_space=pltpu.VMEM)],
+        out_specs=pl.BlockSpec(memory_space=pl.ANY),
+        scratch_shapes=[
+            pltpu.VMEM(terms.shape, terms.dtype),
+            pltpu.VMEM(block, terms.dtype),
+            pltpu.SemaphoreType.DMA((replicas,)),
+            pltpu.SemaphoreType.DMA((replicas,)),
+            pltpu.SemaphoreType.DMA(()),
+            pltpu.SemaphoreType.DMA((replicas,)),
+            pltpu.SemaphoreType.DMA((replicas,)),
+            pltpu.SemaphoreType.DMA(()),
+        ],
+        compiler_params=pltpu.CompilerParams(collective_id=4, has_side_effects=True),
+    )(terms, residual_block)
 
 
 def rep_exchange(blocks):
@@ -327,15 +406,11 @@
         head_out.reshape(group_rows, -1), out_proj, preferred_element_type=jnp.float32
     )
     model_width = attn_terms.shape[1]
-    terms_in = rep_exchange(attn_terms.astype(jnp.bfloat16).reshape(replicas, own_count, model_width))
-    attended = jnp.sum(terms_in.astype(jnp.float32), axis=0).astype(jnp.bfloat16)
     own_residual = lax.dynamic_slice_in_dim(residual, rep_index * own_count, own_count, 0)
-    own_hidden = (own_residual.astype(jnp.float32) + attended.astype(jnp.float32)).astype(
-        jnp.bfloat16
-    )
-    hidden = rep_exchange(
-        jnp.broadcast_to(own_hidden[None], (replicas, own_count, model_width))
+    hidden = hidden_rows(
+        attn_terms.astype(jnp.bfloat16).reshape(replicas, own_count, model_width), own_residual
     ).reshape(group_rows, model_width)
+    own_hidden = lax.dynamic_slice_in_dim(hidden, rep_index * own_count, own_count, 0)
     shared_act = (
         jax.nn.silu(jnp.dot(hidden, shared_gate, preferred_element_type=jnp.float32))
         * jnp.dot(hidden, shared_up, preferred_element_type=jnp.float32)

time: 197 us -> 191 us (0.970)
  Pallas kernels: 111 us -> 122 us
  waiting for transfers between devices: 10 us -> 0.01 us
  starting transfers between devices: 12.7 us -> 4.84 us
    pallas_call x0 -> x1, Pallas kernels: none -> 12 us  [hidden_rows(): pl.pallas_call(_hidden_kernel, out_shape=jax.ShapeDtypeStruct(terms.shape...]
    all_to_all x2 -> x0, waiting for transfers between devices: 10 us -> none  [rep_exchange(): lax.all_to_all(blocks, 'rep', split_axis=0, concat_axis=0, tiled=True)]
    all_to_all x2 -> x0, starting transfers between devices: 7.82 us -> none  [rep_exchange(): lax.all_to_all(blocks, 'rep', split_axis=0, concat_axis=0, tiled=True)]
  transfers between devices with their start and end apart: 3 -> 1, of which waited for: 2 -> 0; matrix products, arithmetic and copies ran while one was open for 4% -> 4% of each run, Pallas kernels for 0% -> 0%
where the time goes in v8:
time: 191 us; the launch traced here: 190 us
  Pallas kernels  122 us (64%)
  matrix products  25.4 us (13%)
  local copies, waits for them, and re-layouts  24.7 us (13%)
  blocking collectives  8.57 us (4%)
  starting transfers between devices  4.84 us (3%)
  other arithmetic  3.88 us (2%)
    pallas_call x1, Pallas kernels, combine_return(): pl.pallas_call(_combine_kernel, out_shape=jax.ShapeDtypeStruct((chunks, g...  57.3 us
    pallas_call x1, Pallas kernels, dispatch(): pl.pallas_call(_dispatch_kernel, out_shape=jax.ShapeDtypeStruct(out_shape...  52.9 us
    pallas_call x1, Pallas kernels, hidden_rows(): pl.pallas_call(_hidden_kernel, out_shape=jax.ShapeDtypeStruct(terms.shape...  12 us
    all_to_all x1, blocking collectives, rep_exchange(): lax.all_to_all(blocks, 'rep', split_axis=0, concat_axis=0, tiled=True)  8.57 us
    dot_general x1, matrix products, per_device(): jnp.einsum('cqgf,fd->qcgd', activated, expert_down[0], preferred_element_...  8.22 us
    reshape x1, local copies, waits for them, and re-layouts, per_device(): dispatch(outgoing, replicas)  5.82 us
    unnamed x22, local copies, waits for them, and re-layouts  5.27 us
    dot_general x1, matrix products, per_device(): jnp.einsum('cqgd,df->cqgf', gathered, expert_gate[0], preferred_element_t...  5.15 us
  transfers between devices with their start and end apart: 1, of which 0 were waited for; matrix products, arithmetic and copies ran while one was open for 4% of the time, Pallas kernels for 0%

profile of v8, /device:TPU:1, one launch (start us, length us, event | category | flops | bytes accessed | tf_op | source)
XLA Modules:
  0.0 190.0 jit_solution(13975338346879279044)
XLA Ops:
  0.0 1.2 copy.63
  1.2 1.2 reshape.217
  2.4 0.9 reshape.216
  3.3 1.0 fusion.56
  4.4 0.1 reshape.213
  4.5 1.7 fusion.83
  6.2 0.3 fusion.21
  6.5 1.3 fusion.16
  7.8 2.1 %fusion.40 = bf16[16,16,512]{2,1,0:T(8,128)(2,1)S(1)} fusion(bf16[1024,512,1]{1,0,2:T(8,128)(2,1)S(1)} %bitcast.117, f32[16,16,1024]{2,1,0:T(8,128)} %fusion.16, f32[16,1024]{1,0:T(8,128)S(1)} %reshape.213), kind=kOutput, calls=%fused_computation.30 | convolution fusion | flops 270140672 | bytes 2424832 | tf_op jit(solution)/shard_map/thp,pr->thr/dot_general | solution.py:49
  10.0 0.8 copy.49
  10.8 4.8 %all-to-all-start = ((bf16[16,16,512]{2,0,1:T(8,128)(2,1)}), bf16[16,16,512]{2,0,1:T(8,128)(2,1)S(1)}, u32[]{:S(2)}, u32[]{:S(2)}) async-start(bf16[16,16,512]{2,0,1:T(8,128)(2,1)} %copy.49), calls=%async_computation | async-start | bytes 524288 | tf_op jit(solution)/shard_map/all_to_all | solution.py:400
  15.6 0.3 select_reduce_fusion.2
  15.9 0.1 copy.42
  16.0 0.1 eq.72
  16.2 0.1 eq.68
  16.3 0.9 reduce-window.6
  17.2 0.2 slice_reduce_fusion
  17.5 0.1 fusion.60
  17.7 0.1 mul.105
  17.9 0.1 copy.52
  18.0 0.2 mul.115
  18.2 3.1 %scatter_custom_fusion = s32[768]{0:T(1024)S(1)} fusion(s32[384]{0:T(512)S(1)} %fusion.78, s32[384]{0:T(512)S(1)} %add_select_fusion, s32[]{:T(128)} %constant.24.clone.1), kind=kCustom, calls=%fused_computation.88 | custom fusion | bytes 3076 | tf_op jit(solution)/shard_map/scatter | solution.py:437
  21.3 0.1 reshape.221
  21.4 0.1 dynamic-slice_bitcast_fusion
  21.5 0.1 reshape.222
  21.6 0.2 and.16
  21.8 0.1 copy.46
  22.0 0.2 select_reduce_fusion.1
  22.2 1.5 constant_dynamic-slice_fusion.resid_ref
  23.7 0.2 fusion.44
  23.9 1.2 convolution_convert_fusion.1
  25.1 12.0 %shard_map.181 = bf16[4,16,2048]{2,1,0:T(8,128)(2,1)} custom-call(bf16[4,16,2048]{2,1,0:T(8,128)(2,1)} %bitcast.115, bf16[16,2048]{1,0:T(8,128)(2,1)} %constant_dynamic-slice_fusion.resid_ref), custom_call_target="tpu_custom_call" | custom-call | tf_op jit(solution)/shard_map/pallas_call | solution.py:349
  37.1 1.0 concatenate.3
  38.1 1.1 gather_fusion
  39.3 1.0 copy.64
  40.3 52.9 %shard_map.182 = bf16[3,4,64,16,128]{4,3,2,1,0:T(8,128)(2,1)} custom-call(bf16[3,64,16,128]{3,2,1,0:T(8,128)(2,1)} %bitcast.112), custom_call_target="tpu_custom_call" | custom-call | tf_op jit(solution)/shard_map/pallas_call | solution.py:166
  93.2 5.8 %reshape.224 = bf16[3,4,64,2048]{3,2,1,0:T(8,128)(2,1)} reshape(bf16[3,4,64,16,128]{4,3,2,1,0:T(8,128)(2,1)} %shard_map.182) | data formatting | bytes 6291456 | tf_op jit(solution)/shard_map/reshape | solution.py:443
  99.1 5.1 %fusion.6 = f32[3,4,64,352]{3,2,1,0:T(8,128)} fusion(bf16[3,4,64,2048]{3,2,1,0:T(8,128)(2,1)} %reshape.224, bf16[1,2048,352]{1,2,0:T(8,128)(2,1)} %param.31), kind=kOutput, calls=%fused_computation.11 | convolution fusion | flops 1107296256 | bytes 5668864 | tf_op jit(solution)/shard_map/cqgd,df->cqgf/dot_general | solution.py:444
  104.2 8.2 %convolution_convert_fusion = bf16[3,4,64,2048]{3,2,1,0:T(8,128)(2,1)} fusion(bf16[1,352,2048]{2,1,0:T(8,128)(2,1)} %param.33, bf16[3,4,64,2048]{3,2,1,0:T(8,128)(2,1)} %reshape.224, bf16[1,2048,352]{1,2,0:T(8,128)(2,1)} %param.32, f32[3,4,64,352]{3,2,1,0:T(8,128)} %fusion.6), kind=kOutput, calls=%fused_computation.4 | convolution fusion | flops 2217787392 | bytes 10256384 | tf_op jit(solution)/shard_map/cqgf,fd->qcgd/dot_general | solution.py:451
  112.4 2.9 %copy.65 = bf16[96,8,16,128]{3,2,1,0:T(8,128)(2,1)S(1)} copy(bf16[96,8,16,128]{3,1,2,0:T(8,128)(2,1)} %bitcast.110) | data formatting | bytes 6291456
  115.4 2.2 %copy.60.terms_ref = bf16[4,3,64,16,128]{4,3,2,1,0:T(8,128)(2,1)} copy(bf16[4,3,64,16,128]{4,3,2,0,1:T(8,128)(2,1)S(1)} %bitcast.104) | data formatting | bytes 6291456 | tf_op jit(solution)/shard_map/reshape | solution.py:455
  117.6 57.3 %shard_map.183 = bf16[3,64,16,128]{3,2,1,0:T(8,128)(2,1)} custom-call(bf16[4,3,64,16,128]{4,3,2,1,0:T(8,128)(2,1)} %copy.60.terms_ref), custom_call_target="tpu_custom_call" | custom-call | tf_op jit(solution)/shard_map/pallas_call | solution.py:270
  174.9 2.0 %fusion.84 = f32[64,352]{1,0:T(8,128)S(1)} fusion(bf16[64,2048]{1,0:T(8,128)(2,1)S(1)} %bitcast.106, bf16[2048,352]{0,1:T(8,128)(2,1)} %param.34), kind=kOutput, calls=%fused_computation.102 | convolution fusion | flops 92274688 | bytes 1794048 | tf_op jit(solution)/shard_map/dot_general | solution.py:415
  176.9 0.6 fusion.47
  177.5 3.0 %fusion.2 = bf16[64,2048]{1,0:T(8,128)(2,1)S(1)} fusion(f32[64,2048]{1,0:T(8,128)S(1)} %fusion.47, bf16[352,2048]{1,0:T(8,128)(2,1)} %param.36, bf16[64,2048]{1,0:T(8,128)(2,1)S(1)} %bitcast.107, bf16[2048,352]{0,1:T(8,128)(2,1)} %param.35, f32[64,352]{1,0:T(8,128)S(1)} %fusion.84), kind=kOutput, calls=%fused_computation.6 | convolution fusion | flops 184946688 | bytes 4022272 | tf_op jit(solution)/shard_map/dot_general | solution.py:418
  180.5 8.6 %all_to_all.23 = bf16[4,16,2048]{2,1,0:T(8,128)(2,1)S(1)} all-to-all(bf16[4,16,2048]{2,1,0:T(8,128)(2,1)S(1)} %bitcast.120), channel_id=1, replica_groups=mesh['ep'=64,'rep'=4] {'rep'}, dimensions={0} | all-to-all | bytes 524288 | tf_op jit(solution)/shard_map/all_to_all | solution.py:369
  189.1 0.1 multiply_reduce_fusion.1
  189.3 0.7 multiply_convert_fusion
  (38 shorter events, 0.5 us)
Async XLA Ops:
  0.0 23.9 %copy-start = (bf16[512,2048]{1,0:T(8,128)(2,1)S(1)}, bf16[512,2048]{1,0:T(8,128)(2,1)}, u32[]{:S(2)}) copy-start(bf16[512,2048]{1,0:T(8,128)(2,1)} %param.27) | copy-start | bytes 6291460
  6.5 1.3 copy-start.3
  7.8 7.8 %copy-start.7 = (s32[64,6]{0,1:T(8,128)S(1)}, s32[64,6]{0,1:T(8,128)}, u32[]{:S(2)}) copy-start(s32[64,6]{0,1:T(8,128)} %param.28) | copy-start | bytes 4612
  7.8 7.8 %copy-start.8 = (s32[64]{0:T(128)S(1)}, s32[64]{0:T(128)}, u32[]{:S(2)}) copy-start(s32[64]{0:T(128)} %param.30) | copy-start | bytes 772
  9.9 11.9 %copy-start.6 = (f32[64,6]{0,1:T(8,128)S(1)}, f32[64,6]{0,1:T(8,128)}, u32[]{:S(2)}) copy-start(f32[64,6]{0,1:T(8,128)} %param.29) | copy-start | bytes 4612
  9.9 13.7 %copy-start.4 = (bf16[4,512,128]{2,1,0:T(8,128)(2,1)S(1)}, bf16[4,512,128]{2,1,0:T(8,128)(2,1)}, u32[]{:S(2)}) copy-start(bf16[4,512,128]{2,1,0:T(8,128)(2,1)} %param.26) | copy-start | bytes 1572868
  10.8 12.9 %all-to-all-start = ((bf16[16,16,512]{2,0,1:T(8,128)(2,1)}), bf16[16,16,512]{2,0,1:T(8,128)(2,1)S(1)}, u32[]{:S(2)}, u32[]{:S(2)}) async-start(bf16[16,16,512]{2,0,1:T(8,128)(2,1)} %copy.49), calls=%async_computation | async-start | bytes 524288 | tf_op jit(solution)/shard_map/all_to_all | solution.py:400
  117.6 57.3 %copy-start.1 = (bf16[4,16,2048]{2,1,0:T(8,128)(2,1)S(1)}, bf16[4,16,2048]{2,1,0:T(8,128)(2,1)}, u32[]{:S(2)}) copy-start(bf16[4,16,2048]{2,1,0:T(8,128)(2,1)} %shard_map.181) | copy-start | bytes 786436
  174.9 2.0 %copy-start.2 = (bf16[3,64,16,128]{3,2,1,0:T(8,128)(2,1)S(1)}, bf16[3,64,16,128]{3,2,1,0:T(8,128)(2,1)}, u32[]{:S(2)}) copy-start(bf16[3,64,16,128]{3,2,1,0:T(8,128)(2,1)} %shard_map.183) | copy-start | bytes 2359300
  177.5 11.8 %copy-start.5 = (f32[2048]{0:T(1024)S(1)}, f32[2048]{0:T(1024)}, u32[]{:S(2)}) copy-start(f32[2048]{0:T(1024)} %param.37) | copy-start | bytes 24580

commit v9 on v8

--- a/solution.py
+++ b/solution.py
@@ -363,6 +363,68 @@
         ],
         compiler_params=pltpu.CompilerParams(collective_id=4, has_side_effects=True),
     )(terms, residual_block)
+
+
+def _finish_kernel(terms_ref, hidden_ref, gain_ref, out_ref, parts, t_send, t_recv, t_local):
+    replicas = terms_ref.shape[0]
+    me_e = lax.axis_index("ep")
+    me_r = lax.axis_index("rep")
+    mesh_id = pl.DeviceIdType.MESH
+
+    def t_copy(peer, slot):
+        return pltpu.make_async_remote_copy(
+            terms_ref.at[peer],
+            parts.at[slot],
+            t_send.at[peer],
+            t_recv.at[slot],
+            device_id=(me_e, peer),
+            device_id_type=mesh_id,
+        )
+
+    barrier = pltpu.get_barrier_semaphore()
+    for step in range(1, replicas):
+        pl.semaphore_signal(
+            barrier, 1, device_id=(me_e, lax.rem(me_r + step, replicas)), device_id_type=mesh_id
+        )
+    pl.semaphore_wait(barrier, replicas - 1)
+    local = pltpu.make_async_copy(terms_ref.at[me_r], parts.at[me_r], t_local)
+    local.start()
+    for step in range(1, replicas):
+        t_copy(lax.rem(me_r + step, replicas), me_r).start()
+    local.wait()
+    for step in range(1, replicas):
+        peer = lax.rem(me_r + step, replicas)
+        t_copy(peer, peer).wait_recv()
+    total = parts[0].astype(jnp.float32)
+    for source in range(1, replicas):
+        total = total + parts[source].astype(jnp.float32)
+    mixed = total + hidden_ref[...].astype(jnp.float32)
+    inverse = lax.rsqrt(jnp.mean(mixed * mixed, axis=1, keepdims=True) + EPSILON)
+    out_ref[...] = (mixed * inverse * gain_ref[...]).astype(out_ref.dtype)
+    for step in range(1, replicas):
+        t_copy(lax.rem(me_r + step, replicas), me_r).wait_send()
+
+
+def finish_rows(terms, hidden_block, gain):
+    replicas = terms.shape[0]
+    block = terms.shape[1:]
+    return pl.pallas_call(
+        _finish_kernel,
+        out_shape=jax.ShapeDtypeStruct(block, hidden_block.dtype),
+        in_specs=[
+            pl.BlockSpec(memory_space=pl.ANY),
+            pl.BlockSpec(memory_space=pltpu.VMEM),
+            pl.BlockSpec(memory_space=pltpu.VMEM),
+        ],
+        out_specs=pl.BlockSpec(memory_space=pltpu.VMEM),
+        scratch_shapes=[
+            pltpu.VMEM(terms.shape, terms.dtype),
+            pltpu.SemaphoreType.DMA((replicas,)),
+            pltpu.SemaphoreType.DMA((replicas,)),
+            pltpu.SemaphoreType.DMA(()),
+        ],
+        compiler_params=pltpu.CompilerParams(collective_id=5, has_side_effects=True),
+    )(terms, hidden_block, gain.reshape(1, -1))
 
 
 def rep_exchange(blocks):
@@ -470,15 +532,11 @@
         combine, returned.astype(jnp.float32), precision=lax.Precision.HIGHEST,
         preferred_element_type=jnp.float32,
     )
-    row_sums = jnp.sum(
-        rep_exchange(
-            (routed + shared_terms).astype(jnp.bfloat16).reshape(replicas, own_count, model_width)
-        ).astype(jnp.float32),
-        axis=0,
-    )
-    mixed = row_sums + own_hidden.astype(jnp.float32)
-    inverse = lax.rsqrt(jnp.mean(mixed * mixed, axis=1, keepdims=True) + EPSILON)
-    return (mixed * inverse * norm_gain).astype(jnp.bfloat16)
+    return finish_rows(
+        (routed + shared_terms).astype(jnp.bfloat16).reshape(replicas, own_count, model_width),
+        own_hidden,
+        norm_gain,
+    )
 
 
 def solution(mesh):

time: 191 us -> 193 us (1.010)
  blocking collectives: 8.57 us -> 0 us
  Pallas kernels: 122 us -> 130 us
  local copies, waits for them, and re-layouts: 24.7 us -> 27.5 us
    all_to_all x1 -> x0, blocking collectives: 8.57 us -> none  [rep_exchange(): lax.all_to_all(blocks, 'rep', split_axis=0, concat_axis=0, tiled=True)]
    pallas_call x0 -> x1, Pallas kernels: none -> 7.81 us  [finish_rows(): pl.pallas_call(_finish_kernel, out_shape=jax.ShapeDtypeStruct(block, hidd...]
    unnamed x22 -> x21, local copies, waits for them, and re-layouts: 5.27 us -> 6.74 us
where the time goes in v9:
time: 193 us; the launch traced here: 192 us
  Pallas kernels  130 us (67%)
  local copies, waits for them, and re-layouts  27.5 us (14%)
  matrix products  26.1 us (14%)
  starting transfers between devices  4.84 us (3%)
  other arithmetic  2.98 us (2%)
    pallas_call x1, Pallas kernels, combine_return(): pl.pallas_call(_combine_kernel, out_shape=jax.ShapeDtypeStruct((chunks, g...  57.3 us
    pallas_call x1, Pallas kernels, dispatch(): pl.pallas_call(_dispatch_kernel, out_shape=jax.ShapeDtypeStruct(out_shape...  52.9 us
    pallas_call x1, Pallas kernels, hidden_rows(): pl.pallas_call(_hidden_kernel, out_shape=jax.ShapeDtypeStruct(terms.shape...  12 us
    dot_general x1, matrix products, per_device(): jnp.einsum('cqgf,fd->qcgd', activated, expert_down[0], preferred_element_...  8.22 us
    pallas_call x1, Pallas kernels, finish_rows(): pl.pallas_call(_finish_kernel, out_shape=jax.ShapeDtypeStruct(block, hidd...  7.81 us
    unnamed x21, local copies, waits for them, and re-layouts  6.74 us
    reshape x1, local copies, waits for them, and re-layouts, per_device(): dispatch(outgoing, replicas)  5.82 us
    dot_general x1, matrix products, per_device(): jnp.einsum('cqgd,df->cqgf', gathered, expert_gate[0], preferred_element_t...  5.15 us
  transfers between devices with their start and end apart: 1, of which 0 were waited for; matrix products, arithmetic and copies ran while one was open for 4% of the time, Pallas kernels for 0%

profile of v9, /device:TPU:1, one launch (start us, length us, event | category | flops | bytes accessed | tf_op | source)
XLA Modules:
  0.0 191.8 jit_solution(3349590721106754998)
XLA Ops:
  0.0 1.2 copy.63
  1.2 1.2 reshape.211
  2.4 0.9 reshape.210
  3.3 1.0 fusion.56
  4.4 0.1 reshape.207
  4.5 1.7 fusion.83
  6.2 0.3 fusion.21
  6.5 1.3 fusion.16
  7.8 2.1 %fusion.40 = bf16[16,16,512]{2,1,0:T(8,128)(2,1)S(1)} fusion(bf16[1024,512,1]{1,0,2:T(8,128)(2,1)S(1)} %bitcast.117, f32[16,16,1024]{2,1,0:T(8,128)} %fusion.16, f32[16,1024]{1,0:T(8,128)S(1)} %reshape.207), kind=kOutput, calls=%fused_computation.30 | convolution fusion | flops 270140672 | bytes 2424832 | tf_op jit(solution)/shard_map/thp,pr->thr/dot_general | solution.py:49
  10.0 0.8 copy.49
  10.8 4.8 %all-to-all-start = ((bf16[16,16,512]{2,0,1:T(8,128)(2,1)}), bf16[16,16,512]{2,0,1:T(8,128)(2,1)S(1)}, u32[]{:S(2)}, u32[]{:S(2)}) async-start(bf16[16,16,512]{2,0,1:T(8,128)(2,1)} %copy.49), calls=%async_computation | async-start | bytes 524288 | tf_op jit(solution)/shard_map/all_to_all | solution.py:462
  15.6 0.3 select_reduce_fusion.2
  15.9 0.1 copy.42
  16.0 0.1 eq.72
  16.2 0.1 eq.68
  16.3 0.9 reduce-window.6
  17.2 0.2 slice_reduce_fusion
  17.5 0.1 fusion.60
  17.7 0.1 mul.86
  17.9 0.1 copy.52
  18.0 0.2 mul.96
  18.2 2.9 %scatter_custom_fusion = s32[768]{0:T(1024)S(1)} fusion(s32[384]{0:T(512)S(1)} %fusion.78, s32[384]{0:T(512)S(1)} %add_select_fusion, s32[]{:T(128)} %constant.22.clone.1), kind=kCustom, calls=%fused_computation.84 | custom fusion | bytes 3076 | tf_op jit(solution)/shard_map/scatter | solution.py:499
  21.1 0.1 reshape.215
  21.2 0.1 dynamic-slice_bitcast_fusion
  21.3 0.1 reshape.216
  21.5 0.2 and.16
  21.6 0.1 copy.46
  21.8 0.2 select_reduce_fusion.1
  22.0 1.5 constant_dynamic-slice_fusion.1.resid_ref
  23.5 0.2 fusion.44
  23.7 1.2 convolution_convert_fusion.1
  24.9 12.0 %shard_map.181 = bf16[4,16,2048]{2,1,0:T(8,128)(2,1)} custom-call(bf16[4,16,2048]{2,1,0:T(8,128)(2,1)} %bitcast.115, bf16[16,2048]{1,0:T(8,128)(2,1)} %constant_dynamic-slice_fusion.1.resid_ref), custom_call_target="tpu_custom_call" | custom-call | tf_op jit(solution)/shard_map/pallas_call | solution.py:349
  36.9 1.5 constant_dynamic-slice_fusion.hidden_ref
  38.4 1.0 concatenate.3
  39.4 1.1 gather_fusion
  40.5 1.0 copy.64
  41.6 52.9 %shard_map.182 = bf16[3,4,64,16,128]{4,3,2,1,0:T(8,128)(2,1)} custom-call(bf16[3,64,16,128]{3,2,1,0:T(8,128)(2,1)} %bitcast.112), custom_call_target="tpu_custom_call" | custom-call | tf_op jit(solution)/shard_map/pallas_call | solution.py:166
  94.5 5.8 %reshape.218 = bf16[3,4,64,2048]{3,2,1,0:T(8,128)(2,1)} reshape(bf16[3,4,64,16,128]{4,3,2,1,0:T(8,128)(2,1)} %shard_map.182) | data formatting | bytes 6291456 | tf_op jit(solution)/shard_map/reshape | solution.py:505
  100.4 5.1 %fusion.6 = f32[3,4,64,352]{3,2,1,0:T(8,128)} fusion(bf16[3,4,64,2048]{3,2,1,0:T(8,128)(2,1)} %reshape.218, bf16[1,2048,352]{1,2,0:T(8,128)(2,1)} %param.31), kind=kOutput, calls=%fused_computation.11 | convolution fusion | flops 1107296256 | bytes 5668864 | tf_op jit(solution)/shard_map/cqgd,df->cqgf/dot_general | solution.py:506
  105.5 8.2 %convolution_convert_fusion = bf16[3,4,64,2048]{3,2,1,0:T(8,128)(2,1)} fusion(bf16[1,352,2048]{2,1,0:T(8,128)(2,1)} %param.33, bf16[3,4,64,2048]{3,2,1,0:T(8,128)(2,1)} %reshape.218, bf16[1,2048,352]{1,2,0:T(8,128)(2,1)} %param.32, f32[3,4,64,352]{3,2,1,0:T(8,128)} %fusion.6), kind=kOutput, calls=%fused_computation.4 | convolution fusion | flops 2217787392 | bytes 10256384 | tf_op jit(solution)/shard_map/cqgf,fd->qcgd/dot_general | solution.py:513
  113.7 2.9 %copy.65 = bf16[96,8,16,128]{3,2,1,0:T(8,128)(2,1)S(1)} copy(bf16[96,8,16,128]{3,1,2,0:T(8,128)(2,1)} %bitcast.110) | data formatting | bytes 6291456
  116.6 2.2 %copy.60.terms_ref = bf16[4,3,64,16,128]{4,3,2,1,0:T(8,128)(2,1)} copy(bf16[4,3,64,16,128]{4,3,2,0,1:T(8,128)(2,1)S(1)} %bitcast.105) | data formatting | bytes 6291456 | tf_op jit(solution)/shard_map/reshape | solution.py:517
  118.9 57.3 %shard_map.183 = bf16[3,64,16,128]{3,2,1,0:T(8,128)(2,1)} custom-call(bf16[4,3,64,16,128]{4,3,2,1,0:T(8,128)(2,1)} %copy.60.terms_ref), custom_call_target="tpu_custom_call" | custom-call | tf_op jit(solution)/shard_map/pallas_call | solution.py:270
  176.2 2.0 %fusion.84 = f32[64,352]{1,0:T(8,128)S(1)} fusion(bf16[64,2048]{1,0:T(8,128)(2,1)S(1)} %bitcast.108, bf16[2048,352]{0,1:T(8,128)(2,1)} %param.34), kind=kOutput, calls=%fused_computation.98 | convolution fusion | flops 92274688 | bytes 1794048 | tf_op jit(solution)/shard_map/dot_general | solution.py:477
  178.3 0.6 fusion.47
  178.8 3.7 %fusion.2 = bf16[64,2048]{1,0:T(8,128)(2,1)} fusion(f32[64,2048]{1,0:T(8,128)S(1)} %fusion.47, bf16[352,2048]{1,0:T(8,128)(2,1)} %param.36, bf16[64,2048]{1,0:T(8,128)(2,1)S(1)} %bitcast.109, bf16[2048,352]{0,1:T(8,128)(2,1)} %param.35, f32[64,352]{1,0:T(8,128)S(1)} %fusion.84), kind=kOutput, calls=%fused_computation.6 | convolution fusion | flops 184946688 | bytes 4022272 | tf_op jit(solution)/shard_map/dot_general | solution.py:480
  182.5 7.8 %shard_map.184 = bf16[16,2048]{1,0:T(8,128)(2,1)} custom-call(bf16[4,16,2048]{2,1,0:T(8,128)(2,1)} %bitcast.120, bf16[16,2048]{1,0:T(8,128)(2,1)} %constant_dynamic-slice_fusion.hidden_ref, f32[1,2048]{1,0:T(1,128)} %bitcast.122), custom_call_target="tpu_custom_call" | custom-call | tf_op jit(solution)/shard_map/pallas_call | solution.py:411
  190.3 1.5 copy.77
  (34 shorter events, 0.5 us)
Async XLA Ops:
  0.0 23.7 %copy-start = (bf16[512,2048]{1,0:T(8,128)(2,1)S(1)}, bf16[512,2048]{1,0:T(8,128)(2,1)}, u32[]{:S(2)}) copy-start(bf16[512,2048]{1,0:T(8,128)(2,1)} %param.27) | copy-start | bytes 6291460
  6.5 1.3 copy-start.3
  7.8 7.8 %copy-start.6 = (s32[64,6]{0,1:T(8,128)S(1)}, s32[64,6]{0,1:T(8,128)}, u32[]{:S(2)}) copy-start(s32[64,6]{0,1:T(8,128)} %param.28) | copy-start | bytes 4612
  7.8 7.8 %copy-start.7 = (s32[64]{0:T(128)S(1)}, s32[64]{0:T(128)}, u32[]{:S(2)}) copy-start(s32[64]{0:T(128)} %param.30) | copy-start | bytes 772
  9.9 11.7 %copy-start.5 = (f32[64,6]{0,1:T(8,128)S(1)}, f32[64,6]{0,1:T(8,128)}, u32[]{:S(2)}) copy-start(f32[64,6]{0,1:T(8,128)} %param.29) | copy-start | bytes 4612
  9.9 13.6 %copy-start.4 = (bf16[4,512,128]{2,1,0:T(8,128)(2,1)S(1)}, bf16[4,512,128]{2,1,0:T(8,128)(2,1)}, u32[]{:S(2)}) copy-start(bf16[4,512,128]{2,1,0:T(8,128)(2,1)} %param.26) | copy-start | bytes 1572868
  10.8 12.7 %all-to-all-start = ((bf16[16,16,512]{2,0,1:T(8,128)(2,1)}), bf16[16,16,512]{2,0,1:T(8,128)(2,1)S(1)}, u32[]{:S(2)}, u32[]{:S(2)}) async-start(bf16[16,16,512]{2,0,1:T(8,128)(2,1)} %copy.49), calls=%async_computation | async-start | bytes 524288 | tf_op jit(solution)/shard_map/all_to_all | solution.py:462
  118.9 57.4 %copy-start.1 = (bf16[4,16,2048]{2,1,0:T(8,128)(2,1)S(1)}, bf16[4,16,2048]{2,1,0:T(8,128)(2,1)}, u32[]{:S(2)}) copy-start(bf16[4,16,2048]{2,1,0:T(8,128)(2,1)} %shard_map.181) | copy-start | bytes 786436
  176.2 2.0 %copy-start.2 = (bf16[3,64,16,128]{3,2,1,0:T(8,128)(2,1)S(1)}, bf16[3,64,16,128]{3,2,1,0:T(8,128)(2,1)}, u32[]{:S(2)}) copy-start(bf16[3,64,16,128]{3,2,1,0:T(8,128)(2,1)} %shard_map.183) | copy-start | bytes 2359300

commit v10 on v8

--- a/solution.py
+++ b/solution.py
@@ -223,12 +223,17 @@
     pl.semaphore_wait(barrier, groups - 1 + replicas - 1)
 
     x_locals = []
-    for c in range(chunks):
+
+    def issue(c):
         local = pltpu.make_async_copy(terms_ref.at[me_r, c], parts.at[c, me_r], x_local.at[c])
         local.start()
         x_locals.append(local)
         for step in range(1, replicas):
             x_copy(c, lax.rem(me_r + step, replicas), me_r).start()
+
+    ahead = 2
+    for c in range(min(ahead, chunks)):
+        issue(c)
 
     ep_locals = []
     for c in range(chunks):
@@ -249,6 +254,8 @@
             return carry
 
         lax.fori_loop(1, groups, send, 0)
+        if c + ahead < chunks:
+            issue(c + ahead)
 
     for c in range(chunks):
         for step in range(1, replicas):

time: 191 us -> 191 us (level)
  no operation moved by 1% of the time
where the time goes in v10:
time: 191 us; the launch traced here: 190 us
  Pallas kernels  122 us (64%)
  matrix products  25.4 us (13%)
  local copies, waits for them, and re-layouts  24.7 us (13%)
  blocking collectives  8.57 us (4%)
  starting transfers between devices  4.84 us (3%)
  other arithmetic  3.88 us (2%)
    pallas_call x1, Pallas kernels, combine_return(): pl.pallas_call(_combine_kernel, out_shape=jax.ShapeDtypeStruct((chunks, g...  57.3 us
    pallas_call x1, Pallas kernels, dispatch(): pl.pallas_call(_dispatch_kernel, out_shape=jax.ShapeDtypeStruct(out_shape...  52.9 us
    pallas_call x1, Pallas kernels, hidden_rows(): pl.pallas_call(_hidden_kernel, out_shape=jax.ShapeDtypeStruct(terms.shape...  12 us
    all_to_all x1, blocking collectives, rep_exchange(): lax.all_to_all(blocks, 'rep', split_axis=0, concat_axis=0, tiled=True)  8.57 us
    dot_general x1, matrix products, per_device(): jnp.einsum('cqgf,fd->qcgd', activated, expert_down[0], preferred_element_...  8.22 us
    reshape x1, local copies, waits for them, and re-layouts, per_device(): dispatch(outgoing, replicas)  5.82 us
    unnamed x22, local copies, waits for them, and re-layouts  5.27 us
    dot_general x1, matrix products, per_device(): jnp.einsum('cqgd,df->cqgf', gathered, expert_gate[0], preferred_element_t...  5.15 us
  transfers between devices with their start and end apart: 1, of which 0 were waited for; matrix products, arithmetic and copies ran while one was open for 4% of the time, Pallas kernels for 0%

profile of v10, /device:TPU:1, one launch (start us, length us, event | category | flops | bytes accessed | tf_op | source)
XLA Modules:
  0.0 190.0 jit_solution(10311859260093177621)
XLA Ops:
  0.0 1.2 copy.63
  1.2 1.2 reshape.217
  2.4 0.9 reshape.216
  3.3 1.0 fusion.56
  4.4 0.1 reshape.213
  4.5 1.7 fusion.83
  6.2 0.3 fusion.21
  6.5 1.3 fusion.16
  7.8 2.1 %fusion.40 = bf16[16,16,512]{2,1,0:T(8,128)(2,1)S(1)} fusion(bf16[1024,512,1]{1,0,2:T(8,128)(2,1)S(1)} %bitcast.117, f32[16,16,1024]{2,1,0:T(8,128)} %fusion.16, f32[16,1024]{1,0:T(8,128)S(1)} %reshape.213), kind=kOutput, calls=%fused_computation.30 | convolution fusion | flops 270140672 | bytes 2424832 | tf_op jit(solution)/shard_map/thp,pr->thr/dot_general | solution.py:49
  10.0 0.8 copy.49
  10.8 4.8 %all-to-all-start = ((bf16[16,16,512]{2,0,1:T(8,128)(2,1)}), bf16[16,16,512]{2,0,1:T(8,128)(2,1)S(1)}, u32[]{:S(2)}, u32[]{:S(2)}) async-start(bf16[16,16,512]{2,0,1:T(8,128)(2,1)} %copy.49), calls=%async_computation | async-start | bytes 524288 | tf_op jit(solution)/shard_map/all_to_all | solution.py:407
  15.6 0.3 select_reduce_fusion.2
  15.9 0.1 copy.42
  16.0 0.1 eq.72
  16.2 0.1 eq.68
  16.3 0.9 reduce-window.6
  17.2 0.2 slice_reduce_fusion
  17.5 0.1 fusion.60
  17.7 0.1 mul.105
  17.9 0.1 copy.52
  18.0 0.2 mul.115
  18.2 3.1 %scatter_custom_fusion = s32[768]{0:T(1024)S(1)} fusion(s32[384]{0:T(512)S(1)} %fusion.78, s32[384]{0:T(512)S(1)} %add_select_fusion, s32[]{:T(128)} %constant.24.clone.1), kind=kCustom, calls=%fused_computation.88 | custom fusion | bytes 3076 | tf_op jit(solution)/shard_map/scatter | solution.py:444
  21.3 0.1 reshape.221
  21.4 0.1 dynamic-slice_bitcast_fusion
  21.5 0.1 reshape.222
  21.6 0.2 and.16
  21.8 0.1 copy.46
  22.0 0.2 select_reduce_fusion.1
  22.2 1.5 constant_dynamic-slice_fusion.resid_ref
  23.7 0.2 fusion.44
  23.9 1.2 convolution_convert_fusion.1
  25.1 12.0 %shard_map.181 = bf16[4,16,2048]{2,1,0:T(8,128)(2,1)} custom-call(bf16[4,16,2048]{2,1,0:T(8,128)(2,1)} %bitcast.115, bf16[16,2048]{1,0:T(8,128)(2,1)} %constant_dynamic-slice_fusion.resid_ref), custom_call_target="tpu_custom_call" | custom-call | tf_op jit(solution)/shard_map/pallas_call | solution.py:356
  37.1 1.0 concatenate.3
  38.1 1.1 gather_fusion
  39.3 1.0 copy.64
  40.3 52.9 %shard_map.182 = bf16[3,4,64,16,128]{4,3,2,1,0:T(8,128)(2,1)} custom-call(bf16[3,64,16,128]{3,2,1,0:T(8,128)(2,1)} %bitcast.112), custom_call_target="tpu_custom_call" | custom-call | tf_op jit(solution)/shard_map/pallas_call | solution.py:166
  93.2 5.8 %reshape.224 = bf16[3,4,64,2048]{3,2,1,0:T(8,128)(2,1)} reshape(bf16[3,4,64,16,128]{4,3,2,1,0:T(8,128)(2,1)} %shard_map.182) | data formatting | bytes 6291456 | tf_op jit(solution)/shard_map/reshape | solution.py:450
  99.1 5.1 %fusion.6 = f32[3,4,64,352]{3,2,1,0:T(8,128)} fusion(bf16[3,4,64,2048]{3,2,1,0:T(8,128)(2,1)} %reshape.224, bf16[1,2048,352]{1,2,0:T(8,128)(2,1)} %param.31), kind=kOutput, calls=%fused_computation.11 | convolution fusion | flops 1107296256 | bytes 5668864 | tf_op jit(solution)/shard_map/cqgd,df->cqgf/dot_general | solution.py:451
  104.2 8.2 %convolution_convert_fusion = bf16[3,4,64,2048]{3,2,1,0:T(8,128)(2,1)} fusion(bf16[1,352,2048]{2,1,0:T(8,128)(2,1)} %param.33, bf16[3,4,64,2048]{3,2,1,0:T(8,128)(2,1)} %reshape.224, bf16[1,2048,352]{1,2,0:T(8,128)(2,1)} %param.32, f32[3,4,64,352]{3,2,1,0:T(8,128)} %fusion.6), kind=kOutput, calls=%fused_computation.4 | convolution fusion | flops 2217787392 | bytes 10256384 | tf_op jit(solution)/shard_map/cqgf,fd->qcgd/dot_general | solution.py:458
  112.4 2.9 %copy.65 = bf16[96,8,16,128]{3,2,1,0:T(8,128)(2,1)S(1)} copy(bf16[96,8,16,128]{3,1,2,0:T(8,128)(2,1)} %bitcast.110) | data formatting | bytes 6291456
  115.4 2.2 %copy.60.terms_ref = bf16[4,3,64,16,128]{4,3,2,1,0:T(8,128)(2,1)} copy(bf16[4,3,64,16,128]{4,3,2,0,1:T(8,128)(2,1)S(1)} %bitcast.104) | data formatting | bytes 6291456 | tf_op jit(solution)/shard_map/reshape | solution.py:462
  117.6 57.3 %shard_map.183 = bf16[3,64,16,128]{3,2,1,0:T(8,128)(2,1)} custom-call(bf16[4,3,64,16,128]{4,3,2,1,0:T(8,128)(2,1)} %copy.60.terms_ref), custom_call_target="tpu_custom_call" | custom-call | tf_op jit(solution)/shard_map/pallas_call | solution.py:277
  174.9 2.0 %fusion.84 = f32[64,352]{1,0:T(8,128)S(1)} fusion(bf16[64,2048]{1,0:T(8,128)(2,1)S(1)} %bitcast.106, bf16[2048,352]{0,1:T(8,128)(2,1)} %param.34), kind=kOutput, calls=%fused_computation.102 | convolution fusion | flops 92274688 | bytes 1794048 | tf_op jit(solution)/shard_map/dot_general | solution.py:422
  176.9 0.6 fusion.47
  177.5 3.0 %fusion.2 = bf16[64,2048]{1,0:T(8,128)(2,1)S(1)} fusion(f32[64,2048]{1,0:T(8,128)S(1)} %fusion.47, bf16[352,2048]{1,0:T(8,128)(2,1)} %param.36, bf16[64,2048]{1,0:T(8,128)(2,1)S(1)} %bitcast.107, bf16[2048,352]{0,1:T(8,128)(2,1)} %param.35, f32[64,352]{1,0:T(8,128)S(1)} %fusion.84), kind=kOutput, calls=%fused_computation.6 | convolution fusion | flops 184946688 | bytes 4022272 | tf_op jit(solution)/shard_map/dot_general | solution.py:425
  180.5 8.6 %all_to_all.23 = bf16[4,16,2048]{2,1,0:T(8,128)(2,1)S(1)} all-to-all(bf16[4,16,2048]{2,1,0:T(8,128)(2,1)S(1)} %bitcast.120), channel_id=1, replica_groups=mesh['ep'=64,'rep'=4] {'rep'}, dimensions={0} | all-to-all | bytes 524288 | tf_op jit(solution)/shard_map/all_to_all | solution.py:376
  189.1 0.1 multiply_reduce_fusion.1
  189.3 0.7 multiply_convert_fusion
  (38 shorter events, 0.5 us)
Async XLA Ops:
  0.0 23.9 %copy-start = (bf16[512,2048]{1,0:T(8,128)(2,1)S(1)}, bf16[512,2048]{1,0:T(8,128)(2,1)}, u32[]{:S(2)}) copy-start(bf16[512,2048]{1,0:T(8,128)(2,1)} %param.27) | copy-start | bytes 6291460
  6.5 1.3 copy-start.3
  7.8 7.8 %copy-start.7 = (s32[64,6]{0,1:T(8,128)S(1)}, s32[64,6]{0,1:T(8,128)}, u32[]{:S(2)}) copy-start(s32[64,6]{0,1:T(8,128)} %param.28) | copy-start | bytes 4612
  7.8 7.8 %copy-start.8 = (s32[64]{0:T(128)S(1)}, s32[64]{0:T(128)}, u32[]{:S(2)}) copy-start(s32[64]{0:T(128)} %param.30) | copy-start | bytes 772
  9.9 11.9 %copy-start.6 = (f32[64,6]{0,1:T(8,128)S(1)}, f32[64,6]{0,1:T(8,128)}, u32[]{:S(2)}) copy-start(f32[64,6]{0,1:T(8,128)} %param.29) | copy-start | bytes 4612
  9.9 13.7 %copy-start.4 = (bf16[4,512,128]{2,1,0:T(8,128)(2,1)S(1)}, bf16[4,512,128]{2,1,0:T(8,128)(2,1)}, u32[]{:S(2)}) copy-start(bf16[4,512,128]{2,1,0:T(8,128)(2,1)} %param.26) | copy-start | bytes 1572868
  10.8 12.9 %all-to-all-start = ((bf16[16,16,512]{2,0,1:T(8,128)(2,1)}), bf16[16,16,512]{2,0,1:T(8,128)(2,1)S(1)}, u32[]{:S(2)}, u32[]{:S(2)}) async-start(bf16[16,16,512]{2,0,1:T(8,128)(2,1)} %copy.49), calls=%async_computation | async-start | bytes 524288 | tf_op jit(solution)/shard_map/all_to_all | solution.py:407
  117.6 57.3 %copy-start.1 = (bf16[4,16,2048]{2,1,0:T(8,128)(2,1)S(1)}, bf16[4,16,2048]{2,1,0:T(8,128)(2,1)}, u32[]{:S(2)}) copy-start(bf16[4,16,2048]{2,1,0:T(8,128)(2,1)} %shard_map.181) | copy-start | bytes 786436
  174.9 2.0 %copy-start.2 = (bf16[3,64,16,128]{3,2,1,0:T(8,128)(2,1)S(1)}, bf16[3,64,16,128]{3,2,1,0:T(8,128)(2,1)}, u32[]{:S(2)}) copy-start(bf16[3,64,16,128]{3,2,1,0:T(8,128)(2,1)} %shard_map.183) | copy-start | bytes 2359300
  177.5 11.8 %copy-start.5 = (f32[2048]{0:T(1024)S(1)}, f32[2048]{0:T(1024)}, u32[]{:S(2)}) copy-start(f32[2048]{0:T(1024)} %param.37) | copy-start | bytes 24580

commit v11 on v10

--- a/solution.py
+++ b/solution.py
@@ -182,14 +182,14 @@
 
 
 def _combine_kernel(terms_ref, out_ref, parts, sums, x_send, x_recv, x_local, ep_send, ep_recv, ep_local):
-    replicas, chunks, groups = terms_ref.shape[:3]
+    chunks, replicas, groups = terms_ref.shape[:3]
     me_e = lax.axis_index("ep")
     me_r = lax.axis_index("rep")
     mesh_id = pl.DeviceIdType.MESH
 
     def x_copy(c, peer, slot):
         return pltpu.make_async_remote_copy(
-            terms_ref.at[peer, c],
+            terms_ref.at[c, peer],
             parts.at[c, slot],
             x_send.at[c, peer],
             x_recv.at[c, slot],
@@ -225,7 +225,7 @@
     x_locals = []
 
     def issue(c):
-        local = pltpu.make_async_copy(terms_ref.at[me_r, c], parts.at[c, me_r], x_local.at[c])
+        local = pltpu.make_async_copy(terms_ref.at[c, me_r], parts.at[c, me_r], x_local.at[c])
         local.start()
         x_locals.append(local)
         for step in range(1, replicas):
@@ -272,7 +272,7 @@
 
 
 def combine_return(terms):
-    replicas, chunks, groups = terms.shape[:3]
+    chunks, replicas, groups = terms.shape[:3]
     tile = terms.shape[3:]
     return pl.pallas_call(
         _combine_kernel,
@@ -447,20 +447,22 @@
     padded = jnp.concatenate([hidden, jnp.zeros((1, model_width), jnp.bfloat16)], axis=0)
     lanes = 128
     outgoing = padded[own_source].reshape(share, experts, model_width // lanes, lanes)
-    gathered = dispatch(outgoing, replicas).reshape(share, replicas, expert_groups, model_width)
+    gathered = dispatch(outgoing, replicas)
+    tiles = (model_width // lanes, lanes)
     gate_values = jnp.einsum(
-        "cqgd,df->cqgf", gathered, expert_gate[0], preferred_element_type=jnp.float32
+        "cqgxy,xyf->cqgf", gathered, expert_gate[0].reshape(tiles + (-1,)),
+        preferred_element_type=jnp.float32,
     )
     up_values = jnp.einsum(
-        "cqgd,df->cqgf", gathered, expert_up[0], preferred_element_type=jnp.float32
+        "cqgxy,xyf->cqgf", gathered, expert_up[0].reshape(tiles + (-1,)),
+        preferred_element_type=jnp.float32,
     )
     activated = (jax.nn.silu(gate_values) * up_values).astype(jnp.bfloat16)
     expert_terms = jnp.einsum(
-        "cqgf,fd->qcgd", activated, expert_down[0], preferred_element_type=jnp.float32
+        "cqgf,fxy->cqgxy", activated, expert_down[0].reshape((-1,) + tiles),
+        preferred_element_type=jnp.float32,
     ).astype(jnp.bfloat16)
-    returned = combine_return(
-        expert_terms.reshape(expert_terms.shape[:3] + (model_width // lanes, lanes))
-    ).reshape(share * experts, model_width)
+    returned = combine_return(expert_terms).reshape(share * experts, model_width)
     local_pos = position - rep_index * share
     mine = (local_pos >= 0) & (local_pos < share)
     column = jnp.clip(local_pos, 0, share - 1) * experts + slot_index

time: 191 us -> 208 us (1.089)
  local copies, waits for them, and re-layouts: 24.7 us -> 35.4 us
  other arithmetic: 3.88 us -> 9.51 us
    reshape x2 -> x0, local copies, waits for them, and re-layouts: 8.06 us -> none  [the longest x1 5.82 us: per_device(): dispatch(outgoing, replicas)]
    dot_general x0 -> x1, local copies, waits for them, and re-layouts: none -> 6 us  [per_device(): jnp.einsum('cqgf,fxy->cqgxy', activated, expert_down[0].reshape((-1,) + t...]
    transpose x2, local copies, waits for them, and re-layouts: 0.15 us -> 2.26 us  [per_device(): lax.dynamic_slice_in_dim(source_row, rep_index * share, share, 1)]
    unnamed x22 -> x36, local copies, waits for them, and re-layouts: 5.27 us -> 6.94 us
  transfers between devices with their start and end apart: 1 -> 1, of which waited for: 0 -> 0; matrix products, arithmetic and copies ran while one was open for 4% -> 13% of each run, Pallas kernels for 0% -> 0%
where the time goes in v11:
time: 208 us; the launch traced here: 207 us
  Pallas kernels  122 us (59%)
  local copies, waits for them, and re-layouts  35.4 us (17%)
  matrix products  26 us (12%)
  other arithmetic  9.51 us (5%)
  blocking collectives  8.57 us (4%)
  starting transfers between devices  4.84 us (2%)
    pallas_call x1, Pallas kernels, combine_return(): pl.pallas_call(_combine_kernel, out_shape=jax.ShapeDtypeStruct((chunks, g...  57.3 us
    pallas_call x1, Pallas kernels, dispatch(): pl.pallas_call(_dispatch_kernel, out_shape=jax.ShapeDtypeStruct(out_shape...  52.9 us
    pallas_call x1, Pallas kernels, hidden_rows(): pl.pallas_call(_hidden_kernel, out_shape=jax.ShapeDtypeStruct(terms.shape...  12.1 us
    all_to_all x1, blocking collectives, rep_exchange(): lax.all_to_all(blocks, 'rep', split_axis=0, concat_axis=0, tiled=True)  8.57 us
    dot_general x1, matrix products, per_device(): jnp.einsum('cqgf,fxy->cqgxy', activated, expert_down[0].reshape((-1,) + t...  7.82 us
    unnamed x36, local copies, waits for them, and re-layouts  6.94 us
    dot_general x1, local copies, waits for them, and re-layouts, per_device(): jnp.einsum('cqgf,fxy->cqgxy', activated, expert_down[0].reshape((-1,) + t...  6 us
    dot_general x1, matrix products, per_device(): jnp.einsum('cqgxy,xyf->cqgf', gathered, expert_gate[0].reshape(tiles + (-...  5.35 us
  transfers between devices with their start and end apart: 1, of which 0 were waited for; matrix products, arithmetic and copies ran while one was open for 13% of the time, Pallas kernels for 0%

profile of v11, /device:TPU:1, one launch (start us, length us, event | category | flops | bytes accessed | tf_op | source)
XLA Modules:
  0.0 206.9 jit_solution(3134874115301609366)
XLA Ops:
  0.0 1.2 copy.87
  1.2 1.2 reshape.211
  2.4 0.9 reshape.210
  3.3 1.0 fusion.85
  4.5 1.7 fusion.112
  6.5 1.3 fusion.26
  7.8 2.8 %fusion.66 = bf16[16,16,512]{2,1,0:T(8,128)(2,1)} fusion(bf16[1024,512,1]{1,0,2:T(8,128)(2,1)S(1)} %bitcast.121, f32[16,16,1024]{2,1,0:T(8,128)} %fusion.26, f32[16,1024]{1,0:T(8,128)S(1)} %reshape.207), kind=kOutput, calls=%fused_computation.36 | convolution fusion | flops 270140672 | bytes 2424832 | tf_op jit(solution)/shard_map/thp,pr->thr/dot_general | solution.py:49
  10.6 1.9 copy.60
  12.6 4.8 %all-to-all-start = ((bf16[16,16,512]{2,0,1:T(8,128)(2,1)}), bf16[16,16,512]{2,0,1:T(8,128)(2,1)}, u32[]{:S(2)}, u32[]{:S(2)}) async-start(bf16[16,16,512]{2,0,1:T(8,128)(2,1)} %copy.60), calls=%async_computation | async-start | bytes 524288 | tf_op jit(solution)/shard_map/all_to_all | solution.py:407
  17.7 0.7 copy.53
  18.4 0.9 eq.72
  19.3 0.9 eq.68
  20.2 0.6 add_select_fusion
  20.8 0.7 fusion.95
  21.4 2.7 %reduce-window.6 = s32[64,3,128]{2,0,1:T(8,128)} reduce-window(s32[64,3,128]{2,0,1:T(8,128)} %fusion.95, s32[]{:T(128)} %constant.20.clone.1), window={size=1x1x128 pad=0_0x0_0x127_0}, to_apply=%region_1.2 | reduce-window | flops 3121152 | bytes 196612 | tf_op jit(solution)/shard_map/reduce-window
  24.2 1.1 slice_reduce_fusion
  25.3 1.0 fusion.89
  26.3 0.5 compare_and_fusion
  26.8 0.8 mul.105
  27.6 0.8 copy.56
  28.4 0.6 broadcast_multiply_fusion
  29.0 1.4 copy.63
  30.4 0.9 mul.115
  31.3 3.1 %scatter_custom_fusion = s32[768]{0:T(1024)S(1)} fusion(s32[384]{0:T(512)S(1)} %fusion.107, s32[384]{0:T(512)} %add_select_fusion, s32[]{:T(128)} %constant.24.clone.1), kind=kCustom, calls=%fused_computation.99 | custom fusion | bytes 3584 | tf_op jit(solution)/shard_map/scatter | solution.py:444
  34.4 0.7 reshape.215
  35.1 1.4 dynamic-slice_bitcast_fusion
  36.5 0.8 copy.64
  37.5 1.5 copy.89
  39.0 1.4 copy.90
  40.5 1.5 copy.91
  42.4 0.8 select_reduce_fusion.1
  43.2 1.5 constant_dynamic-slice_fusion.resid_ref
  44.6 1.0 copy.61
  45.9 1.2 convolution_convert_fusion
  47.1 12.1 %shard_map.181 = bf16[4,16,2048]{2,1,0:T(8,128)(2,1)} custom-call(bf16[4,16,2048]{2,1,0:T(8,128)(2,1)} %bitcast.119, bf16[16,2048]{1,0:T(8,128)(2,1)} %constant_dynamic-slice_fusion.resid_ref), custom_call_target="tpu_custom_call" | custom-call | tf_op jit(solution)/shard_map/pallas_call | solution.py:356
  59.1 1.0 concatenate.3
  60.1 1.1 gather_fusion
  61.3 1.1 copy.88
  62.4 52.9 %shard_map.182 = bf16[3,4,64,16,128]{4,3,2,1,0:T(8,128)(2,1)} custom-call(bf16[3,64,16,128]{3,2,1,0:T(8,128)(2,1)} %bitcast.110), custom_call_target="tpu_custom_call" | custom-call | tf_op jit(solution)/shard_map/pallas_call | solution.py:166
  115.3 5.3 %fusion.11 = f32[3,4,64,352]{3,2,1,0:T(8,128)} fusion(bf16[16,128,352,1,1]{1,0,2,4,3:T(8,128)(2,1)} %bitcast.117, bf16[3,4,64,16,128]{4,3,2,1,0:T(8,128)(2,1)} %shard_map.182), kind=kOutput, calls=%fused_computation.16 | convolution fusion | flops 1107296256 | bytes 5668864 | tf_op jit(solution)/shard_map/cqgxy,xyf->cqgf/dot_general | solution.py:452
  120.6 7.8 %fusion.7 = bf16[3,4,64,16,128]{4,2,3,1,0:T(8,128)(2,1)} fusion(bf16[352,16,128,1,1]{2,1,0,4,3:T(8,128)(2,1)} %bitcast.116, bf16[16,128,352,1,1]{1,0,2,4,3:T(8,128)(2,1)S(1)} %bitcast.115, bf16[3,4,64,16,128]{4,3,2,1,0:T(8,128)(2,1)} %shard_map.182, f32[3,4,64,352]{3,2,1,0:T(8,128)} %fusion.11), kind=kOutput, calls=%fused_computation.12 | convolution fusion | flops 2216214528 | bytes 10256384 | tf_op jit(solution)/shard_map/cqgf,fxy->cqgxy/dot_general | solution.py:461
  128.4 6.0 %copy.137.terms_ref = bf16[3,4,64,16,128]{4,3,2,1,0:T(8,128)(2,1)} copy(bf16[3,4,64,16,128]{4,2,3,1,0:T(8,128)(2,1)} %fusion.7) | data formatting | bytes 6291456 | tf_op jit(solution)/shard_map/cqgf,fxy->cqgxy/dot_general | solution.py:461
  134.4 57.3 %shard_map.183 = bf16[3,64,16,128]{3,2,1,0:T(8,128)(2,1)} custom-call(bf16[3,4,64,16,128]{4,3,2,1,0:T(8,128)(2,1)} %copy.137.terms_ref), custom_call_target="tpu_custom_call" | custom-call | tf_op jit(solution)/shard_map/pallas_call | solution.py:277
  191.8 2.0 fusion.113
  193.8 0.6 fusion.76
  194.4 3.0 %fusion.6 = bf16[64,2048]{1,0:T(8,128)(2,1)S(1)} fusion(f32[64,2048]{1,0:T(8,128)S(1)} %fusion.76, bf16[352,2048]{1,0:T(8,128)(2,1)} %param.36, bf16[64,2048]{1,0:T(8,128)(2,1)S(1)} %bitcast.106, bf16[2048,352]{0,1:T(8,128)(2,1)} %param.35, f32[64,352]{1,0:T(8,128)S(1)} %fusion.113), kind=kOutput, calls=%fused_computation.10 | convolution fusion | flops 184946688 | bytes 4022272 | tf_op jit(solution)/shard_map/dot_general | solution.py:425
  197.4 8.6 %all_to_all.23 = bf16[4,16,2048]{2,1,0:T(8,128)(2,1)S(1)} all-to-all(bf16[4,16,2048]{2,1,0:T(8,128)(2,1)S(1)} %bitcast.123), channel_id=1, replica_groups=mesh['ep'=64,'rep'=4] {'rep'}, dimensions={0} | all-to-all | bytes 524288 | tf_op jit(solution)/shard_map/all_to_all | solution.py:376
  206.2 0.7 multiply_convert_fusion
  (51 shorter events, 1.9 us)
Async XLA Ops:
  0.0 45.8 %copy-start = (bf16[512,2048]{1,0:T(8,128)(2,1)S(1)}, bf16[512,2048]{1,0:T(8,128)(2,1)}, u32[]{:S(2)}) copy-start(bf16[512,2048]{1,0:T(8,128)(2,1)} %param.27) | copy-start | bytes 6291460
  6.5 1.3 copy-start.7
  7.8 9.6 %copy-start.12 = (s32[64,6]{0,1:T(8,128)S(1)}, s32[64,6]{0,1:T(8,128)}, u32[]{:S(2)}) copy-start(s32[64,6]{0,1:T(8,128)} %param.28) | copy-start | bytes 4612
  7.8 9.6 %copy-start.14 = (s32[64]{0:T(128)S(1)}, s32[64]{0:T(128)}, u32[]{:S(2)}) copy-start(s32[64]{0:T(128)} %param.30) | copy-start | bytes 772
  10.6 26.8 %copy-start.3 = (bf16[1,2048,352]{1,2,0:T(8,128)(2,1)S(1)}, bf16[1,2048,352]{1,2,0:T(8,128)(2,1)}, u32[]{:S(2)}) copy-start(bf16[1,2048,352]{1,2,0:T(8,128)(2,1)} %param.31) | copy-start | bytes 4325380
  12.6 32.1 %all-to-all-start = ((bf16[16,16,512]{2,0,1:T(8,128)(2,1)}), bf16[16,16,512]{2,0,1:T(8,128)(2,1)}, u32[]{:S(2)}, u32[]{:S(2)}) async-start(bf16[16,16,512]{2,0,1:T(8,128)(2,1)} %copy.60), calls=%async_computation | async-start | bytes 524288 | tf_op jit(solution)/shard_map/all_to_all | solution.py:407
  37.5 1.5 copy-start.4
  39.0 1.5 copy-start.5
  40.5 1.5 copy-start.13
  40.5 1.6 copy-start.11
  40.5 5.1 %copy-start.8 = (bf16[4,512,128]{2,1,0:T(8,128)(2,1)S(1)}, bf16[4,512,128]{2,1,0:T(8,128)(2,1)}, u32[]{:S(2)}) copy-start(bf16[4,512,128]{2,1,0:T(8,128)(2,1)} %param.26) | copy-start | bytes 1572868
  115.3 5.4 %copy-start.6 = (bf16[44,8,16,128]{3,2,1,0:T(8,128)(2,1)S(1)}, bf16[44,8,16,128]{3,2,1,0:T(8,128)(2,1)}, u32[]{:S(2)}) copy-start(bf16[44,8,16,128]{3,2,1,0:T(8,128)(2,1)} %copy.90) | copy-start | bytes 4325380
  134.4 57.3 %copy-start.1 = (bf16[4,16,2048]{2,1,0:T(8,128)(2,1)S(1)}, bf16[4,16,2048]{2,1,0:T(8,128)(2,1)}, u32[]{:S(2)}) copy-start(bf16[4,16,2048]{2,1,0:T(8,128)(2,1)} %shard_map.181) | copy-start | bytes 786436
  191.8 2.0 copy-start.2
  191.8 2.0 copy-start.9
  194.4 11.8 %copy-start.10 = (f32[2048]{0:T(1024)S(1)}, f32[2048]{0:T(1024)}, u32[]{:S(2)}) copy-start(f32[2048]{0:T(1024)} %param.37) | copy-start | bytes 24580

commit v12 on v8

--- a/solution.py
+++ b/solution.py
@@ -182,14 +182,14 @@
 
 
 def _combine_kernel(terms_ref, out_ref, parts, sums, x_send, x_recv, x_local, ep_send, ep_recv, ep_local):
-    replicas, chunks, groups = terms_ref.shape[:3]
+    chunks, replicas, groups = terms_ref.shape[:3]
     me_e = lax.axis_index("ep")
     me_r = lax.axis_index("rep")
     mesh_id = pl.DeviceIdType.MESH
 
     def x_copy(c, peer, slot):
         return pltpu.make_async_remote_copy(
-            terms_ref.at[peer, c],
+            terms_ref.at[c, peer],
             parts.at[c, slot],
             x_send.at[c, peer],
             x_recv.at[c, slot],
@@ -224,7 +224,7 @@
 
     x_locals = []
     for c in range(chunks):
-        local = pltpu.make_async_copy(terms_ref.at[me_r, c], parts.at[c, me_r], x_local.at[c])
+        local = pltpu.make_async_copy(terms_ref.at[c, me_r], parts.at[c, me_r], x_local.at[c])
         local.start()
         x_locals.append(local)
         for step in range(1, replicas):
@@ -265,7 +265,7 @@
 
 
 def combine_return(terms):
-    replicas, chunks, groups = terms.shape[:3]
+    chunks, replicas, groups = terms.shape[:3]
     tile = terms.shape[3:]
     return pl.pallas_call(
         _combine_kernel,
@@ -431,12 +431,16 @@
     earlier = jnp.cumsum(one_hot, axis=0) - one_hot
     position = jnp.sum(earlier * one_hot, axis=1)
     assignments = slot_index.shape[0]
-    source_row = (
-        jnp.full((experts * capacity,), group_rows, jnp.int32)
-        .at[slot_index * capacity + position]
-        .set(jnp.arange(assignments, dtype=jnp.int32) // route_count)
-    ).reshape(experts, capacity)
-    own_source = lax.dynamic_slice_in_dim(source_row, rep_index * share, share, 1).T.reshape(-1)
+    row_tag = (jnp.arange(assignments, dtype=jnp.int32) // route_count + 1).astype(jnp.float32)
+    own_pos = rep_index * share + jnp.arange(share, dtype=jnp.int32)
+    filled = jnp.einsum(
+        "ae,ac->ce",
+        one_hot.astype(jnp.float32) * row_tag[:, None],
+        (position[:, None] == own_pos[None, :]).astype(jnp.float32),
+        precision=lax.Precision.HIGHEST,
+        preferred_element_type=jnp.float32,
+    )
+    own_source = jnp.where(filled > 0, filled.astype(jnp.int32) - 1, group_rows).reshape(-1)
     padded = jnp.concatenate([hidden, jnp.zeros((1, model_width), jnp.bfloat16)], axis=0)
     lanes = 128
     outgoing = padded[own_source].reshape(share, experts, model_width // lanes, lanes)
@@ -449,7 +453,7 @@
     )
     activated = (jax.nn.silu(gate_values) * up_values).astype(jnp.bfloat16)
     expert_terms = jnp.einsum(
-        "cqgf,fd->qcgd", activated, expert_down[0], preferred_element_type=jnp.float32
+        "cqgf,fd->cqgd", activated, expert_down[0], preferred_element_type=jnp.float32
     ).astype(jnp.bfloat16)
     returned = combine_return(
         expert_terms.reshape(expert_terms.shape[:3] + (model_width // lanes, lanes))

time: 191 us -> 187 us (0.979)
  local copies, waits for them, and re-layouts: 24.7 us -> 20.6 us
    scatter x1 -> x0, local copies, waits for them, and re-layouts: 3.1 us -> none  [per_device(): source_row = jnp.full((experts * capacity,), group_rows, jnp.int32).at[sl...]
    reshape x3 -> x1, local copies, waits for them, and re-layouts: 2.41 us -> 0.11 us  [per_device(): jnp.where(filled > 0, filled.astype(jnp.int32) - 1, group_rows).reshape(-1)]
    dot_general x1 -> x2, matrix products: 8.22 us -> 8.53 us  [the longest x1 8.22 us: per_device(): jnp.einsum('cqgf,fd->cqgd', activated, expert_down[0], preferred_element_...]
  transfers between devices with their start and end apart: 1 -> 1, of which waited for: 0 -> 1; matrix products, arithmetic and copies ran while one was open for 4% -> 2% of each run, Pallas kernels for 0% -> 0%
where the time goes in v12:
time: 187 us; the launch traced here: 186 us
  Pallas kernels  122 us (65%)
  matrix products  25.7 us (14%)
  local copies, waits for them, and re-layouts  20.6 us (11%)
  blocking collectives  8.38 us (4%)
  starting transfers between devices  4.84 us (3%)
  other arithmetic  3.88 us (2%)
    pallas_call x1, Pallas kernels, combine_return(): pl.pallas_call(_combine_kernel, out_shape=jax.ShapeDtypeStruct((chunks, g...  57.6 us
    pallas_call x1, Pallas kernels, dispatch(): pl.pallas_call(_dispatch_kernel, out_shape=jax.ShapeDtypeStruct(out_shape...  52.8 us
    pallas_call x1, Pallas kernels, hidden_rows(): pl.pallas_call(_hidden_kernel, out_shape=jax.ShapeDtypeStruct(terms.shape...  11.4 us
    all_to_all x1, blocking collectives, rep_exchange(): lax.all_to_all(blocks, 'rep', split_axis=0, concat_axis=0, tiled=True)  8.38 us
    dot_general x1, matrix products, per_device(): jnp.einsum('cqgf,fd->cqgd', activated, expert_down[0], preferred_element_...  8.22 us
    unnamed x22, local copies, waits for them, and re-layouts  6.95 us
    reshape x1, local copies, waits for them, and re-layouts, per_device(): dispatch(outgoing, replicas)  5.82 us
    dot_general x1, matrix products, per_device(): jnp.einsum('cqgd,df->cqgf', gathered, expert_gate[0], preferred_element_t...  5.15 us
  transfers between devices with their start and end apart: 1, of which 1 were waited for; matrix products, arithmetic and copies ran while one was open for 2% of the time, Pallas kernels for 0%

profile of v12, /device:TPU:1, one launch (start us, length us, event | category | flops | bytes accessed | tf_op | source)
XLA Modules:
  0.0 186.4 jit_solution(12137576146173594446)
XLA Ops:
  0.0 1.2 copy.54
  1.2 1.2 reshape.206
  2.4 0.9 reshape.205
  3.3 0.1 iota_add_fusion
  3.3 1.0 fusion.56
  4.4 0.1 reshape.202
  4.5 1.7 fusion.90
  6.2 0.3 fusion.21
  6.5 0.0 copy-start.3
  6.5 1.3 fusion.16
  7.8 2.1 %fusion.40 = bf16[16,16,512]{2,1,0:T(8,128)(2,1)S(1)} fusion(bf16[1024,512,1]{1,0,2:T(8,128)(2,1)S(1)} %bitcast.104, f32[16,16,1024]{2,1,0:T(8,128)} %fusion.16, f32[16,1024]{1,0:T(8,128)S(1)} %reshape.202), kind=kOutput, calls=%fused_computation.29 | convolution fusion | flops 270140672 | bytes 2424832 | tf_op jit(solution)/shard_map/thp,pr->thr/dot_general | solution.py:49
  10.0 0.8 copy.44
  10.8 4.8 %all-to-all-start = ((bf16[16,16,512]{2,0,1:T(8,128)(2,1)}), bf16[16,16,512]{2,0,1:T(8,128)(2,1)S(1)}, u32[]{:S(2)}, u32[]{:S(2)}) async-start(bf16[16,16,512]{2,0,1:T(8,128)(2,1)} %copy.44), calls=%async_computation | async-start | bytes 524288 | tf_op jit(solution)/shard_map/all_to_all | solution.py:400
  15.6 0.3 select_reduce_fusion.2
  15.9 0.1 copy.37
  16.0 0.1 eq.85
  16.2 0.1 eq.81
  16.3 0.9 reduce-window.6
  17.2 0.2 slice_reduce_fusion
  17.5 0.1 fusion.59
  17.7 0.3 add_select_fusion.1
  18.0 0.1 reshape.210
  18.1 0.1 mul.97
  18.3 0.1 copy.40
  18.3 0.2 and.20
  18.5 0.1 copy.41
  18.6 0.1 copy.42
  18.7 0.2 select_reduce_fusion.1
  18.9 1.5 constant_dynamic-slice_fusion.resid_ref
  20.4 0.8 all-to-all-done
  21.2 0.2 fusion.44
  21.4 1.2 convolution_convert_fusion.1
  22.6 11.4 %shard_map.181 = bf16[4,16,2048]{2,1,0:T(8,128)(2,1)} custom-call(bf16[4,16,2048]{2,1,0:T(8,128)(2,1)} %bitcast.102, bf16[16,2048]{1,0:T(8,128)(2,1)} %constant_dynamic-slice_fusion.resid_ref), custom_call_target="tpu_custom_call" | custom-call | tf_op jit(solution)/shard_map/pallas_call | solution.py:349
  34.1 1.0 concatenate.3
  35.0 1.1 gather_fusion
  36.2 1.0 copy.55
  37.2 52.8 %shard_map.182 = bf16[3,4,64,16,128]{4,3,2,1,0:T(8,128)(2,1)} custom-call(bf16[3,64,16,128]{3,2,1,0:T(8,128)(2,1)} %bitcast.99), custom_call_target="tpu_custom_call" | custom-call | tf_op jit(solution)/shard_map/pallas_call | solution.py:166
  90.0 5.8 %reshape.212 = bf16[3,4,64,2048]{3,2,1,0:T(8,128)(2,1)} reshape(bf16[3,4,64,16,128]{4,3,2,1,0:T(8,128)(2,1)} %shard_map.182) | data formatting | bytes 6291456 | tf_op jit(solution)/shard_map/reshape | solution.py:447
  95.9 5.1 %fusion.6 = f32[3,4,64,352]{3,2,1,0:T(8,128)} fusion(bf16[3,4,64,2048]{3,2,1,0:T(8,128)(2,1)} %reshape.212, bf16[1,2048,352]{1,2,0:T(8,128)(2,1)} %param.31), kind=kOutput, calls=%fused_computation.10 | convolution fusion | flops 1107296256 | bytes 5668864 | tf_op jit(solution)/shard_map/cqgd,df->cqgf/dot_general | solution.py:448
  101.0 8.2 %convolution_convert_fusion = bf16[3,4,64,2048]{3,2,1,0:T(8,128)(2,1)} fusion(bf16[1,352,2048]{2,1,0:T(8,128)(2,1)} %param.33, bf16[3,4,64,2048]{3,2,1,0:T(8,128)(2,1)} %reshape.212, bf16[1,2048,352]{1,2,0:T(8,128)(2,1)} %param.32, f32[3,4,64,352]{3,2,1,0:T(8,128)} %fusion.6), kind=kOutput, calls=%fused_computation.3 | convolution fusion | flops 2217787392 | bytes 10256384 | tf_op jit(solution)/shard_map/cqgf,fd->cqgd/dot_general | solution.py:455
  109.2 4.6 %copy.56 = bf16[96,8,16,128]{3,2,1,0:T(8,128)(2,1)} copy(bf16[96,8,16,128]{3,1,2,0:T(8,128)(2,1)} %bitcast.97) | data formatting | bytes 6291456
  113.8 57.6 %shard_map.183 = bf16[3,64,16,128]{3,2,1,0:T(8,128)(2,1)} custom-call(bf16[3,4,64,16,128]{4,3,2,1,0:T(8,128)(2,1)} %bitcast.91), custom_call_target="tpu_custom_call" | custom-call | tf_op jit(solution)/shard_map/pallas_call | solution.py:270
  171.5 2.0 %fusion.91 = f32[64,352]{1,0:T(8,128)S(1)} fusion(bf16[64,2048]{1,0:T(8,128)(2,1)S(1)} %bitcast.93, bf16[2048,352]{0,1:T(8,128)(2,1)} %param.34), kind=kOutput, calls=%fused_computation.107 | convolution fusion | flops 92274688 | bytes 1794048 | tf_op jit(solution)/shard_map/dot_general | solution.py:415
  173.5 0.6 fusion.47
  174.1 3.0 %fusion.2 = bf16[64,2048]{1,0:T(8,128)(2,1)S(1)} fusion(f32[64,2048]{1,0:T(8,128)S(1)} %fusion.47, bf16[352,2048]{1,0:T(8,128)(2,1)} %param.36, bf16[64,2048]{1,0:T(8,128)(2,1)S(1)} %bitcast.94, bf16[2048,352]{0,1:T(8,128)(2,1)} %param.35, f32[64,352]{1,0:T(8,128)S(1)} %fusion.91), kind=kOutput, calls=%fused_computation.5 | convolution fusion | flops 184946688 | bytes 4022272 | tf_op jit(solution)/shard_map/dot_general | solution.py:418
  177.1 8.4 %all_to_all.23 = bf16[4,16,2048]{2,1,0:T(8,128)(2,1)S(1)} all-to-all(bf16[4,16,2048]{2,1,0:T(8,128)(2,1)S(1)} %bitcast.107), channel_id=1, replica_groups=mesh['ep'=64,'rep'=4] {'rep'}, dimensions={0} | all-to-all | bytes 524288 | tf_op jit(solution)/shard_map/all_to_all | solution.py:369
  185.5 0.1 multiply_reduce_fusion.1
  185.7 0.7 multiply_convert_fusion
  (32 shorter events, 0.2 us)
Async XLA Ops:
  0.0 21.4 %copy-start = (bf16[512,2048]{1,0:T(8,128)(2,1)S(1)}, bf16[512,2048]{1,0:T(8,128)(2,1)}, u32[]{:S(2)}) copy-start(bf16[512,2048]{1,0:T(8,128)(2,1)} %param.27) | copy-start | bytes 6291460
  6.5 1.3 copy-start.3
  7.8 7.8 %copy-start.7 = (s32[64,6]{0,1:T(8,128)S(1)}, s32[64,6]{0,1:T(8,128)}, u32[]{:S(2)}) copy-start(s32[64,6]{0,1:T(8,128)} %param.28) | copy-start | bytes 4612
  7.8 7.8 %copy-start.8 = (s32[64]{0:T(128)S(1)}, s32[64]{0:T(128)}, u32[]{:S(2)}) copy-start(s32[64]{0:T(128)} %param.30) | copy-start | bytes 772
  9.9 8.6 %copy-start.6 = (f32[64,6]{0,1:T(8,128)S(1)}, f32[64,6]{0,1:T(8,128)}, u32[]{:S(2)}) copy-start(f32[64,6]{0,1:T(8,128)} %param.29) | copy-start | bytes 4612
  9.9 11.3 %copy-start.4 = (bf16[4,512,128]{2,1,0:T(8,128)(2,1)S(1)}, bf16[4,512,128]{2,1,0:T(8,128)(2,1)}, u32[]{:S(2)}) copy-start(bf16[4,512,128]{2,1,0:T(8,128)(2,1)} %param.26) | copy-start | bytes 1572868
  10.8 10.4 %all-to-all-start = ((bf16[16,16,512]{2,0,1:T(8,128)(2,1)}), bf16[16,16,512]{2,0,1:T(8,128)(2,1)S(1)}, u32[]{:S(2)}, u32[]{:S(2)}) async-start(bf16[16,16,512]{2,0,1:T(8,128)(2,1)} %copy.44), calls=%async_computation | async-start | bytes 524288 | tf_op jit(solution)/shard_map/all_to_all | solution.py:400
  113.8 57.7 %copy-start.1 = (bf16[4,16,2048]{2,1,0:T(8,128)(2,1)S(1)}, bf16[4,16,2048]{2,1,0:T(8,128)(2,1)}, u32[]{:S(2)}) copy-start(bf16[4,16,2048]{2,1,0:T(8,128)(2,1)} %shard_map.181) | copy-start | bytes 786436
  171.5 2.0 %copy-start.2 = (bf16[3,64,16,128]{3,2,1,0:T(8,128)(2,1)S(1)}, bf16[3,64,16,128]{3,2,1,0:T(8,128)(2,1)}, u32[]{:S(2)}) copy-start(bf16[3,64,16,128]{3,2,1,0:T(8,128)(2,1)} %shard_map.183) | copy-start | bytes 2359300
  174.1 11.6 %copy-start.5 = (f32[2048]{0:T(1024)S(1)}, f32[2048]{0:T(1024)}, u32[]{:S(2)}) copy-start(f32[2048]{0:T(1024)} %param.37) | copy-start | bytes 24580

commit v13 on v12

--- a/solution.py
+++ b/solution.py
@@ -330,7 +330,9 @@
     for source in range(1, replicas):
         total = total + parts[source].astype(jnp.float32)
     attended = total.astype(own.dtype).astype(jnp.float32)
-    own[...] = (resid_ref[...].astype(jnp.float32) + attended).astype(own.dtype)
+    rows = own.shape[0]
+    block = resid_ref[pl.ds(pl.multiple_of(me_r * rows, rows), rows), :]
+    own[...] = (block.astype(jnp.float32) + attended).astype(own.dtype)
     keep = pltpu.make_async_copy(own, out_ref.at[me_r], h_local)
     keep.start()
     for step in range(1, replicas):
@@ -343,7 +345,7 @@
     keep.wait()
 
 
-def hidden_rows(terms, residual_block):
+def hidden_rows(terms, residual):
     replicas = terms.shape[0]
     block = terms.shape[1:]
     return pl.pallas_call(
@@ -362,7 +364,7 @@
             pltpu.SemaphoreType.DMA(()),
         ],
         compiler_params=pltpu.CompilerParams(collective_id=4, has_side_effects=True),
-    )(terms, residual_block)
+    )(terms, residual)
 
 
 def rep_exchange(blocks):
@@ -406,9 +408,8 @@
         head_out.reshape(group_rows, -1), out_proj, preferred_element_type=jnp.float32
     )
     model_width = attn_terms.shape[1]
-    own_residual = lax.dynamic_slice_in_dim(residual, rep_index * own_count, own_count, 0)
     hidden = hidden_rows(
-        attn_terms.astype(jnp.bfloat16).reshape(replicas, own_count, model_width), own_residual
+        attn_terms.astype(jnp.bfloat16).reshape(replicas, own_count, model_width), residual
     ).reshape(group_rows, model_width)
     own_hidden = lax.dynamic_slice_in_dim(hidden, rep_index * own_count, own_count, 0)
     shared_act = (

time: 187 us -> 189 us (1.011)
  blocking collectives: 8.38 us -> 0 us
  waiting for transfers between devices: 0.8 us -> 8.36 us
  starting transfers between devices: 4.84 us -> 8.25 us
    all_to_all x1 -> x0, blocking collectives: 8.38 us -> none  [rep_exchange(): lax.all_to_all(blocks, 'rep', split_axis=0, concat_axis=0, tiled=True)]
    all_to_all x0 -> x1, waiting for transfers between devices: none -> 6.07 us  [rep_exchange(): lax.all_to_all(blocks, 'rep', split_axis=0, concat_axis=0, tiled=True)]
    all_to_all x0 -> x1, starting transfers between devices: none -> 3.4 us  [rep_exchange(): lax.all_to_all(blocks, 'rep', split_axis=0, concat_axis=0, tiled=True)]
  transfers between devices with their start and end apart: 1 -> 2, of which waited for: 1 -> 2; matrix products, arithmetic and copies ran while one was open for 2% -> 2% of each run, Pallas kernels for 0% -> 0%
where the time goes in v13:
time: 189 us; the launch traced here: 188 us
  Pallas kernels  122 us (65%)
  matrix products  26.4 us (14%)
  local copies, waits for them, and re-layouts  19.1 us (10%)
  waiting for transfers between devices  8.36 us (4%)
  starting transfers between devices  8.25 us (4%)
  other arithmetic  3.85 us (2%)
    pallas_call x1, Pallas kernels, combine_return(): pl.pallas_call(_combine_kernel, out_shape=jax.ShapeDtypeStruct((chunks, g...  57.2 us
    pallas_call x1, Pallas kernels, dispatch(): pl.pallas_call(_dispatch_kernel, out_shape=jax.ShapeDtypeStruct(out_shape...  53.3 us
    pallas_call x1, Pallas kernels, hidden_rows(): pl.pallas_call(_hidden_kernel, out_shape=jax.ShapeDtypeStruct(terms.shape...  11.6 us
    dot_general x1, matrix products, per_device(): jnp.einsum('cqgf,fd->cqgd', activated, expert_down[0], preferred_element_...  8.22 us
    unnamed x22, local copies, waits for them, and re-layouts  6.95 us
    all_to_all x1, waiting for transfers between devices, rep_exchange(): lax.all_to_all(blocks, 'rep', split_axis=0, concat_axis=0, tiled=True)  6.07 us
    reshape x1, local copies, waits for them, and re-layouts, per_device(): dispatch(outgoing, replicas)  5.82 us
    dot_general x1, matrix products, per_device(): jnp.einsum('cqgd,df->cqgf', gathered, expert_gate[0], preferred_element_t...  5.15 us
  transfers between devices with their start and end apart: 2, of which 2 were waited for; matrix products, arithmetic and copies ran while one was open for 2% of the time, Pallas kernels for 0%

profile of v13, /device:TPU:1, one launch (start us, length us, event | category | flops | bytes accessed | tf_op | source)
XLA Modules:
  0.0 188.4 jit_solution(16019196769105439270)
XLA Ops:
  0.0 1.2 copy.54
  1.2 1.2 reshape.206
  2.4 0.9 reshape.205
  3.3 0.1 iota_add_fusion
  3.3 1.0 fusion.56
  4.4 0.1 reshape.202
  4.5 1.7 fusion.90
  6.2 0.3 fusion.21
  6.5 0.0 copy-start.3
  6.5 1.3 fusion.16
  7.8 2.1 %fusion.40 = bf16[16,16,512]{2,1,0:T(8,128)(2,1)S(1)} fusion(bf16[1024,512,1]{1,0,2:T(8,128)(2,1)S(1)} %bitcast.104, f32[16,16,1024]{2,1,0:T(8,128)} %fusion.16, f32[16,1024]{1,0:T(8,128)S(1)} %reshape.202), kind=kOutput, calls=%fused_computation.29 | convolution fusion | flops 270140672 | bytes 2424832 | tf_op jit(solution)/shard_map/thp,pr->thr/dot_general | solution.py:49
  10.0 0.8 copy.44
  10.8 4.8 %all-to-all-start = ((bf16[16,16,512]{2,0,1:T(8,128)(2,1)}), bf16[16,16,512]{2,0,1:T(8,128)(2,1)S(1)}, u32[]{:S(2)}, u32[]{:S(2)}) async-start(bf16[16,16,512]{2,0,1:T(8,128)(2,1)} %copy.44), calls=%async_computation | async-start | bytes 524288 | tf_op jit(solution)/shard_map/all_to_all | solution.py:402
  15.6 0.3 select_reduce_fusion.2
  15.9 0.1 copy.37
  16.0 0.1 eq.85
  16.2 0.1 eq.81
  16.3 0.9 reduce-window.6
  17.3 0.2 slice_reduce_fusion
  17.5 0.1 fusion.59
  17.7 0.3 add_select_fusion.1
  18.0 0.1 reshape.210
  18.1 0.2 mul.96
  18.2 0.1 copy.40
  18.3 0.2 and.20
  18.5 0.1 copy.41
  18.6 0.1 copy.42
  18.7 0.2 select_reduce_fusion.1
  18.9 2.3 %all-to-all-done = bf16[16,16,512]{2,0,1:T(8,128)(2,1)S(1)} async-done(((bf16[16,16,512]{2,0,1:T(8,128)(2,1)}), bf16[16,16,512]{2,0,1:T(8,128)(2,1)S(1)}, u32[]{:S(2)}, u32[]{:S(2)}) %all-to-all-start) | async-done | bytes 262176 | tf_op jit(solution)/shard_map/all_to_all | solution.py:402
  21.2 0.2 fusion.44
  21.4 1.2 convolution_convert_fusion.1
  22.6 11.6 %shard_map.181 = bf16[4,16,2048]{2,1,0:T(8,128)(2,1)} custom-call(bf16[4,16,2048]{2,1,0:T(8,128)(2,1)} %bitcast.101, bf16[64,2048]{1,0:T(8,128)(2,1)} %resid_ref.1), custom_call_target="tpu_custom_call" | custom-call | tf_op jit(solution)/shard_map/pallas_call | solution.py:351
  34.3 1.0 concatenate.3
  35.2 1.1 gather_fusion
  36.4 1.0 copy.55
  37.4 53.3 %shard_map.182 = bf16[3,4,64,16,128]{4,3,2,1,0:T(8,128)(2,1)} custom-call(bf16[3,64,16,128]{3,2,1,0:T(8,128)(2,1)} %bitcast.99), custom_call_target="tpu_custom_call" | custom-call | tf_op jit(solution)/shard_map/pallas_call | solution.py:166
  90.7 5.8 %reshape.212 = bf16[3,4,64,2048]{3,2,1,0:T(8,128)(2,1)} reshape(bf16[3,4,64,16,128]{4,3,2,1,0:T(8,128)(2,1)} %shard_map.182) | data formatting | bytes 6291456 | tf_op jit(solution)/shard_map/reshape | solution.py:448
  96.5 5.1 %fusion.6 = f32[3,4,64,352]{3,2,1,0:T(8,128)} fusion(bf16[3,4,64,2048]{3,2,1,0:T(8,128)(2,1)} %reshape.212, bf16[1,2048,352]{1,2,0:T(8,128)(2,1)} %param.31), kind=kOutput, calls=%fused_computation.10 | convolution fusion | flops 1107296256 | bytes 5668864 | tf_op jit(solution)/shard_map/cqgd,df->cqgf/dot_general | solution.py:449
  101.7 8.2 %convolution_convert_fusion = bf16[3,4,64,2048]{3,2,1,0:T(8,128)(2,1)} fusion(bf16[1,352,2048]{2,1,0:T(8,128)(2,1)} %param.33, bf16[3,4,64,2048]{3,2,1,0:T(8,128)(2,1)} %reshape.212, bf16[1,2048,352]{1,2,0:T(8,128)(2,1)} %param.32, f32[3,4,64,352]{3,2,1,0:T(8,128)} %fusion.6), kind=kOutput, calls=%fused_computation.3 | convolution fusion | flops 2217787392 | bytes 10256384 | tf_op jit(solution)/shard_map/cqgf,fd->cqgd/dot_general | solution.py:456
  109.9 4.6 %copy.56 = bf16[96,8,16,128]{3,2,1,0:T(8,128)(2,1)} copy(bf16[96,8,16,128]{3,1,2,0:T(8,128)(2,1)} %bitcast.97) | data formatting | bytes 6291456
  114.5 57.2 %shard_map.183 = bf16[3,64,16,128]{3,2,1,0:T(8,128)(2,1)} custom-call(bf16[3,4,64,16,128]{4,3,2,1,0:T(8,128)(2,1)} %bitcast.91), custom_call_target="tpu_custom_call" | custom-call | tf_op jit(solution)/shard_map/pallas_call | solution.py:270
  171.7 2.0 %fusion.91 = f32[64,352]{1,0:T(8,128)S(1)} fusion(bf16[64,2048]{1,0:T(8,128)(2,1)S(1)} %bitcast.93, bf16[2048,352]{0,1:T(8,128)(2,1)} %param.34), kind=kOutput, calls=%fused_computation.106 | convolution fusion | flops 92274688 | bytes 1794048 | tf_op jit(solution)/shard_map/dot_general | solution.py:416
  173.7 0.6 fusion.47
  174.3 3.7 %fusion.2 = bf16[64,2048]{1,0:T(8,128)(2,1)} fusion(f32[64,2048]{1,0:T(8,128)S(1)} %fusion.47, bf16[352,2048]{1,0:T(8,128)(2,1)} %param.36, bf16[64,2048]{1,0:T(8,128)(2,1)S(1)} %bitcast.94, bf16[2048,352]{0,1:T(8,128)(2,1)} %param.35, f32[64,352]{1,0:T(8,128)S(1)} %fusion.91), kind=kOutput, calls=%fused_computation.5 | convolution fusion | flops 184946688 | bytes 4022272 | tf_op jit(solution)/shard_map/dot_general | solution.py:419
  178.0 3.4 %all-to-all-start.1 = ((bf16[4,16,2048]{2,1,0:T(8,128)(2,1)}), bf16[4,16,2048]{2,1,0:T(8,128)(2,1)S(1)}, u32[]{:S(2)}, u32[]{:S(2)}) async-start(bf16[4,16,2048]{2,1,0:T(8,128)(2,1)} %bitcast.20), calls=%async_computation.1 | async-start | bytes 524288 | tf_op jit(solution)/shard_map/all_to_all | solution.py:371
  181.4 6.1 %all-to-all-done.1 = bf16[4,16,2048]{2,1,0:T(8,128)(2,1)S(1)} async-done(((bf16[4,16,2048]{2,1,0:T(8,128)(2,1)}), bf16[4,16,2048]{2,1,0:T(8,128)(2,1)S(1)}, u32[]{:S(2)}, u32[]{:S(2)}) %all-to-all-start.1) | async-done | bytes 262176 | tf_op jit(solution)/shard_map/all_to_all | solution.py:371
  187.5 0.1 multiply_reduce_fusion.1
  187.7 0.7 multiply_convert_fusion
  (32 shorter events, 0.2 us)
Async XLA Ops:
  0.0 21.4 %copy-start = (bf16[512,2048]{1,0:T(8,128)(2,1)S(1)}, bf16[512,2048]{1,0:T(8,128)(2,1)}, u32[]{:S(2)}) copy-start(bf16[512,2048]{1,0:T(8,128)(2,1)} %param.27) | copy-start | bytes 6291460
  6.5 1.3 copy-start.3
  7.8 7.8 %copy-start.7 = (s32[64,6]{0,1:T(8,128)S(1)}, s32[64,6]{0,1:T(8,128)}, u32[]{:S(2)}) copy-start(s32[64,6]{0,1:T(8,128)} %param.28) | copy-start | bytes 4612
  7.8 7.8 %copy-start.8 = (s32[64]{0:T(128)S(1)}, s32[64]{0:T(128)}, u32[]{:S(2)}) copy-start(s32[64]{0:T(128)} %param.30) | copy-start | bytes 772
  9.9 8.6 %copy-start.6 = (f32[64,6]{0,1:T(8,128)S(1)}, f32[64,6]{0,1:T(8,128)}, u32[]{:S(2)}) copy-start(f32[64,6]{0,1:T(8,128)} %param.29) | copy-start | bytes 4612
  9.9 11.3 %copy-start.4 = (bf16[4,512,128]{2,1,0:T(8,128)(2,1)S(1)}, bf16[4,512,128]{2,1,0:T(8,128)(2,1)}, u32[]{:S(2)}) copy-start(bf16[4,512,128]{2,1,0:T(8,128)(2,1)} %param.26) | copy-start | bytes 1572868
  10.8 10.4 %all-to-all-start = ((bf16[16,16,512]{2,0,1:T(8,128)(2,1)}), bf16[16,16,512]{2,0,1:T(8,128)(2,1)S(1)}, u32[]{:S(2)}, u32[]{:S(2)}) async-start(bf16[16,16,512]{2,0,1:T(8,128)(2,1)} %copy.44), calls=%async_computation | async-start | bytes 524288 | tf_op jit(solution)/shard_map/all_to_all | solution.py:402
  114.5 57.2 %copy-start.1 = (bf16[4,16,2048]{2,1,0:T(8,128)(2,1)S(1)}, bf16[4,16,2048]{2,1,0:T(8,128)(2,1)}, u32[]{:S(2)}) copy-start(bf16[4,16,2048]{2,1,0:T(8,128)(2,1)} %shard_map.181) | copy-start | bytes 786436
  171.7 2.0 %copy-start.2 = (bf16[3,64,16,128]{3,2,1,0:T(8,128)(2,1)S(1)}, bf16[3,64,16,128]{3,2,1,0:T(8,128)(2,1)}, u32[]{:S(2)}) copy-start(bf16[3,64,16,128]{3,2,1,0:T(8,128)(2,1)} %shard_map.183) | copy-start | bytes 2359300
  174.3 13.4 %copy-start.5 = (f32[2048]{0:T(1024)S(1)}, f32[2048]{0:T(1024)}, u32[]{:S(2)}) copy-start(f32[2048]{0:T(1024)} %param.37) | copy-start | bytes 24580
  178.0 9.5 %all-to-all-start.1 = ((bf16[4,16,2048]{2,1,0:T(8,128)(2,1)}), bf16[4,16,2048]{2,1,0:T(8,128)(2,1)S(1)}, u32[]{:S(2)}, u32[]{:S(2)}) async-start(bf16[4,16,2048]{2,1,0:T(8,128)(2,1)} %bitcast.20), calls=%async_computation.1 | async-start | bytes 524288 | tf_op jit(solution)/shard_map/all_to_all | solution.py:371

commit v14 on v12

--- a/solution.py
+++ b/solution.py
@@ -239,7 +239,7 @@
         total = parts[c, 0].astype(jnp.float32)
         for source in range(1, replicas):
             total = total + parts[c, source].astype(jnp.float32)
-        sums[c] = total.astype(sums.dtype)
+        sums[c] = total.reshape(sums.shape[1:]).astype(sums.dtype)
         local = pltpu.make_async_copy(sums.at[c, me_e], out_ref.at[c, me_e], ep_local.at[c])
         local.start()
         ep_locals.append(local)
@@ -265,15 +265,16 @@
 
 
 def combine_return(terms):
-    chunks, replicas, groups = terms.shape[:3]
-    tile = terms.shape[3:]
+    chunks, replicas, groups, width = terms.shape
+    lanes = 128
+    tile = (width // lanes, lanes)
     return pl.pallas_call(
         _combine_kernel,
         out_shape=jax.ShapeDtypeStruct((chunks, groups) + tile, terms.dtype),
         in_specs=[pl.BlockSpec(memory_space=pl.ANY)],
         out_specs=pl.BlockSpec(memory_space=pl.ANY),
         scratch_shapes=[
-            pltpu.VMEM((chunks, replicas, groups) + tile, terms.dtype),
+            pltpu.VMEM(terms.shape, terms.dtype),
             pltpu.VMEM((chunks, groups) + tile, terms.dtype),
             pltpu.SemaphoreType.DMA((chunks, replicas)),
             pltpu.SemaphoreType.DMA((chunks, replicas)),
@@ -455,9 +456,7 @@
     expert_terms = jnp.einsum(
         "cqgf,fd->cqgd", activated, expert_down[0], preferred_element_type=jnp.float32
     ).astype(jnp.bfloat16)
-    returned = combine_return(
-        expert_terms.reshape(expert_terms.shape[:3] + (model_width // lanes, lanes))
-    ).reshape(share * experts, model_width)
+    returned = combine_return(expert_terms).reshape(share * experts, model_width)
     local_pos = position - rep_index * share
     mine = (local_pos >= 0) & (local_pos < share)
     column = jnp.clip(local_pos, 0, share - 1) * experts + slot_index

time: 187 us -> 182 us (0.973)
  local copies, waits for them, and re-layouts: 20.6 us -> 16 us
    unnamed x22 -> x21, local copies, waits for them, and re-layouts: 6.95 us -> 2.37 us
  transfers between devices with their start and end apart: 1 -> 1, of which waited for: 1 -> 1; matrix products, arithmetic and copies ran while one was open for 2% -> 3% of each run, Pallas kernels for 0% -> 0%
where the time goes in v14:
time: 182 us
  Pallas kernels  122 us (67%)
  matrix products  25.7 us (14%)
  local copies, waits for them, and re-layouts  16 us (9%)
  blocking collectives  8.38 us (5%)
  starting transfers between devices  4.84 us (3%)
  other arithmetic  3.88 us (2%)
    pallas_call x1, Pallas kernels, combine_return(): pl.pallas_call(_combine_kernel, out_shape=jax.ShapeDtypeStruct((chunks, g...  57.5 us
    pallas_call x1, Pallas kernels, dispatch(): pl.pallas_call(_dispatch_kernel, out_shape=jax.ShapeDtypeStruct(out_shape...  52.8 us
    pallas_call x1, Pallas kernels, hidden_rows(): pl.pallas_call(_hidden_kernel, out_shape=jax.ShapeDtypeStruct(terms.shape...  11.4 us
    all_to_all x1, blocking collectives, rep_exchange(): lax.all_to_all(blocks, 'rep', split_axis=0, concat_axis=0, tiled=True)  8.38 us
    dot_general x1, matrix products, per_device(): jnp.einsum('cqgf,fd->cqgd', activated, expert_down[0], preferred_element_...  8.22 us
    reshape x1, local copies, waits for them, and re-layouts, per_device(): dispatch(outgoing, replicas)  5.82 us
    dot_general x1, matrix products, per_device(): jnp.einsum('cqgd,df->cqgf', gathered, expert_gate[0], preferred_element_t...  5.15 us
    all_to_all x1, starting transfers between devices, per_device(): lax.all_to_all(latent_out, 'rep', split_axis=1, concat_axis=0, tiled=True)  4.84 us
  transfers between devices with their start and end apart: 1, of which 1 were waited for; matrix products, arithmetic and copies ran while one was open for 3% of the time, Pallas kernels for 0%

profile of v14, /device:TPU:1, one launch (start us, length us, event | category | flops | bytes accessed | tf_op | source)
XLA Modules:
  0.0 181.7 jit_solution(691729329051635151)
XLA Ops:
  0.0 1.2 copy.54
  1.2 1.2 reshape.203
  2.4 0.9 reshape.202
  3.3 0.1 iota_add_fusion
  3.3 1.0 fusion.56
  4.4 0.1 reshape.199
  4.5 1.7 fusion.90
  6.2 0.3 fusion.21
  6.5 0.0 copy-start.3
  6.5 1.3 fusion.16
  7.8 2.1 %fusion.40 = bf16[16,16,512]{2,1,0:T(8,128)(2,1)S(1)} fusion(bf16[1024,512,1]{1,0,2:T(8,128)(2,1)S(1)} %bitcast.97, f32[16,16,1024]{2,1,0:T(8,128)} %fusion.16, f32[16,1024]{1,0:T(8,128)S(1)} %reshape.199), kind=kOutput, calls=%fused_computation.29 | convolution fusion | flops 270140672 | bytes 2424832 | tf_op jit(solution)/shard_map/thp,pr->thr/dot_general | solution.py:49
  9.9 0.0 copy-start.6
  10.0 0.8 copy.44
  10.8 4.8 %all-to-all-start = ((bf16[16,16,512]{2,0,1:T(8,128)(2,1)}), bf16[16,16,512]{2,0,1:T(8,128)(2,1)S(1)}, u32[]{:S(2)}, u32[]{:S(2)}) async-start(bf16[16,16,512]{2,0,1:T(8,128)(2,1)} %copy.44), calls=%async_computation | async-start | bytes 524288 | tf_op jit(solution)/shard_map/all_to_all | solution.py:401
  15.6 0.3 select_reduce_fusion.2
  15.9 0.1 copy.37
  16.0 0.1 eq.85
  16.2 0.1 eq.81
  16.3 0.9 reduce-window.6
  17.2 0.2 slice_reduce_fusion
  17.5 0.1 fusion.59
  17.7 0.3 add_select_fusion.1
  18.0 0.1 reshape.207
  18.1 0.1 mul.97
  18.3 0.1 copy.40
  18.3 0.2 and.20
  18.5 0.1 copy.41
  18.6 0.1 copy.42
  18.7 0.2 select_reduce_fusion.1
  18.9 1.5 constant_dynamic-slice_fusion.resid_ref
  20.4 0.8 all-to-all-done
  21.2 0.2 fusion.44
  21.4 1.2 convolution_convert_fusion.1
  22.6 11.4 %shard_map.181 = bf16[4,16,2048]{2,1,0:T(8,128)(2,1)} custom-call(bf16[4,16,2048]{2,1,0:T(8,128)(2,1)} %bitcast.95, bf16[16,2048]{1,0:T(8,128)(2,1)} %constant_dynamic-slice_fusion.resid_ref), custom_call_target="tpu_custom_call" | custom-call | tf_op jit(solution)/shard_map/pallas_call | solution.py:350
  34.1 1.0 concatenate.3
  35.0 1.1 gather_fusion
  36.2 1.0 copy.55
  37.2 52.8 %shard_map.182 = bf16[3,4,64,16,128]{4,3,2,1,0:T(8,128)(2,1)} custom-call(bf16[3,64,16,128]{3,2,1,0:T(8,128)(2,1)} %bitcast.92), custom_call_target="tpu_custom_call" | custom-call | tf_op jit(solution)/shard_map/pallas_call | solution.py:166
  90.0 5.8 %reshape.209 = bf16[3,4,64,2048]{3,2,1,0:T(8,128)(2,1)} reshape(bf16[3,4,64,16,128]{4,3,2,1,0:T(8,128)(2,1)} %shard_map.182) | data formatting | bytes 6291456 | tf_op jit(solution)/shard_map/reshape | solution.py:448
  95.9 5.1 %fusion.6 = f32[3,4,64,352]{3,2,1,0:T(8,128)} fusion(bf16[3,4,64,2048]{3,2,1,0:T(8,128)(2,1)} %reshape.209, bf16[1,2048,352]{1,2,0:T(8,128)(2,1)} %param.31), kind=kOutput, calls=%fused_computation.10 | convolution fusion | flops 1107296256 | bytes 5668864 | tf_op jit(solution)/shard_map/cqgd,df->cqgf/dot_general | solution.py:449
  101.0 8.2 %convolution_convert_fusion.terms_ref = bf16[3,4,64,2048]{3,2,1,0:T(8,128)(2,1)} fusion(bf16[1,352,2048]{2,1,0:T(8,128)(2,1)} %param.33, bf16[3,4,64,2048]{3,2,1,0:T(8,128)(2,1)} %reshape.209, bf16[1,2048,352]{1,2,0:T(8,128)(2,1)} %param.32, f32[3,4,64,352]{3,2,1,0:T(8,128)} %fusion.6), kind=kOutput, calls=%fused_computation.3 | convolution fusion | flops 2217787392 | bytes 10256384 | tf_op jit(solution)/shard_map/cqgf,fd->cqgd/dot_general | solution.py:456
  109.2 57.5 %shard_map.183 = bf16[3,64,16,128]{3,2,1,0:T(8,128)(2,1)} custom-call(bf16[3,4,64,2048]{3,2,1,0:T(8,128)(2,1)} %convolution_convert_fusion.terms_ref), custom_call_target="tpu_custom_call" | custom-call | tf_op jit(solution)/shard_map/pallas_call | solution.py:271
  166.8 2.0 %fusion.91 = f32[64,352]{1,0:T(8,128)S(1)} fusion(bf16[64,2048]{1,0:T(8,128)(2,1)S(1)} %bitcast.87, bf16[2048,352]{0,1:T(8,128)(2,1)} %param.34), kind=kOutput, calls=%fused_computation.107 | convolution fusion | flops 92274688 | bytes 1794048 | tf_op jit(solution)/shard_map/dot_general | solution.py:416
  168.8 0.6 fusion.47
  169.4 3.0 %fusion.2 = bf16[64,2048]{1,0:T(8,128)(2,1)S(1)} fusion(f32[64,2048]{1,0:T(8,128)S(1)} %fusion.47, bf16[352,2048]{1,0:T(8,128)(2,1)} %param.36, bf16[64,2048]{1,0:T(8,128)(2,1)S(1)} %bitcast.88, bf16[2048,352]{0,1:T(8,128)(2,1)} %param.35, f32[64,352]{1,0:T(8,128)S(1)} %fusion.91), kind=kOutput, calls=%fused_computation.5 | convolution fusion | flops 184946688 | bytes 4022272 | tf_op jit(solution)/shard_map/dot_general | solution.py:419
  172.4 8.4 %all_to_all.23 = bf16[4,16,2048]{2,1,0:T(8,128)(2,1)S(1)} all-to-all(bf16[4,16,2048]{2,1,0:T(8,128)(2,1)S(1)} %bitcast.100), channel_id=1, replica_groups=mesh['ep'=64,'rep'=4] {'rep'}, dimensions={0} | all-to-all | bytes 524288 | tf_op jit(solution)/shard_map/all_to_all | solution.py:370
  180.8 0.1 multiply_reduce_fusion.1
  181.0 0.7 multiply_convert_fusion
  (31 shorter events, 0.2 us)
Async XLA Ops:
  0.0 21.4 %copy-start = (bf16[512,2048]{1,0:T(8,128)(2,1)S(1)}, bf16[512,2048]{1,0:T(8,128)(2,1)}, u32[]{:S(2)}) copy-start(bf16[512,2048]{1,0:T(8,128)(2,1)} %param.27) | copy-start | bytes 6291460
  6.5 1.3 copy-start.3
  7.8 7.8 %copy-start.7 = (s32[64,6]{0,1:T(8,128)S(1)}, s32[64,6]{0,1:T(8,128)}, u32[]{:S(2)}) copy-start(s32[64,6]{0,1:T(8,128)} %param.28) | copy-start | bytes 4612
  7.8 7.8 %copy-start.8 = (s32[64]{0:T(128)S(1)}, s32[64]{0:T(128)}, u32[]{:S(2)}) copy-start(s32[64]{0:T(128)} %param.30) | copy-start | bytes 772
  9.9 8.6 %copy-start.6 = (f32[64,6]{0,1:T(8,128)S(1)}, f32[64,6]{0,1:T(8,128)}, u32[]{:S(2)}) copy-start(f32[64,6]{0,1:T(8,128)} %param.29) | copy-start | bytes 4612
  9.9 11.3 %copy-start.4 = (bf16[4,512,128]{2,1,0:T(8,128)(2,1)S(1)}, bf16[4,512,128]{2,1,0:T(8,128)(2,1)}, u32[]{:S(2)}) copy-start(bf16[4,512,128]{2,1,0:T(8,128)(2,1)} %param.26) | copy-start | bytes 1572868
  10.8 10.4 %all-to-all-start = ((bf16[16,16,512]{2,0,1:T(8,128)(2,1)}), bf16[16,16,512]{2,0,1:T(8,128)(2,1)S(1)}, u32[]{:S(2)}, u32[]{:S(2)}) async-start(bf16[16,16,512]{2,0,1:T(8,128)(2,1)} %copy.44), calls=%async_computation | async-start | bytes 524288 | tf_op jit(solution)/shard_map/all_to_all | solution.py:401
  109.2 57.6 %copy-start.1 = (bf16[4,16,2048]{2,1,0:T(8,128)(2,1)S(1)}, bf16[4,16,2048]{2,1,0:T(8,128)(2,1)}, u32[]{:S(2)}) copy-start(bf16[4,16,2048]{2,1,0:T(8,128)(2,1)} %shard_map.181) | copy-start | bytes 786436
  166.8 2.0 %copy-start.2 = (bf16[3,64,16,128]{3,2,1,0:T(8,128)(2,1)S(1)}, bf16[3,64,16,128]{3,2,1,0:T(8,128)(2,1)}, u32[]{:S(2)}) copy-start(bf16[3,64,16,128]{3,2,1,0:T(8,128)(2,1)} %shard_map.183) | copy-start | bytes 2359300
  169.4 11.6 %copy-start.5 = (f32[2048]{0:T(1024)S(1)}, f32[2048]{0:T(1024)}, u32[]{:S(2)}) copy-start(f32[2048]{0:T(1024)} %param.37) | copy-start | bytes 24580

commit v15 on v14

--- a/solution.py
+++ b/solution.py
@@ -68,9 +68,9 @@
     pl.semaphore_wait(barrier, groups - 1 + replicas - 1)
 
 
-def _dispatch_kernel(src_ref, out_ref, ep_send, ep_recv, local_sem, x_send, x_recv, f_send, f_recv):
+def _dispatch_kernel(src_ref, out_ref, land, ep_send, ep_recv, local_sem, x_send, x_recv, f_send, f_recv):
     chunks, groups = src_ref.shape[:2]
-    replicas = out_ref.shape[1]
+    replicas = land.shape[1]
     half = groups // 2
     me_e = lax.axis_index("ep")
     me_r = lax.axis_index("rep")
@@ -82,7 +82,7 @@
     def ep_copy(c, peer, slot):
         return pltpu.make_async_remote_copy(
             src_ref.at[c, peer],
-            out_ref.at[c, me_r, slot],
+            land.at[c, me_r, slot],
             ep_send.at[c, peer],
             ep_recv.at[c, slot],
             device_id=(peer, me_r),
@@ -91,8 +91,8 @@
 
     def x_copy(c, side, slot):
         return pltpu.make_async_remote_copy(
-            out_ref.at[c, slot],
-            out_ref.at[c, slot],
+            land.at[c, slot],
+            land.at[c, slot],
             x_send.at[c, side],
             x_recv.at[c, side],
             device_id=(me_e, right if side == 0 else left),
@@ -102,8 +102,8 @@
     def f_copy(c, side, slot, part):
         rows = pl.ds(part * half, half)
         return pltpu.make_async_remote_copy(
-            out_ref.at[c, slot, rows],
-            out_ref.at[c, slot, rows],
+            land.at[c, slot, rows],
+            land.at[c, slot, rows],
             f_send.at[c, side],
             f_recv.at[c, side],
             device_id=(me_e, right if side == 0 else left),
@@ -114,7 +114,7 @@
 
     locals_ = []
     for c in range(chunks):
-        local = pltpu.make_async_copy(src_ref.at[c, me_e], out_ref.at[c, me_r, me_e], local_sem.at[c])
+        local = pltpu.make_async_copy(src_ref.at[c, me_e], land.at[c, me_r, me_e], local_sem.at[c])
         local.start()
         locals_.append(local)
 
@@ -148,6 +148,8 @@
     for c in range(chunks):
         f_copy(c, 0, across, 1).wait_recv()
         f_copy(c, 1, across, 0).wait_recv()
+        for slot in range(replicas):
+            out_ref[c, slot] = land[c, slot].reshape(out_ref.shape[2:])
         for side in range(2):
             x_copy(c, side, me_r).wait_send()
         f_copy(c, 0, left, 1).wait_send()
@@ -162,13 +164,15 @@
 
 def dispatch(blocks, replicas):
     chunks, groups = blocks.shape[:2]
-    out_shape = (chunks, replicas) + blocks.shape[1:]
+    tile = blocks.shape[2:]
+    out_shape = (chunks, replicas, groups, tile[0] * tile[1])
     return pl.pallas_call(
         _dispatch_kernel,
         out_shape=jax.ShapeDtypeStruct(out_shape, blocks.dtype),
         in_specs=[pl.BlockSpec(memory_space=pl.ANY)],
-        out_specs=pl.BlockSpec(memory_space=pl.ANY),
+        out_specs=pl.BlockSpec(memory_space=pltpu.VMEM),
         scratch_shapes=[
+            pltpu.VMEM((chunks, replicas) + blocks.shape[1:], blocks.dtype),
             pltpu.SemaphoreType.DMA((chunks, groups)),
             pltpu.SemaphoreType.DMA((chunks, groups)),
             pltpu.SemaphoreType.DMA((chunks,)),
@@ -445,7 +449,7 @@
     padded = jnp.concatenate([hidden, jnp.zeros((1, model_width), jnp.bfloat16)], axis=0)
     lanes = 128
     outgoing = padded[own_source].reshape(share, experts, model_width // lanes, lanes)
-    gathered = dispatch(outgoing, replicas).reshape(share, replicas, expert_groups, model_width)
+    gathered = dispatch(outgoing, replicas)
     gate_values = jnp.einsum(
         "cqgd,df->cqgf", gathered, expert_gate[0], preferred_element_type=jnp.float32
     )

time: 182 us -> 178 us (0.978)
  local copies, waits for them, and re-layouts: 16 us -> 10.2 us
    reshape x1 -> x0, local copies, waits for them, and re-layouts: 5.82 us -> none  [per_device(): dispatch(outgoing, replicas)]
    pallas_call x1, Pallas kernels: 52.8 us -> 54.8 us  [dispatch(): pl.pallas_call(_dispatch_kernel, out_shape=jax.ShapeDtypeStruct(out_shape...]
where the time goes in v15:
time: 178 us
  Pallas kernels  123 us (69%)
  matrix products  25.7 us (14%)
  local copies, waits for them, and re-layouts  10.2 us (6%)
  blocking collectives  8.6 us (5%)
  starting transfers between devices  4.84 us (3%)
  other arithmetic  3.88 us (2%)
    pallas_call x1, Pallas kernels, combine_return(): pl.pallas_call(_combine_kernel, out_shape=jax.ShapeDtypeStruct((chunks, g...  57.2 us
    pallas_call x1, Pallas kernels, dispatch(): pl.pallas_call(_dispatch_kernel, out_shape=jax.ShapeDtypeStruct(out_shape...  54.8 us
    pallas_call x1, Pallas kernels, hidden_rows(): pl.pallas_call(_hidden_kernel, out_shape=jax.ShapeDtypeStruct(terms.shape...  11.4 us
    all_to_all x1, blocking collectives, rep_exchange(): lax.all_to_all(blocks, 'rep', split_axis=0, concat_axis=0, tiled=True)  8.6 us
    dot_general x1, matrix products, per_device(): jnp.einsum('cqgf,fd->cqgd', activated, expert_down[0], preferred_element_...  8.22 us
    dot_general x1, matrix products, per_device(): jnp.einsum('cqgd,df->cqgf', gathered, expert_gate[0], preferred_element_t...  5.15 us
    all_to_all x1, starting transfers between devices, per_device(): lax.all_to_all(latent_out, 'rep', split_axis=1, concat_axis=0, tiled=True)  4.84 us
  transfers between devices with their start and end apart: 1, of which 1 were waited for; matrix products, arithmetic and copies ran while one was open for 3% of the time, Pallas kernels for 0%

profile of v15, /device:TPU:1, one launch (start us, length us, event | category | flops | bytes accessed | tf_op | source)
XLA Modules:
  0.0 177.8 jit_solution(9089188040337734570)
XLA Ops:
  0.0 1.2 copy.54
  1.2 1.2 reshape.200
  2.4 0.9 reshape.199
  3.3 0.1 iota_add_fusion
  3.3 1.0 fusion.56
  4.4 0.1 reshape.196
  4.5 1.7 fusion.90
  6.2 0.3 fusion.21
  6.5 0.0 copy-start.3
  6.5 1.3 fusion.16
  7.8 2.1 %fusion.40 = bf16[16,16,512]{2,1,0:T(8,128)(2,1)S(1)} fusion(bf16[1024,512,1]{1,0,2:T(8,128)(2,1)S(1)} %bitcast.95, f32[16,16,1024]{2,1,0:T(8,128)} %fusion.16, f32[16,1024]{1,0:T(8,128)S(1)} %reshape.196), kind=kOutput, calls=%fused_computation.29 | convolution fusion | flops 270140672 | bytes 2424832 | tf_op jit(solution)/shard_map/thp,pr->thr/dot_general | solution.py:49
  9.9 0.0 copy-start.6
  10.0 0.8 copy.44
  10.8 4.8 %all-to-all-start = ((bf16[16,16,512]{2,0,1:T(8,128)(2,1)}), bf16[16,16,512]{2,0,1:T(8,128)(2,1)S(1)}, u32[]{:S(2)}, u32[]{:S(2)}) async-start(bf16[16,16,512]{2,0,1:T(8,128)(2,1)} %copy.44), calls=%async_computation | async-start | bytes 524288 | tf_op jit(solution)/shard_map/all_to_all | solution.py:405
  15.6 0.3 select_reduce_fusion.2
  15.9 0.1 copy.37
  16.0 0.1 eq.85
  16.2 0.1 eq.81
  16.3 0.9 reduce-window.6
  17.2 0.2 slice_reduce_fusion
  17.5 0.1 fusion.59
  17.7 0.3 add_select_fusion.1
  18.0 0.1 reshape.204
  18.1 0.1 mul.97
  18.3 0.1 copy.40
  18.3 0.2 and.20
  18.5 0.1 copy.41
  18.6 0.1 copy.42
  18.7 0.2 select_reduce_fusion.1
  18.9 1.5 constant_dynamic-slice_fusion.resid_ref
  20.4 0.8 all-to-all-done
  21.2 0.2 fusion.44
  21.4 1.2 convolution_convert_fusion.1
  22.6 11.4 %shard_map.181 = bf16[4,16,2048]{2,1,0:T(8,128)(2,1)} custom-call(bf16[4,16,2048]{2,1,0:T(8,128)(2,1)} %bitcast.93, bf16[16,2048]{1,0:T(8,128)(2,1)} %constant_dynamic-slice_fusion.resid_ref), custom_call_target="tpu_custom_call" | custom-call | tf_op jit(solution)/shard_map/pallas_call | solution.py:354
  34.1 1.0 concatenate.3
  35.0 1.1 gather_fusion
  36.2 1.1 copy.55
  37.2 54.8 %shard_map.182 = bf16[3,4,64,2048]{3,2,1,0:T(8,128)(2,1)} custom-call(bf16[3,64,16,128]{3,2,1,0:T(8,128)(2,1)} %bitcast.90), custom_call_target="tpu_custom_call" | custom-call | tf_op jit(solution)/shard_map/pallas_call | solution.py:169
  92.0 5.2 %fusion.6 = f32[3,4,64,352]{3,2,1,0:T(8,128)} fusion(bf16[3,4,64,2048]{3,2,1,0:T(8,128)(2,1)} %shard_map.182, bf16[1,2048,352]{1,2,0:T(8,128)(2,1)} %param.31), kind=kOutput, calls=%fused_computation.10 | convolution fusion | flops 1107296256 | bytes 5668864 | tf_op jit(solution)/shard_map/cqgd,df->cqgf/dot_general | solution.py:453
  97.2 8.2 %convolution_convert_fusion.terms_ref = bf16[3,4,64,2048]{3,2,1,0:T(8,128)(2,1)} fusion(bf16[1,352,2048]{2,1,0:T(8,128)(2,1)} %param.33, bf16[3,4,64,2048]{3,2,1,0:T(8,128)(2,1)} %shard_map.182, bf16[1,2048,352]{1,2,0:T(8,128)(2,1)} %param.32, f32[3,4,64,352]{3,2,1,0:T(8,128)} %fusion.6), kind=kOutput, calls=%fused_computation.3 | convolution fusion | flops 2217787392 | bytes 10256384 | tf_op jit(solution)/shard_map/cqgf,fd->cqgd/dot_general | solution.py:460
  105.4 57.2 %shard_map.183 = bf16[3,64,16,128]{3,2,1,0:T(8,128)(2,1)} custom-call(bf16[3,4,64,2048]{3,2,1,0:T(8,128)(2,1)} %convolution_convert_fusion.terms_ref), custom_call_target="tpu_custom_call" | custom-call | tf_op jit(solution)/shard_map/pallas_call | solution.py:275
  162.7 2.0 %fusion.91 = f32[64,352]{1,0:T(8,128)S(1)} fusion(bf16[64,2048]{1,0:T(8,128)(2,1)S(1)} %bitcast.85, bf16[2048,352]{0,1:T(8,128)(2,1)} %param.34), kind=kOutput, calls=%fused_computation.107 | convolution fusion | flops 92274688 | bytes 1794048 | tf_op jit(solution)/shard_map/dot_general | solution.py:420
  164.7 0.6 fusion.47
  165.2 0.0 copy-start.5
  165.3 3.0 %fusion.2 = bf16[64,2048]{1,0:T(8,128)(2,1)S(1)} fusion(f32[64,2048]{1,0:T(8,128)S(1)} %fusion.47, bf16[352,2048]{1,0:T(8,128)(2,1)} %param.36, bf16[64,2048]{1,0:T(8,128)(2,1)S(1)} %bitcast.86, bf16[2048,352]{0,1:T(8,128)(2,1)} %param.35, f32[64,352]{1,0:T(8,128)S(1)} %fusion.91), kind=kOutput, calls=%fused_computation.5 | convolution fusion | flops 184946688 | bytes 4022272 | tf_op jit(solution)/shard_map/dot_general | solution.py:423
  168.3 8.6 %all_to_all.23 = bf16[4,16,2048]{2,1,0:T(8,128)(2,1)S(1)} all-to-all(bf16[4,16,2048]{2,1,0:T(8,128)(2,1)S(1)} %bitcast.98), channel_id=1, replica_groups=mesh['ep'=64,'rep'=4] {'rep'}, dimensions={0} | all-to-all | bytes 524288 | tf_op jit(solution)/shard_map/all_to_all | solution.py:374
  176.9 0.1 multiply_reduce_fusion.1
  177.0 0.7 multiply_convert_fusion
  (30 shorter events, 0.2 us)
Async XLA Ops:
  0.0 21.4 %copy-start = (bf16[512,2048]{1,0:T(8,128)(2,1)S(1)}, bf16[512,2048]{1,0:T(8,128)(2,1)}, u32[]{:S(2)}) copy-start(bf16[512,2048]{1,0:T(8,128)(2,1)} %param.27) | copy-start | bytes 6291460
  6.5 1.3 copy-start.3
  7.8 7.8 %copy-start.7 = (s32[64,6]{0,1:T(8,128)S(1)}, s32[64,6]{0,1:T(8,128)}, u32[]{:S(2)}) copy-start(s32[64,6]{0,1:T(8,128)} %param.28) | copy-start | bytes 4612
  7.8 7.8 %copy-start.8 = (s32[64]{0:T(128)S(1)}, s32[64]{0:T(128)}, u32[]{:S(2)}) copy-start(s32[64]{0:T(128)} %param.30) | copy-start | bytes 772
  9.9 8.6 %copy-start.6 = (f32[64,6]{0,1:T(8,128)S(1)}, f32[64,6]{0,1:T(8,128)}, u32[]{:S(2)}) copy-start(f32[64,6]{0,1:T(8,128)} %param.29) | copy-start | bytes 4612
  9.9 11.3 %copy-start.4 = (bf16[4,512,128]{2,1,0:T(8,128)(2,1)S(1)}, bf16[4,512,128]{2,1,0:T(8,128)(2,1)}, u32[]{:S(2)}) copy-start(bf16[4,512,128]{2,1,0:T(8,128)(2,1)} %param.26) | copy-start | bytes 1572868
  10.8 10.4 %all-to-all-start = ((bf16[16,16,512]{2,0,1:T(8,128)(2,1)}), bf16[16,16,512]{2,0,1:T(8,128)(2,1)S(1)}, u32[]{:S(2)}, u32[]{:S(2)}) async-start(bf16[16,16,512]{2,0,1:T(8,128)(2,1)} %copy.44), calls=%async_computation | async-start | bytes 524288 | tf_op jit(solution)/shard_map/all_to_all | solution.py:405
  105.4 57.3 %copy-start.1 = (bf16[4,16,2048]{2,1,0:T(8,128)(2,1)S(1)}, bf16[4,16,2048]{2,1,0:T(8,128)(2,1)}, u32[]{:S(2)}) copy-start(bf16[4,16,2048]{2,1,0:T(8,128)(2,1)} %shard_map.181) | copy-start | bytes 786436
  162.7 2.0 %copy-start.2 = (bf16[3,64,16,128]{3,2,1,0:T(8,128)(2,1)S(1)}, bf16[3,64,16,128]{3,2,1,0:T(8,128)(2,1)}, u32[]{:S(2)}) copy-start(bf16[3,64,16,128]{3,2,1,0:T(8,128)(2,1)} %shard_map.183) | copy-start | bytes 2359300
  165.2 11.8 %copy-start.5 = (f32[2048]{0:T(1024)S(1)}, f32[2048]{0:T(1024)}, u32[]{:S(2)}) copy-start(f32[2048]{0:T(1024)} %param.37) | copy-start | bytes 24580

commit v16 on v15

--- a/solution.py
+++ b/solution.py
@@ -446,9 +446,13 @@
         preferred_element_type=jnp.float32,
     )
     own_source = jnp.where(filled > 0, filled.astype(jnp.int32) - 1, group_rows).reshape(-1)
-    padded = jnp.concatenate([hidden, jnp.zeros((1, model_width), jnp.bfloat16)], axis=0)
     lanes = 128
-    outgoing = padded[own_source].reshape(share, experts, model_width // lanes, lanes)
+    hidden_tiles = hidden.reshape(group_rows, model_width // lanes, lanes)
+    outgoing = jnp.where(
+        (own_source < group_rows)[:, None, None],
+        hidden_tiles[jnp.minimum(own_source, group_rows - 1)],
+        jnp.zeros((), jnp.bfloat16),
+    ).reshape(share, experts, model_width // lanes, lanes)
     gathered = dispatch(outgoing, replicas)
     gate_values = jnp.einsum(
         "cqgd,df->cqgf", gathered, expert_gate[0], preferred_element_type=jnp.float32

time: 178 us -> 179 us (level)
  no operation moved by 1% of the time
where the time goes in v16:
time: 179 us
  Pallas kernels  123 us (69%)
  matrix products  26.8 us (15%)
  local copies, waits for them, and re-layouts  8.78 us (5%)
  blocking collectives  8.56 us (5%)
  other arithmetic  5.02 us (3%)
  starting transfers between devices  4.84 us (3%)
    pallas_call x1, Pallas kernels, combine_return(): pl.pallas_call(_combine_kernel, out_shape=jax.ShapeDtypeStruct((chunks, g...  57.2 us
    pallas_call x1, Pallas kernels, dispatch(): pl.pallas_call(_dispatch_kernel, out_shape=jax.ShapeDtypeStruct(out_shape...  54.8 us
    pallas_call x1, Pallas kernels, hidden_rows(): pl.pallas_call(_hidden_kernel, out_shape=jax.ShapeDtypeStruct(terms.shape...  11.4 us
    all_to_all x1, blocking collectives, rep_exchange(): lax.all_to_all(blocks, 'rep', split_axis=0, concat_axis=0, tiled=True)  8.56 us
    dot_general x1, matrix products, per_device(): jnp.einsum('cqgf,fd->cqgd', activated, expert_down[0], preferred_element_...  8.22 us
    dot_general x1, matrix products, per_device(): jnp.einsum('cqgd,df->cqgf', gathered, expert_gate[0], preferred_element_t...  5.15 us
    all_to_all x1, starting transfers between devices, per_device(): lax.all_to_all(latent_out, 'rep', split_axis=1, concat_axis=0, tiled=True)  4.84 us
  transfers between devices with their start and end apart: 1, of which 1 were waited for; matrix products, arithmetic and copies ran while one was open for 3% of the time, Pallas kernels for 0%

profile of v16, /device:TPU:1, one launch (start us, length us, event | category | flops | bytes accessed | tf_op | source)
XLA Modules:
  0.0 178.5 jit_solution(2091802383218504133)
XLA Ops:
  0.0 1.2 copy.54
  1.2 1.2 reshape.196
  2.4 0.9 reshape.195
  3.3 0.1 iota_add_fusion
  3.3 1.0 fusion.56
  4.4 0.1 reshape.192
  4.5 1.7 fusion.90
  6.2 0.3 fusion.21
  6.5 0.0 copy-start.2
  6.5 1.3 fusion.16
  7.8 2.1 %fusion.40 = bf16[16,16,512]{2,1,0:T(8,128)(2,1)S(1)} fusion(bf16[1024,512,1]{1,0,2:T(8,128)(2,1)S(1)} %bitcast.96, f32[16,16,1024]{2,1,0:T(8,128)} %fusion.16, f32[16,1024]{1,0:T(8,128)S(1)} %reshape.192), kind=kOutput, calls=%fused_computation.29 | convolution fusion | flops 270140672 | bytes 2424832 | tf_op jit(solution)/shard_map/thp,pr->thr/dot_general | solution.py:49
  9.9 0.0 copy-start.5
  10.0 0.8 copy.44
  10.8 4.8 %all-to-all-start = ((bf16[16,16,512]{2,0,1:T(8,128)(2,1)}), bf16[16,16,512]{2,0,1:T(8,128)(2,1)S(1)}, u32[]{:S(2)}, u32[]{:S(2)}) async-start(bf16[16,16,512]{2,0,1:T(8,128)(2,1)} %copy.44), calls=%async_computation | async-start | bytes 524288 | tf_op jit(solution)/shard_map/all_to_all | solution.py:405
  15.6 0.3 select_reduce_fusion.2
  15.9 0.1 copy.37
  16.0 0.1 eq.85
  16.2 0.1 eq.81
  16.3 0.9 reduce-window.6
  17.3 0.2 slice_reduce_fusion
  17.5 0.1 fusion.59
  17.7 0.3 broadcast_minimum_fusion
  18.0 0.1 min.28
  18.1 0.1 mul.97
  18.3 0.1 copy.40
  18.3 0.2 and.20
  18.5 0.1 copy.41
  18.6 0.1 copy.42
  18.7 1.5 constant_dynamic-slice_fusion.resid_ref
  20.2 0.2 select_reduce_fusion.1
  20.4 0.8 all-to-all-done
  21.2 0.2 fusion.44
  21.4 1.2 convolution_convert_fusion.1
  22.6 11.4 %shard_map.181 = bf16[4,16,2048]{2,1,0:T(8,128)(2,1)} custom-call(bf16[4,16,2048]{2,1,0:T(8,128)(2,1)} %bitcast.94, bf16[16,2048]{1,0:T(8,128)(2,1)} %constant_dynamic-slice_fusion.resid_ref), custom_call_target="tpu_custom_call" | custom-call | tf_op jit(solution)/shard_map/pallas_call | solution.py:354
  34.1 1.0 copy.55
  35.1 0.8 gather_fusion
  35.8 1.2 broadcast_select_fusion.src_ref
  37.0 54.8 %shard_map.182 = bf16[3,4,64,2048]{3,2,1,0:T(8,128)(2,1)} custom-call(bf16[3,64,16,128]{3,2,1,0:T(8,128)(2,1)} %broadcast_select_fusion.src_ref), custom_call_target="tpu_custom_call" | custom-call | tf_op jit(solution)/shard_map/pallas_call | solution.py:169
  91.8 5.2 %fusion.6 = f32[3,4,64,352]{3,2,1,0:T(8,128)} fusion(bf16[3,4,64,2048]{3,2,1,0:T(8,128)(2,1)} %shard_map.182, bf16[1,2048,352]{1,2,0:T(8,128)(2,1)} %param.31), kind=kOutput, calls=%fused_computation.10 | convolution fusion | flops 1107296256 | bytes 5668864 | tf_op jit(solution)/shard_map/cqgd,df->cqgf/dot_general | solution.py:457
  97.0 8.2 %convolution_convert_fusion.terms_ref = bf16[3,4,64,2048]{3,2,1,0:T(8,128)(2,1)} fusion(bf16[1,352,2048]{2,1,0:T(8,128)(2,1)} %param.33, bf16[3,4,64,2048]{3,2,1,0:T(8,128)(2,1)} %shard_map.182, bf16[1,2048,352]{1,2,0:T(8,128)(2,1)} %param.32, f32[3,4,64,352]{3,2,1,0:T(8,128)} %fusion.6), kind=kOutput, calls=%fused_computation.3 | convolution fusion | flops 2217787392 | bytes 10256384 | tf_op jit(solution)/shard_map/cqgf,fd->cqgd/dot_general | solution.py:464
  105.2 57.2 %shard_map.183 = bf16[3,64,16,128]{3,2,1,0:T(8,128)(2,1)} custom-call(bf16[3,4,64,2048]{3,2,1,0:T(8,128)(2,1)} %convolution_convert_fusion.terms_ref), custom_call_target="tpu_custom_call" | custom-call | tf_op jit(solution)/shard_map/pallas_call | solution.py:275
  162.4 1.7 fusion.47
  164.1 1.9 %fusion.91 = f32[64,352]{1,0:T(8,128)S(1)} fusion(bf16[64,2048]{1,0:T(8,128)(2,1)S(1)} %bitcast.86, bf16[2048,352]{0,1:T(8,128)(2,1)} %param.34), kind=kOutput, calls=%fused_computation.110 | convolution fusion | flops 92274688 | bytes 1794048 | tf_op jit(solution)/shard_map/dot_general | solution.py:420
  166.0 0.0 copy-start.4
  166.1 3.0 %fusion.2 = bf16[64,2048]{1,0:T(8,128)(2,1)S(1)} fusion(f32[64,2048]{1,0:T(8,128)S(1)} %fusion.47, bf16[352,2048]{1,0:T(8,128)(2,1)} %param.36, bf16[64,2048]{1,0:T(8,128)(2,1)S(1)} %bitcast.87, bf16[2048,352]{0,1:T(8,128)(2,1)} %param.35, f32[64,352]{1,0:T(8,128)S(1)} %fusion.91), kind=kOutput, calls=%fused_computation.5 | convolution fusion | flops 184946688 | bytes 4022272 | tf_op jit(solution)/shard_map/dot_general | solution.py:423
  169.1 8.6 %all_to_all.23 = bf16[4,16,2048]{2,1,0:T(8,128)(2,1)S(1)} all-to-all(bf16[4,16,2048]{2,1,0:T(8,128)(2,1)S(1)} %bitcast.99), channel_id=1, replica_groups=mesh['ep'=64,'rep'=4] {'rep'}, dimensions={0} | all-to-all | bytes 524288 | tf_op jit(solution)/shard_map/all_to_all | solution.py:374
  177.6 0.1 multiply_reduce_fusion.1
  177.8 0.7 multiply_convert_fusion
  (29 shorter events, 0.2 us)
Async XLA Ops:
  0.0 21.4 %copy-start = (bf16[512,2048]{1,0:T(8,128)(2,1)S(1)}, bf16[512,2048]{1,0:T(8,128)(2,1)}, u32[]{:S(2)}) copy-start(bf16[512,2048]{1,0:T(8,128)(2,1)} %param.27) | copy-start | bytes 6291460
  6.5 1.3 copy-start.2
  7.8 7.8 %copy-start.6 = (s32[64,6]{0,1:T(8,128)S(1)}, s32[64,6]{0,1:T(8,128)}, u32[]{:S(2)}) copy-start(s32[64,6]{0,1:T(8,128)} %param.28) | copy-start | bytes 4612
  7.8 7.8 %copy-start.7 = (s32[64]{0:T(128)S(1)}, s32[64]{0:T(128)}, u32[]{:S(2)}) copy-start(s32[64]{0:T(128)} %param.30) | copy-start | bytes 772
  9.9 8.6 %copy-start.5 = (f32[64,6]{0,1:T(8,128)S(1)}, f32[64,6]{0,1:T(8,128)}, u32[]{:S(2)}) copy-start(f32[64,6]{0,1:T(8,128)} %param.29) | copy-start | bytes 4612
  9.9 11.3 %copy-start.3 = (bf16[4,512,128]{2,1,0:T(8,128)(2,1)S(1)}, bf16[4,512,128]{2,1,0:T(8,128)(2,1)}, u32[]{:S(2)}) copy-start(bf16[4,512,128]{2,1,0:T(8,128)(2,1)} %param.26) | copy-start | bytes 1572868
  10.8 10.4 %all-to-all-start = ((bf16[16,16,512]{2,0,1:T(8,128)(2,1)}), bf16[16,16,512]{2,0,1:T(8,128)(2,1)S(1)}, u32[]{:S(2)}, u32[]{:S(2)}) async-start(bf16[16,16,512]{2,0,1:T(8,128)(2,1)} %copy.44), calls=%async_computation | async-start | bytes 524288 | tf_op jit(solution)/shard_map/all_to_all | solution.py:405
  162.4 1.7 copy-start.1
  166.0 11.8 %copy-start.4 = (f32[2048]{0:T(1024)S(1)}, f32[2048]{0:T(1024)}, u32[]{:S(2)}) copy-start(f32[2048]{0:T(1024)} %param.37) | copy-start | bytes 24580

commit v17 on v15

--- a/solution.py
+++ b/solution.py
@@ -185,7 +185,7 @@
     )(blocks)
 
 
-def _combine_kernel(terms_ref, out_ref, parts, sums, x_send, x_recv, x_local, ep_send, ep_recv, ep_local):
+def _combine_kernel(terms_ref, out_ref, parts, sums, land, x_send, x_recv, x_local, ep_send, ep_recv, ep_local):
     chunks, replicas, groups = terms_ref.shape[:3]
     me_e = lax.axis_index("ep")
     me_r = lax.axis_index("rep")
@@ -204,7 +204,7 @@
     def ep_copy(c, peer, slot):
         return pltpu.make_async_remote_copy(
             sums.at[c, peer],
-            out_ref.at[c, slot],
+            land.at[c, slot],
             ep_send.at[c, peer],
             ep_recv.at[c, slot],
             device_id=(peer, me_r),
@@ -244,7 +244,7 @@
         for source in range(1, replicas):
             total = total + parts[c, source].astype(jnp.float32)
         sums[c] = total.reshape(sums.shape[1:]).astype(sums.dtype)
-        local = pltpu.make_async_copy(sums.at[c, me_e], out_ref.at[c, me_e], ep_local.at[c])
+        local = pltpu.make_async_copy(sums.at[c, me_e], land.at[c, me_e], ep_local.at[c])
         local.start()
         ep_locals.append(local)
 
@@ -266,6 +266,7 @@
             return carry
 
         lax.fori_loop(1, groups, finish, 0)
+        out_ref[c] = land[c].reshape(out_ref.shape[1:])
 
 
 def combine_return(terms):
@@ -274,11 +275,12 @@
     tile = (width // lanes, lanes)
     return pl.pallas_call(
         _combine_kernel,
-        out_shape=jax.ShapeDtypeStruct((chunks, groups) + tile, terms.dtype),
+        out_shape=jax.ShapeDtypeStruct((chunks, groups, width), terms.dtype),
         in_specs=[pl.BlockSpec(memory_space=pl.ANY)],
-        out_specs=pl.BlockSpec(memory_space=pl.ANY),
+        out_specs=pl.BlockSpec(memory_space=pltpu.VMEM),
         scratch_shapes=[
             pltpu.VMEM(terms.shape, terms.dtype),
+            pltpu.VMEM((chunks, groups) + tile, terms.dtype),
             pltpu.VMEM((chunks, groups) + tile, terms.dtype),
             pltpu.SemaphoreType.DMA((chunks, replicas)),
             pltpu.SemaphoreType.DMA((chunks, replicas)),

time: 178 us -> 179 us (level)
  no operation moved by 1% of the time
where the time goes in v17:
time: 179 us
  Pallas kernels  124 us (69%)
  matrix products  25.7 us (14%)
  local copies, waits for them, and re-layouts  10.2 us (6%)
  blocking collectives  8.59 us (5%)
  starting transfers between devices  4.84 us (3%)
  other arithmetic  3.88 us (2%)
    pallas_call x1, Pallas kernels, combine_return(): pl.pallas_call(_combine_kernel, out_shape=jax.ShapeDtypeStruct((chunks, g...  58.1 us
    pallas_call x1, Pallas kernels, dispatch(): pl.pallas_call(_dispatch_kernel, out_shape=jax.ShapeDtypeStruct(out_shape...  54.8 us
    pallas_call x1, Pallas kernels, hidden_rows(): pl.pallas_call(_hidden_kernel, out_shape=jax.ShapeDtypeStruct(terms.shape...  11.4 us
    all_to_all x1, blocking collectives, rep_exchange(): lax.all_to_all(blocks, 'rep', split_axis=0, concat_axis=0, tiled=True)  8.59 us
    dot_general x1, matrix products, per_device(): jnp.einsum('cqgf,fd->cqgd', activated, expert_down[0], preferred_element_...  8.22 us
    dot_general x1, matrix products, per_device(): jnp.einsum('cqgd,df->cqgf', gathered, expert_gate[0], preferred_element_t...  5.15 us
    all_to_all x1, starting transfers between devices, per_device(): lax.all_to_all(latent_out, 'rep', split_axis=1, concat_axis=0, tiled=True)  4.84 us
  transfers between devices with their start and end apart: 1, of which 1 were waited for; matrix products, arithmetic and copies ran while one was open for 3% of the time, Pallas kernels for 0%

profile of v17, /device:TPU:1, one launch (start us, length us, event | category | flops | bytes accessed | tf_op | source)
XLA Modules:
  0.0 178.6 jit_solution(11677063878735319256)
XLA Ops:
  0.0 1.2 copy.54
  1.2 1.2 reshape.200
  2.4 0.9 reshape.199
  3.3 0.1 iota_add_fusion
  3.3 1.0 fusion.53
  4.4 0.1 reshape.196
  4.5 1.7 fusion.87
  6.2 0.3 fusion.21
  6.5 0.0 copy-start.3
  6.5 1.3 fusion.16
  7.8 2.1 %fusion.40 = bf16[16,16,512]{2,1,0:T(8,128)(2,1)S(1)} fusion(bf16[1024,512,1]{1,0,2:T(8,128)(2,1)S(1)} %bitcast.92, f32[16,16,1024]{2,1,0:T(8,128)} %fusion.16, f32[16,1024]{1,0:T(8,128)S(1)} %reshape.196), kind=kOutput, calls=%fused_computation.29 | convolution fusion | flops 270140672 | bytes 2424832 | tf_op jit(solution)/shard_map/thp,pr->thr/dot_general | solution.py:49
  9.9 0.0 copy-start.6
  9.9 0.0 copy-start.4
  10.0 0.8 copy.44
  10.8 4.8 %all-to-all-start = ((bf16[16,16,512]{2,0,1:T(8,128)(2,1)}), bf16[16,16,512]{2,0,1:T(8,128)(2,1)S(1)}, u32[]{:S(2)}, u32[]{:S(2)}) async-start(bf16[16,16,512]{2,0,1:T(8,128)(2,1)} %copy.44), calls=%async_computation | async-start | bytes 524288 | tf_op jit(solution)/shard_map/all_to_all | solution.py:407
  15.6 0.3 select_reduce_fusion.2
  15.9 0.1 copy.37
  16.0 0.1 eq.85
  16.2 0.1 eq.81
  16.3 0.9 reduce-window.6
  17.2 0.2 slice_reduce_fusion
  17.5 0.1 fusion.56
  17.7 0.3 add_select_fusion.1
  18.0 0.1 reshape.204
  18.1 0.1 mul.97
  18.3 0.1 copy.40
  18.3 0.2 and.20
  18.5 0.1 copy.41
  18.6 0.1 copy.42
  18.7 0.2 select_reduce_fusion.1
  18.9 1.5 constant_dynamic-slice_fusion.resid_ref
  20.4 0.8 all-to-all-done
  21.2 0.2 fusion.44
  21.4 1.2 convolution_convert_fusion.1
  22.6 11.4 %shard_map.181 = bf16[4,16,2048]{2,1,0:T(8,128)(2,1)} custom-call(bf16[4,16,2048]{2,1,0:T(8,128)(2,1)} %bitcast.90, bf16[16,2048]{1,0:T(8,128)(2,1)} %constant_dynamic-slice_fusion.resid_ref), custom_call_target="tpu_custom_call" | custom-call | tf_op jit(solution)/shard_map/pallas_call | solution.py:356
  34.1 1.0 concatenate.3
  35.0 1.1 gather_fusion
  36.2 1.1 copy.55
  37.2 54.8 %shard_map.182 = bf16[3,4,64,2048]{3,2,1,0:T(8,128)(2,1)} custom-call(bf16[3,64,16,128]{3,2,1,0:T(8,128)(2,1)} %bitcast.87), custom_call_target="tpu_custom_call" | custom-call | tf_op jit(solution)/shard_map/pallas_call | solution.py:169
  92.0 5.2 %fusion.6 = f32[3,4,64,352]{3,2,1,0:T(8,128)} fusion(bf16[3,4,64,2048]{3,2,1,0:T(8,128)(2,1)} %shard_map.182, bf16[1,2048,352]{1,2,0:T(8,128)(2,1)} %param.31), kind=kOutput, calls=%fused_computation.10 | convolution fusion | flops 1107296256 | bytes 5668864 | tf_op jit(solution)/shard_map/cqgd,df->cqgf/dot_general | solution.py:455
  97.2 8.2 %convolution_convert_fusion.terms_ref = bf16[3,4,64,2048]{3,2,1,0:T(8,128)(2,1)} fusion(bf16[1,352,2048]{2,1,0:T(8,128)(2,1)} %param.33, bf16[3,4,64,2048]{3,2,1,0:T(8,128)(2,1)} %shard_map.182, bf16[1,2048,352]{1,2,0:T(8,128)(2,1)} %param.32, f32[3,4,64,352]{3,2,1,0:T(8,128)} %fusion.6), kind=kOutput, calls=%fused_computation.3 | convolution fusion | flops 2217787392 | bytes 10256384 | tf_op jit(solution)/shard_map/cqgf,fd->cqgd/dot_general | solution.py:462
  105.4 58.1 %shard_map.183 = bf16[3,64,2048]{2,1,0:T(8,128)(2,1)} custom-call(bf16[3,4,64,2048]{3,2,1,0:T(8,128)(2,1)} %convolution_convert_fusion.terms_ref), custom_call_target="tpu_custom_call" | custom-call | tf_op jit(solution)/shard_map/pallas_call | solution.py:276
  163.5 2.0 %fusion.89 = f32[64,352]{1,0:T(8,128)S(1)} fusion(bf16[64,2048]{1,0:T(8,128)(2,1)S(1)} %bitcast.82, bf16[2048,352]{0,1:T(8,128)(2,1)} %param.34), kind=kOutput, calls=%fused_computation.105 | convolution fusion | flops 92274688 | bytes 1794048 | tf_op jit(solution)/shard_map/dot_general | solution.py:422
  165.5 0.5 fusion.88
  166.1 3.0 %fusion.2 = bf16[64,2048]{1,0:T(8,128)(2,1)S(1)} fusion(f32[64,2048]{1,0:T(8,128)S(1)} %fusion.88, bf16[352,2048]{1,0:T(8,128)(2,1)} %param.36, bf16[64,2048]{1,0:T(8,128)(2,1)S(1)} %bitcast.83, bf16[2048,352]{0,1:T(8,128)(2,1)} %param.35, f32[64,352]{1,0:T(8,128)S(1)} %fusion.89), kind=kOutput, calls=%fused_computation.5 | convolution fusion | flops 184946688 | bytes 4022272 | tf_op jit(solution)/shard_map/dot_general | solution.py:425
  169.1 8.6 %all_to_all.23 = bf16[4,16,2048]{2,1,0:T(8,128)(2,1)S(1)} all-to-all(bf16[4,16,2048]{2,1,0:T(8,128)(2,1)S(1)} %bitcast.95), channel_id=1, replica_groups=mesh['ep'=64,'rep'=4] {'rep'}, dimensions={0} | all-to-all | bytes 524288 | tf_op jit(solution)/shard_map/all_to_all | solution.py:376
  177.7 0.1 multiply_reduce_fusion.1
  177.9 0.7 multiply_convert_fusion
  (30 shorter events, 0.2 us)
Async XLA Ops:
  0.0 21.4 %copy-start = (bf16[512,2048]{1,0:T(8,128)(2,1)S(1)}, bf16[512,2048]{1,0:T(8,128)(2,1)}, u32[]{:S(2)}) copy-start(bf16[512,2048]{1,0:T(8,128)(2,1)} %param.27) | copy-start | bytes 6291460
  6.5 1.3 copy-start.3
  7.8 7.8 %copy-start.7 = (s32[64,6]{0,1:T(8,128)S(1)}, s32[64,6]{0,1:T(8,128)}, u32[]{:S(2)}) copy-start(s32[64,6]{0,1:T(8,128)} %param.28) | copy-start | bytes 4612
  7.8 7.8 %copy-start.8 = (s32[64]{0:T(128)S(1)}, s32[64]{0:T(128)}, u32[]{:S(2)}) copy-start(s32[64]{0:T(128)} %param.30) | copy-start | bytes 772
  9.9 8.6 %copy-start.6 = (f32[64,6]{0,1:T(8,128)S(1)}, f32[64,6]{0,1:T(8,128)}, u32[]{:S(2)}) copy-start(f32[64,6]{0,1:T(8,128)} %param.29) | copy-start | bytes 4612
  9.9 11.3 %copy-start.4 = (bf16[4,512,128]{2,1,0:T(8,128)(2,1)S(1)}, bf16[4,512,128]{2,1,0:T(8,128)(2,1)}, u32[]{:S(2)}) copy-start(bf16[4,512,128]{2,1,0:T(8,128)(2,1)} %param.26) | copy-start | bytes 1572868
  10.8 10.4 %all-to-all-start = ((bf16[16,16,512]{2,0,1:T(8,128)(2,1)}), bf16[16,16,512]{2,0,1:T(8,128)(2,1)S(1)}, u32[]{:S(2)}, u32[]{:S(2)}) async-start(bf16[16,16,512]{2,0,1:T(8,128)(2,1)} %copy.44), calls=%async_computation | async-start | bytes 524288 | tf_op jit(solution)/shard_map/all_to_all | solution.py:407
  105.4 58.1 %copy-start.1 = (bf16[4,16,2048]{2,1,0:T(8,128)(2,1)S(1)}, bf16[4,16,2048]{2,1,0:T(8,128)(2,1)}, u32[]{:S(2)}) copy-start(bf16[4,16,2048]{2,1,0:T(8,128)(2,1)} %shard_map.181) | copy-start | bytes 786436
  163.5 2.0 %copy-start.2 = (bf16[3,64,2048]{2,1,0:T(8,128)(2,1)S(1)}, bf16[3,64,2048]{2,1,0:T(8,128)(2,1)}, u32[]{:S(2)}) copy-start(bf16[3,64,2048]{2,1,0:T(8,128)(2,1)} %shard_map.183) | copy-start | bytes 2359300
  166.1 11.8 %copy-start.5 = (f32[2048]{0:T(1024)S(1)}, f32[2048]{0:T(1024)}, u32[]{:S(2)}) copy-start(f32[2048]{0:T(1024)} %param.37) | copy-start | bytes 24580
